TPU v7x, 32 devices: a whole 2x2x4 slice. The times are simulated.
32 devices in a mesh: dp: 4 (over y, x), label: 8 (over z, core).
Axes of the slice: x: 2, y: 2, z: 4, core: 2. Of those that a mesh axis runs over, the one named last changes fastest.
Arguments:
- samples: bfloat16 [4096, 4096], P(('dp', 'label')), may hold values from -6 to 6
- weight: bfloat16 [4096, 16, 256], P('dp', 'label'), may hold values from -0.09375 to 0.09375
- matches: int32 [4096, 8], P(('dp', 'label')), may hold values from 0 to 15, all different within a row; in each aligned block of 128 rows (0 to 127, 128 to 255, ...) at most 128 rows name the same one
- positives: int32 [4096, 8], P(('dp', 'label')), may hold values from 0 to 255
Outputs:
- weight_grad: bfloat16 [4096, 16, 256], P('dp', 'label')
- sample_loss: float32 [4096], P(('dp', 'label'))
Inputs may be any that keep to these rules, and one draw needn't show every extreme that they name: `matches`: each sample names 8 different clusters; among the 128 samples of one device (aligned blocks of rows) no cluster is named by more than 128 samples, a bound that some block reaches.
All inputs are finite; a program needn't handle non-finite values.
Results may differ from a plain program's by a relative error of at most 0.0043.
Values may be sent and summed in bfloat16 or wider, within the bound.
No kernel may reach another device: no remote copies, remote signals or barrier semaphores. Data moves between devices by JAX's collectives and lax.ppermute only.
A program may use at most 128 MiB of HBM per device.

v0:
```python
import jax
import jax.numpy as jnp
from jax import lax
from jax.sharding import PartitionSpec as P

inv_temp = 2.0
grad_scale = 0.03125


def slot_tables(matches, positives, clusters, capacity):
    row_count, pick_count = matches.shape
    flat_ids = matches.reshape(row_count * pick_count)
    onehot = (flat_ids[:, None] == jnp.arange(clusters, dtype=jnp.int32)[None, :]).astype(jnp.int32)
    rank_ids = jnp.sum((jnp.cumsum(onehot, axis=0) - 1) * onehot, axis=1)
    slot_ids = flat_ids * capacity + rank_ids
    owners = jnp.arange(row_count * pick_count, dtype=jnp.int32) // pick_count
    slot_row = jnp.zeros((clusters * capacity,), jnp.int32).at[slot_ids].set(owners)
    slot_label = (
        jnp.full((clusters * capacity,), -1, jnp.int32)
        .at[slot_ids]
        .set(positives.reshape(row_count * pick_count))
    )
    return (slot_ids, slot_row, slot_label.reshape(clusters, capacity))


def slot_terms(scores, labels):
    logits = scores * inv_temp
    label_ids = jnp.arange(scores.shape[-1], dtype=jnp.int32)
    targets = (label_ids == labels[..., None]).astype(jnp.float32)
    valid_mask = (labels >= 0).astype(jnp.float32)[..., None]
    per_label = jnp.maximum(logits, 0.0) + jnp.log1p(jnp.exp(-jnp.abs(logits))) - targets * logits
    slot_loss = jnp.sum(per_label * valid_mask, axis=-1)
    gradients = ((jax.nn.sigmoid(logits) - targets) * (inv_temp * grad_scale) * valid_mask).astype(
        jnp.bfloat16
    )
    return (slot_loss, gradients)


def body(samples, weight, matches, positives):
    row_count, feat_width = samples.shape
    groups = lax.axis_size("label")
    local_count = weight.shape[1]
    label_count = weight.shape[2]
    clusters = groups * local_count
    pick_count = matches.shape[1]
    capacity = 2 * row_count * pick_count // clusters
    slot_ids, slot_row, slot_label = slot_tables(matches, positives, clusters, capacity)
    outgoing = samples[slot_row].reshape(clusters, capacity, feat_width)
    incoming, labels = (
        lax.all_to_all(outgoing, "label", split_axis=0, concat_axis=0, tiled=True),
        lax.all_to_all(slot_label, "label", split_axis=0, concat_axis=0, tiled=True),
    )
    incoming = incoming.reshape(groups, local_count, capacity, feat_width)
    labels = labels.reshape(groups, local_count, capacity)
    column_part = incoming
    scores = jnp.einsum(
        "scpd,dcl->scpl",
        column_part,
        lax.all_gather(weight, "dp", axis=0, tiled=True),
        preferred_element_type=jnp.float32,
    )
    slot_loss, gradients = slot_terms(scores, labels)
    column_part = incoming
    weight_grad = lax.psum_scatter(
        jnp.einsum("scpd,scpl->dcl", column_part, gradients, preferred_element_type=jnp.float32),
        "dp",
        scatter_dimension=0,
        tiled=True,
    ).astype(jnp.bfloat16)
    returned = lax.all_to_all(
        slot_loss.reshape(clusters, -1), "label", split_axis=0, concat_axis=0, tiled=True
    )
    per_match = returned.reshape(-1)[slot_ids].reshape(row_count, pick_count)
    sample_loss = jnp.sum(per_match, axis=1) / (pick_count * label_count)
    return (weight_grad, sample_loss)


def solution(mesh):
    placed = (
        P(("dp", "label"), None),
        P("dp", "label", None),
        P(("dp", "label"), None),
        P(("dp", "label"), None),
    )
    return jax.shard_map(
        body,
        mesh=mesh,
        in_specs=placed,
        out_specs=(P("dp", "label", None), P(("dp", "label"))),
        check_vma=False,
    )
```

profile of v0, /device:TPU:0, one launch (start us, length us, event | category | flops | bytes accessed | tf_op | source)
XLA Modules:
  0.0 532.0 jit_solution(11962595919325059766)
XLA Ops:
  7.2 0.0 copy-start
  7.2 0.8 broadcast_multiply_fusion
  8.0 0.8 copy.55
  8.7 0.1 eq.42
  8.8 0.1 eq.38
  8.9 0.1 copy.54
  9.0 0.1 mul.55
  9.1 4.5 reduce-window.6
  13.7 0.1 slice.12
  13.7 0.1 copy.57
  13.9 0.1 copy.58
  14.0 0.1 add_add_fusion
  14.1 0.8 copy.61
  14.9 0.1 reshape.118
  15.0 4.9 scatter_custom_fusion.1
  19.9 6.3 %all-to-all-start.1 = ((s32[8,2,128]{2,1,0:T(2,128)}), s32[8,2,128]{2,1,0:T(2,128)S(1)}, u32[]{:S(2)}, u32[]{:S(2)}) async-start(s32[8,2,128]{2,1,0:T(2,128)} %bitcast.9), calls=%async_computation.1 | async-start | bytes 16384 | tf_op jit(solution)/shard_map/all_to_all | solution.py:51
  26.2 4.3 scatter_custom_fusion
  30.6 0.0 copy-done
  30.6 14.3 %gather_fusion = bf16[2048,4096]{1,0:T(8,128)(2,1)} fusion(bf16[128,4096]{1,0:T(8,128)(2,1)S(1)} %copy-done, s32[2048]{0:T(1024)S(1)} %fusion.29), kind=kCustom, calls=%fused_computation | custom fusion | bytes 33562624 | tf_op jit(solution)/shard_map/gather | solution.py:48
  44.9 0.0 all-to-all-done.1
  44.9 0.0 copy-start.1
  44.9 5.9 %all-to-all-start = ((bf16[16,128,4096]{2,1,0:T(8,128)(2,1)}), bf16[16,128,4096]{2,1,0:T(8,128)(2,1)}, u32[]{:S(2)}, u32[]{:S(2)}) async-start(bf16[16,128,4096]{2,1,0:T(8,128)(2,1)} %bitcast.69), calls=%async_computation | async-start | bytes 33554432 | tf_op jit(solution)/shard_map/all_to_all | solution.py:50
  50.8 0.0 all-gather.2.cloned.1.call-start
  50.8 0.0 copy-done.1
  50.8 1.1 copy.59
  52.0 0.0 all-gather.2.cloned.1.call-update
  52.0 0.0 reduce-scatter.2.cloned.1.call-start
  52.1 56.1 %all-gather.2.cloned.1.call-done = bf16[4096,2,256]{2,0,1:T(8,128)(2,1)} async-done(((bf16[1024,2,256]{2,0,1:T(8,128)(2,1)}), bf16[4096,2,256]{2,0,1:T(8,128)(2,1)}) %all-gather.2.cloned.1.call-update) | async-done | bytes 4194320 | tf_op jit(solution)/shard_map/all_gather | solution.py:59
  108.2 306.2 %all-to-all-done = bf16[16,128,4096]{2,1,0:T(8,128)(2,1)} async-done(((bf16[16,128,4096]{2,1,0:T(8,128)(2,1)}), bf16[16,128,4096]{2,1,0:T(8,128)(2,1)}, u32[]{:S(2)}, u32[]{:S(2)}) %all-to-all-start) | async-done | bytes 16777248 | tf_op jit(solution)/shard_map/all_to_all | solution.py:50
  414.4 10.8 %fusion.16 = (f32[8,2,128]{2,0,1:T(8,128)S(1)}, f32[2,8,128,256]{3,2,1,0:T(8,128)S(1)}) fusion(f32[8,2,128]{2,0,1:T(8,128)S(1)} %copy.66, s32[8,2,128]{2,0,1:T(8,128)S(1)} %copy.62, bf16[4096,2,256]{2,0,1:T(8,128)(2,1)} %all-gather.2.cloned.1.call-done, bf16[8,2,128,4096]{3,2,1,0:T(8,128)(2,1)} %bitcast.5), kind=kOutput, calls=%fused_computation.22 | convolution fusion | flops 4300208128 | bytes 23093248 | tf_op jit(solution)/shard_map/scpd,dcl->scpl/dot_general | solution.py:56
  425.2 10.7 %fusion.4 = f32[4096,2,256]{0,2,1:T(8,128)} fusion(bf16[8,2,128,4096]{3,2,1,0:T(8,128)(2,1)} %bitcast.5, f32[2,8,128,256]{3,2,1,0:T(8,128)S(1)} %get-tuple-element.13, f32[8,2,128]{2,0,1:T(8,128)S(1)} %copy.63, s32[8,2,128]{2,0,1:T(8,128)S(1)} %copy.62), kind=kOutput, calls=%fused_computation.8 | convolution fusion | flops 4299685888 | bytes 27279360 | tf_op jit(solution)/shard_map/scpd,scpl->dcl/dot_general | solution.py:65
  435.9 0.0 reduce-scatter.2.cloned.1.call-update
  435.9 0.6 copy.67
  436.5 3.3 all-to-all-start.2
  439.9 5.5 %all-to-all-done.2 = f32[8,2,128]{2,1,0:T(2,128)S(1)} async-done(((f32[8,2,128]{2,1,0:T(2,128)}), f32[8,2,128]{2,1,0:T(2,128)S(1)}, u32[]{:S(2)}, u32[]{:S(2)}) %all-to-all-start.2) | async-done | bytes 8224 | tf_op jit(solution)/shard_map/all_to_all | solution.py:70
  445.4 6.1 %gather_fusion.1 = f32[1024]{0:T(1024)S(1)} fusion(f32[2048]{0:T(1024)S(1)} %bitcast.68, s32[1024]{0:T(1024)S(1)} %broadcast_clamp_fusion), kind=kCustom, calls=%fused_computation.1 | custom fusion | bytes 12288 | tf_op jit(solution)/shard_map/gather | solution.py:73
  451.6 0.1 reshape.89
  451.6 0.1 reduce_sum.32
  451.8 0.5 broadcast_multiply_fusion.1
  452.3 69.1 %reduce-scatter.2.cloned.1.call-done = f32[1024,2,256]{0,2,1:T(8,128)} async-done(((f32[4096,2,256]{0,2,1:T(8,128)}), f32[1024,2,256]{0,2,1:T(8,128)}) %reduce-scatter.2.cloned.1.call-update) | async-done | bytes 2097168 | tf_op jit(solution)/shard_map/reduce_scatter | solution.py:64
  521.4 1.7 convert_element_type.22
  523.1 2.0 copy.68
  (13 shorter events, 0.1 us)
Async XLA Ops:
  7.2 23.4 %copy-start = (bf16[128,4096]{1,0:T(8,128)(2,1)S(1)}, bf16[128,4096]{1,0:T(8,128)(2,1)}, u32[]{:S(2)}) copy-start(bf16[128,4096]{1,0:T(8,128)(2,1)} %param.4) | copy-start | bytes 3145732
  19.9 25.0 %all-to-all-start.1 = ((s32[8,2,128]{2,1,0:T(2,128)}), s32[8,2,128]{2,1,0:T(2,128)S(1)}, u32[]{:S(2)}, u32[]{:S(2)}) async-start(s32[8,2,128]{2,1,0:T(2,128)} %bitcast.9), calls=%async_computation.1 | async-start | bytes 16384 | tf_op jit(solution)/shard_map/all_to_all | solution.py:51
  44.9 6.0 %copy-start.1 = (bf16[1024,2,256]{2,1,0:T(2,128)(2,1)S(1)}, bf16[1024,2,256]{2,1,0:T(2,128)(2,1)}, u32[]{:S(2)}) copy-start(bf16[1024,2,256]{2,1,0:T(2,128)(2,1)} %param.5) | copy-start | bytes 3145732
  44.9 369.6 %all-to-all-start = ((bf16[16,128,4096]{2,1,0:T(8,128)(2,1)}), bf16[16,128,4096]{2,1,0:T(8,128)(2,1)}, u32[]{:S(2)}, u32[]{:S(2)}) async-start(bf16[16,128,4096]{2,1,0:T(8,128)(2,1)} %bitcast.69), calls=%async_computation | async-start | bytes 33554432 | tf_op jit(solution)/shard_map/all_to_all | solution.py:50
  50.8 57.4 %all-gather.2.cloned.1.call-start = ((), (), s32[]{:S(2)}) async-start(), calls=%async_computation.4 | async-start | bytes 5242880 | tf_op jit(solution)/shard_map/all_gather | solution.py:59
  52.0 469.4 %reduce-scatter.2.cloned.1.call-start = ((), (), s32[]{:S(2)}) async-start(), calls=%async_computation.5 | async-start | bytes 10485760 | tf_op jit(solution)/shard_map/reduce_scatter | solution.py:64
  436.5 8.9 %all-to-all-start.2 = ((f32[8,2,128]{2,1,0:T(2,128)}), f32[8,2,128]{2,1,0:T(2,128)S(1)}, u32[]{:S(2)}, u32[]{:S(2)}) async-start(f32[8,2,128]{2,1,0:T(2,128)} %copy.67), calls=%async_computation.3 | async-start | bytes 16384 | tf_op jit(solution)/shard_map/all_to_all | solution.py:70
Sparse Core Ops, SparseCore 0:
  54.0 54.1 all-gather.1
  436.0 85.2 reduce-scatter.1
where the time goes:
time: 532 us
  waiting for transfers between devices  437 us (82%)
  local copies, waits for them, and re-layouts  35.8 us (7%)
  matrix products  21.5 us (4%)
  starting transfers between devices  15.6 us (3%)
  between operations  14.2 us (3%)
  other arithmetic  7.86 us (1%)
    all_to_all x1, waiting for transfers between devices, body(): lax.all_to_all(outgoing, 'label', split_axis=0, concat_axis=0, tiled=True)  306 us
    reduce_scatter x1, waiting for transfers between devices, body(): lax.psum_scatter(jnp.einsum('scpd,scpl->dcl', column_part, gradients, pre...  69.1 us
    all_gather x1, waiting for transfers between devices, body(): lax.all_gather(weight, 'dp', axis=0, tiled=True)  56.1 us
    gather x1, local copies, waits for them, and re-layouts, body(): outgoing = samples[slot_row].reshape(clusters, capacity, feat_width)  14.3 us
    dot_general x1, matrix products, body(): jnp.einsum('scpd,dcl->scpl', column_part, lax.all_gather(weight, 'dp', ax...  10.8 us
    dot_general x1, matrix products, body(): jnp.einsum('scpd,scpl->dcl', column_part, gradients, preferred_element_ty...  10.7 us
  transfers between devices with their start and end apart: 5, of which 4 were waited for; matrix products, arithmetic and copies ran while one was open for 5% of the time, Pallas kernels for 0%

commit v1 on v0

--- a/solution.py
+++ b/solution.py
@@ -1,10 +1,18 @@
+import functools
+
 import jax
 import jax.numpy as jnp
 from jax import lax
+from jax.experimental import pallas as pl
+from jax.experimental.pallas import tpu as pltpu
 from jax.sharding import PartitionSpec as P
 
 inv_temp = 2.0
 grad_scale = 0.03125
+
+ring_next = (1, 3, 0, 2)
+ring_prev = (2, 0, 3, 1)
+halves = 2
 
 
 def slot_tables(matches, positives, clusters, capacity):
@@ -36,7 +44,7 @@
     return (slot_loss, gradients)
 
 
-def body(samples, weight, matches, positives):
+def slot_body(samples, weight, matches, positives):
     row_count, feat_width = samples.shape
     groups = lax.axis_size("label")
     local_count = weight.shape[1]
@@ -52,17 +60,15 @@
     )
     incoming = incoming.reshape(groups, local_count, capacity, feat_width)
     labels = labels.reshape(groups, local_count, capacity)
-    column_part = incoming
     scores = jnp.einsum(
         "scpd,dcl->scpl",
-        column_part,
+        incoming,
         lax.all_gather(weight, "dp", axis=0, tiled=True),
         preferred_element_type=jnp.float32,
     )
     slot_loss, gradients = slot_terms(scores, labels)
-    column_part = incoming
     weight_grad = lax.psum_scatter(
-        jnp.einsum("scpd,scpl->dcl", column_part, gradients, preferred_element_type=jnp.float32),
+        jnp.einsum("scpd,scpl->dcl", incoming, gradients, preferred_element_type=jnp.float32),
         "dp",
         scatter_dimension=0,
         tiled=True,
@@ -75,6 +81,208 @@
     return (weight_grad, sample_loss)
 
 
+def score_kernel(blocks, local_count, me_ref, *refs):
+    xs, ws, code_ref = refs[:blocks], refs[blocks : blocks + 4], refs[blocks + 4]
+    grad_ref, loss_ref = refs[blocks + 5 :]
+    me = me_ref[0]
+    depth, columns = ws[0].shape
+    scores = None
+    for offset in range(4):
+        start = pl.multiple_of((me ^ offset) * depth, depth)
+        rows = jnp.concatenate([x[:, pl.ds(start, depth)] for x in xs], axis=0)
+        part = jnp.dot(rows, ws[offset][...], preferred_element_type=jnp.float32)
+        scores = part if scores is None else scores + part
+    label_count = columns // local_count
+    label_ids = lax.broadcasted_iota(jnp.int32, (scores.shape[0], label_count), 1) + 1
+    loss = None
+    for cluster in range(local_count):
+        span = slice(cluster * label_count, (cluster + 1) * label_count)
+        code = code_ref[:, cluster : cluster + 1]
+        logits = scores[:, span] * inv_temp
+        hit = label_ids == code
+        decay = jnp.exp(-jnp.abs(logits))
+        each = jnp.maximum(logits, 0.0) + jnp.log1p(decay) - jnp.where(hit, logits, 0.0)
+        share = jnp.where(logits >= 0.0, 1.0, decay) / (1.0 + decay)
+        valid = code > 0
+        grad = (share - jnp.where(hit, 1.0, 0.0)) * (inv_temp * grad_scale)
+        grad_ref[:, span] = jnp.where(valid, grad, 0.0).astype(jnp.bfloat16)
+        sums = jnp.where(valid, jnp.sum(each, axis=1, keepdims=True), 0.0)
+        loss = sums if loss is None else loss + sums
+    loss_ref[...] = loss
+
+
+def score_call(me, xs, ws, codes):
+    rows = sum(x.shape[0] for x in xs)
+    feat_width = xs[0].shape[1]
+    columns = ws[0].shape[1]
+    whole = pl.BlockSpec(memory_space=pltpu.VMEM)
+    return pl.pallas_call(
+        functools.partial(score_kernel, len(xs), codes.shape[1]),
+        out_shape=(
+            jax.ShapeDtypeStruct((rows, columns), jnp.bfloat16),
+            jax.ShapeDtypeStruct((rows, 1), jnp.float32),
+        ),
+        in_specs=[pl.BlockSpec(memory_space=pltpu.SMEM)] + [whole] * (len(xs) + 5),
+        out_specs=(whole, whole),
+        compiler_params=pltpu.CompilerParams(vmem_limit_bytes=32 << 20),
+        cost_estimate=pl.CostEstimate(
+            flops=2 * rows * feat_width * columns,
+            bytes_accessed=2 * (rows + columns) * feat_width,
+            transcendentals=2 * rows * columns,
+        ),
+        name="scores",
+    )(me, *xs, *ws, codes)
+
+
+def grad_kernel(counts, outs, me_ref, *refs):
+    blocks = sum(counts)
+    xs, gs = refs[:blocks], refs[blocks : blocks + len(counts)]
+    out_refs = refs[blocks + len(counts) :]
+    total = None
+    at = 0
+    for count, g in zip(counts, gs):
+        rows = jnp.concatenate([x[...] for x in xs[at : at + count]], axis=0)
+        at += count
+        part = lax.dot_general(
+            rows, g[...], (((0,), (0,)), ((), ())), preferred_element_type=jnp.float32
+        )
+        total = part if total is None else total + part
+    width = total.shape[1] // outs
+    for place in range(outs):
+        out_refs[place][...] = total[:, place * width : (place + 1) * width].astype(
+            out_refs[place].dtype
+        )
+
+
+def grad_call(me, offset, depth, groups_x, gs, kinds):
+    xs = [x for group in groups_x for x in group]
+    counts = [len(group) for group in groups_x]
+    columns = gs[0].shape[1]
+    rows = sum(g.shape[0] for g in gs)
+    width = columns // len(kinds)
+    steps = 4
+    tile = depth // steps
+    whole = pl.BlockSpec(memory_space=pltpu.VMEM)
+    return pl.pallas_call(
+        functools.partial(grad_kernel, counts, len(kinds)),
+        out_shape=tuple(jax.ShapeDtypeStruct((depth, width), kind) for kind in kinds),
+        grid_spec=pltpu.PrefetchScalarGridSpec(
+            num_scalar_prefetch=1,
+            grid=(steps,),
+            in_specs=[
+                pl.BlockSpec(
+                    (x.shape[0], tile), lambda i, me_ref: (0, (me_ref[0] ^ offset) * steps + i)
+                )
+                for x in xs
+            ]
+            + [pl.BlockSpec(g.shape, lambda i, me_ref: (0, 0)) for g in gs],
+            out_specs=tuple(pl.BlockSpec((tile, width), lambda i, me_ref: (i, 0)) for _ in kinds),
+        ),
+        compiler_params=pltpu.CompilerParams(vmem_limit_bytes=32 << 20),
+        cost_estimate=pl.CostEstimate(
+            flops=2 * rows * depth * columns,
+            bytes_accessed=2 * rows * (depth + columns) + 3 * depth * columns,
+            transcendentals=0,
+        ),
+        name="grads",
+    )(me, *xs, *gs)
+
+
+def ring_body(samples, weight, matches, positives):
+    row_count, feat_width = samples.shape
+    depth, local_count, label_count = weight.shape
+    groups = lax.axis_size("label")
+    pick_count = matches.shape[1]
+    clusters = groups * local_count
+    dp = lax.axis_index("dp")
+    label = lax.axis_index("label")
+    me = dp.reshape(1).astype(jnp.int32)
+
+    chips = groups // 2
+    hop = [(z * 2 + c, ring_next[z] * 2 + c) for z in range(chips) for c in range(2)]
+    swap = [(i, i ^ 1) for i in range(groups)]
+    along_x = [(i, i ^ 1) for i in range(4)]
+    along_y = [(i, i ^ 2) for i in range(4)]
+    diagonal = [(i, i ^ 3) for i in range(4)]
+
+    part = row_count // halves
+    mine = [[samples[h * part : (h + 1) * part] for h in range(halves)]]
+    for step in range(1, chips):
+        mine.append([lax.ppermute(b, "label", hop) for b in mine[-1]])
+    mate = [[lax.ppermute(b, "label", swap) for b in row] for row in mine]
+
+    flat = weight.reshape(depth, local_count * label_count)
+    ws = [
+        flat,
+        lax.ppermute(flat, "dp", along_x),
+        lax.ppermute(flat, "dp", along_y),
+        lax.ppermute(flat, "dp", diagonal),
+    ]
+
+    cluster_ids = jnp.arange(clusters, dtype=jnp.int32)[:, None, None]
+    code = jnp.sum(
+        jnp.where(matches.T[None] == cluster_ids, positives.T[None] + 1, 0), axis=1
+    ).reshape(groups, local_count, row_count)
+    code = lax.all_to_all(code, "label", split_axis=0, concat_axis=0, tiled=True)
+
+    order = []
+    for z in range(chips):
+        for c in range(2):
+            at, rows = z, []
+            for _ in range(chips):
+                rows.append([at * 2 + c, at * 2 + 1 - c])
+                at = ring_prev[at]
+            order.append(rows)
+    order = jnp.array(order, jnp.int32)[label]
+    code = jnp.transpose(code[order], (0, 1, 3, 2))
+
+    groups_x, gs, losses = [], [], []
+    for step in range(chips):
+        pieces = [range(halves)] if step < chips - 1 else [[h] for h in range(halves)]
+        for piece in pieces:
+            xs = [mine[step][h] for h in piece] + [mate[step][h] for h in piece]
+            span = slice(piece[0] * part, (piece[-1] + 1) * part)
+            codes = code[step, :, span].reshape(-1, local_count)
+            grad, loss = score_call(me, xs, ws, codes)
+            groups_x.append(xs)
+            gs.append(grad)
+            losses.append((step, span, loss.reshape(2, -1)))
+
+    far = grad_call(me, 3, depth, groups_x, gs, (jnp.bfloat16, jnp.bfloat16))
+    far_x = lax.ppermute(far[0], "dp", along_x)
+    far_y = lax.ppermute(far[1], "dp", along_y)
+    near_x = grad_call(me, 1, depth, groups_x, gs, (jnp.bfloat16, jnp.float32))
+    got_x = lax.ppermute(near_x[0], "dp", along_x)
+    near_y = grad_call(me, 2, depth, groups_x, gs, (jnp.float32, jnp.bfloat16))
+    got_y = lax.ppermute(near_y[1], "dp", along_y)
+    own = grad_call(me, 0, depth, groups_x, gs, (jnp.float32, jnp.float32))
+    pass_y = lax.ppermute((near_y[0] + far_x).astype(jnp.bfloat16), "dp", along_y)
+    pass_x = lax.ppermute((near_x[1] + far_y).astype(jnp.bfloat16), "dp", along_x)
+
+    total = jnp.zeros((groups, row_count), jnp.float32)
+    by_step = jnp.concatenate(
+        [
+            jnp.concatenate([loss for at, _, loss in losses if at == step], axis=1)
+            for step in range(chips)
+        ],
+        axis=0,
+    )
+    total = total.at[order.reshape(-1)].set(by_step)
+    returned = lax.all_to_all(total, "label", split_axis=0, concat_axis=0, tiled=True)
+    sample_loss = jnp.sum(returned, axis=0) / (pick_count * label_count)
+
+    first = own[0] + got_x.astype(jnp.float32) + pass_y.astype(jnp.float32)
+    second = own[1] + got_y.astype(jnp.float32) + pass_x.astype(jnp.float32)
+    weight_grad = jnp.stack([first, second], axis=1).astype(jnp.bfloat16)
+    return (weight_grad, sample_loss)
+
+
+def body(samples, weight, matches, positives):
+    if (lax.axis_size("dp"), lax.axis_size("label"), weight.shape[1]) == (4, 8, 2):
+        return ring_body(samples, weight, matches, positives)
+    return slot_body(samples, weight, matches, positives)
+
+
 def solution(mesh):
     placed = (
         P(("dp", "label"), None),

time: 532 us -> 172 us (0.32)
  waiting for transfers between devices: 437 us -> 60.4 us
  Pallas kernels: 0 us -> 33.5 us
  matrix products: 21.5 us -> 0 us
  starting transfers between devices: 15.6 us -> 33.6 us
  between operations: 14.2 us -> 1.12 us
  local copies, waits for them, and re-layouts: 35.8 us -> 24.9 us
  other arithmetic: 7.86 us -> 16.5 us
    all_to_all x3 -> x2, waiting for transfers between devices: 312 us -> 0.01 us  [the longest x1 0.01 us: ring_body(): lax.all_to_all(code, 'label', split_axis=0, concat_axis=0, tiled=True)]
    reduce_scatter x1 -> x0, waiting for transfers between devices: 69.1 us -> none  [body(): lax.psum_scatter(jnp.einsum('scpd,scpl->dcl', column_part, gradients, pre...]
    ppermute x0 -> x23, waiting for transfers between devices: none -> 60.4 us  [the longest x6 40.2 us: ring_body(): mine.append([lax.ppermute(b, 'label', hop) for b in mine[-1]])]
    all_gather x1 -> x0, waiting for transfers between devices: 56.1 us -> none  [body(): lax.all_gather(weight, 'dp', axis=0, tiled=True)]
    pallas_call x0 -> x9, Pallas kernels: none -> 33.5 us  [the longest x4 17.5 us: grad_call(): pl.pallas_call(functools.partial(grad_kernel, counts, len(kinds)), out_sh...]
    ppermute x0 -> x23, starting transfers between devices: none -> 23.7 us  [the longest x6 11.6 us: ring_body(): mine.append([lax.ppermute(b, 'label', hop) for b in mine[-1]])]
    dot_general x2 -> x0, matrix products: 21.5 us -> none  [the longest x1 10.8 us: body(): jnp.einsum('scpd,dcl->scpl', column_part, lax.all_gather(weight, 'dp', ax...]
    gather x2, local copies, waits for them, and re-layouts: 20.5 us -> 1.62 us  [ring_body(): code = jnp.transpose(code[order], (0, 1, 3, 2))]
  transfers between devices with their start and end apart: 5 -> 25, of which waited for: 4 -> 8; matrix products, arithmetic and copies ran while one was open for 5% -> 13% of each run, Pallas kernels for 0% -> 15%
where the time goes in v1:
time: 172 us; the launch traced here: 170 us
  waiting for transfers between devices  60.4 us (35%)
  starting transfers between devices  33.6 us (20%)
  Pallas kernels  33.5 us (19%)
  local copies, waits for them, and re-layouts  24.9 us (14%)
  other arithmetic  16.5 us (10%)
    ppermute x6, waiting for transfers between devices, ring_body(): mine.append([lax.ppermute(b, 'label', hop) for b in mine[-1]])  40.2 us
    pallas_call x4, Pallas kernels, grad_call(): pl.pallas_call(functools.partial(grad_kernel, counts, len(kinds)), out_sh...  17.5 us
    unnamed x106, local copies, waits for them, and re-layouts  16.8 us
    pallas_call x5, Pallas kernels, score_call(): pl.pallas_call(functools.partial(score_kernel, len(xs), codes.shape[1]),...  16 us
    ppermute x6, starting transfers between devices, ring_body(): mine.append([lax.ppermute(b, 'label', hop) for b in mine[-1]])  11.6 us
    ppermute x1, waiting for transfers between devices, ring_body(): lax.ppermute((near_x[1] + far_y).astype(jnp.bfloat16), 'dp', along_x)  11.4 us
    ppermute x1, waiting for transfers between devices, ring_body(): lax.ppermute(flat, 'dp', along_y)  8.61 us
    pallas_call x5, other arithmetic, score_call(): pl.pallas_call(functools.partial(score_kernel, len(xs), codes.shape[1]),...  6.1 us
  transfers between devices with their start and end apart: 25, of which 8 were waited for; matrix products, arithmetic and copies ran while one was open for 13% of the time, Pallas kernels for 15%

profile of v1, /device:TPU:0, one launch (start us, length us, event | category | flops | bytes accessed | tf_op | source)
XLA Modules:
  0.0 170.0 jit_solution(2945832001161556305)
XLA Ops:
  0.6 1.4 fusion.14
  2.0 3.1 %collective-permute-start.3 = (bf16[64,4096]{1,0:T(8,128)(2,1)S(1)}, bf16[64,4096]{1,0:T(8,128)(2,1)S(1)}, u32[]{:S(2)}, u32[]{:S(2)}) collective-permute-start(bf16[64,4096]{1,0:T(8,128)(2,1)S(1)} %get-tuple-element.46.refs_1_), channel_id=1, source_target_pairs={{0,2},{1,3},{2,6},{3,7},{4,0},{5,1},{6,4},{7,5},{8,10},{9,11},{10,... | collective-permute-start | bytes 1572872 | tf_op jit(solution)/shard_map/ppermute | solution.py:211
  5.1 2.6 %collective-permute-start.2 = (bf16[64,4096]{1,0:T(8,128)(2,1)S(1)}, bf16[64,4096]{1,0:T(8,128)(2,1)}, u32[]{:S(2)}, u32[]{:S(2)}) collective-permute-start(bf16[64,4096]{1,0:T(8,128)(2,1)S(1)} %get-tuple-element.47.refs_0_), channel_id=1, source_target_pairs={{0,2},{1,3},{2,6},{3,7},{4,0},{5,1},{6,4},{7,5},{8,10},{9,11},{10,... | collective-permute-start | bytes 1572872 | tf_op jit(solution)/shard_map/ppermute | solution.py:211
  7.7 11.2 %collective-permute-done.3.refs_1_.refs_5_ = bf16[64,4096]{1,0:T(8,128)(2,1)S(1)} collective-permute-done((bf16[64,4096]{1,0:T(8,128)(2,1)S(1)}, bf16[64,4096]{1,0:T(8,128)(2,1)S(1)}, u32[]{:S(2)}, u32[]{:S(2)}) %collective-permute-start.3) | collective-permute-done | bytes 524320 | tf_op jit(solution)/shard_map/ppermute | solution.py:211
  18.9 1.2 collective-permute-start.7
  20.3 2.5 %collective-permute-start.16 = (bf16[1024,512]{1,0:T(8,128)(2,1)S(1)}, bf16[1024,512]{1,0:T(8,128)(2,1)S(1)}, u32[]{:S(2)}, u32[]{:S(2)}) collective-permute-start(bf16[1024,512]{1,0:T(8,128)(2,1)S(1)} %bitcast.29), channel_id=1, source_target_pairs={{0,24},{8,16},{16,8},{24,0},{1,25},{9,17},{17,9},{25,1},{2,26},{10... | collective-permute-start | bytes 3145736 | tf_op jit(solution)/shard_map/ppermute | solution.py:219
  24.1 6.1 %collective-permute-done.2.refs_0_.refs_4_ = bf16[64,4096]{1,0:T(8,128)(2,1)} collective-permute-done((bf16[64,4096]{1,0:T(8,128)(2,1)S(1)}, bf16[64,4096]{1,0:T(8,128)(2,1)}, u32[]{:S(2)}, u32[]{:S(2)}) %collective-permute-start.2) | collective-permute-done | bytes 524320 | tf_op jit(solution)/shard_map/ppermute | solution.py:211
  30.2 1.9 %collective-permute-start.14 = (bf16[1024,512]{1,0:T(8,128)(2,1)S(1)}, bf16[1024,512]{1,0:T(8,128)(2,1)}, u32[]{:S(2)}, u32[]{:S(2)}) collective-permute-start(bf16[1024,512]{1,0:T(8,128)(2,1)S(1)} %bitcast.31), channel_id=1, source_target_pairs={{0,8},{8,0},{16,24},{24,16},{1,9},{9,1},{17,25},{25,17},{2,10},{10... | collective-permute-start | bytes 3145736 | tf_op jit(solution)/shard_map/ppermute | solution.py:217
  32.1 8.4 %collective-permute-done.7.refs_1_.refs_9_ = bf16[64,4096]{1,0:T(8,128)(2,1)S(1)} collective-permute-done((bf16[64,4096]{1,0:T(8,128)(2,1)S(1)}, bf16[64,4096]{1,0:T(8,128)(2,1)S(1)}, u32[]{:S(2)}, u32[]{:S(2)}) %collective-permute-start.7) | collective-permute-done | bytes 524320 | tf_op jit(solution)/shard_map/ppermute | solution.py:211
  42.8 5.0 %all-to-all-start = ((s32[8,2,128]{2,1,0:T(2,128)}), s32[8,2,128]{2,1,0:T(2,128)S(1)}, u32[]{:S(2)}, u32[]{:S(2)}) async-start(s32[8,2,128]{2,1,0:T(2,128)} %bitcast.3), calls=%async_computation | async-start | bytes 16384 | tf_op jit(solution)/shard_map/all_to_all | solution.py:226
  48.6 6.3 %collective-permute-done.6.refs_0_.refs_8_ = bf16[64,4096]{1,0:T(8,128)(2,1)} collective-permute-done((bf16[64,4096]{1,0:T(8,128)(2,1)}, bf16[64,4096]{1,0:T(8,128)(2,1)}, u32[]{:S(2)}, u32[]{:S(2)}) %collective-permute-start.6) | collective-permute-done | bytes 524320 | tf_op jit(solution)/shard_map/ppermute | solution.py:211
  55.5 3.4 %collective-permute-start.10 = (bf16[64,4096]{1,0:T(8,128)(2,1)}, bf16[64,4096]{1,0:T(8,128)(2,1)}, u32[]{:S(2)}, u32[]{:S(2)}) collective-permute-start(bf16[64,4096]{1,0:T(8,128)(2,1)} %collective-permute-done.6.refs_0_.refs_8_), channel_id=1, source_target_pairs={{0,2},{1,3},{2,6},{3,7},{4,0},{5,1},{6,4},{7,5},{8,10},{9,11},{10,... | collective-permute-start | bytes 1572872 | tf_op jit(solution)/shard_map/ppermute | solution.py:211
  59.6 1.0 copy.20
  60.7 8.6 %collective-permute-done.15.refs_6_.refs_4_ = bf16[1024,512]{1,0:T(8,128)(2,1)S(1)} collective-permute-done((bf16[1024,512]{1,0:T(8,128)(2,1)S(1)}, bf16[1024,512]{1,0:T(8,128)(2,1)S(1)}, u32[]{:S(2)}, u32[]{:S(2)}) %collective-permute-start.15) | collective-permute-done | bytes 1048608 | tf_op jit(solution)/shard_map/ppermute | solution.py:218
  69.8 1.1 fusion.16
  71.2 8.2 %collective-permute-done.10.refs_0_.refs_12_ = bf16[64,4096]{1,0:T(8,128)(2,1)} collective-permute-done((bf16[64,4096]{1,0:T(8,128)(2,1)}, bf16[64,4096]{1,0:T(8,128)(2,1)}, u32[]{:S(2)}, u32[]{:S(2)}) %collective-permute-start.10) | collective-permute-done | bytes 524320 | tf_op jit(solution)/shard_map/ppermute | solution.py:211
  80.4 3.5 %scores.6 = (bf16[256,512]{1,0:T(8,128)(2,1)S(1)}, f32[256,1]{1,0:T(8,128)S(1)}) custom-call(s32[1]{0:T(128)} %bitcast.me_ref, bf16[64,4096]{1,0:T(8,128)(2,1)} %collective-permute-done.2.refs_0_.refs_4_, bf16[64,4096]{1,0:T(8,128)(2,1)S(1)} %copy-done.7, bf16[64,4096]{1,0:T(8,128)(2,1)} %collective-permute-done.4.refs_2_.refs_6_, ...), custom_call_target="tpu_custom_call" | custom-call | flops 1073741824 | bytes 6291456 | tf_op jit(solution)/shard_map/scores/pallas_call | solution.py:119
  84.6 3.3 %scores.5 = (bf16[256,512]{1,0:T(8,128)(2,1)S(1)}, f32[256,1]{1,0:T(8,128)S(1)}) custom-call(s32[1]{0:T(128)} %bitcast.me_ref, bf16[64,4096]{1,0:T(8,128)(2,1)S(1)} %copy-done.4, bf16[64,4096]{1,0:T(8,128)(2,1)S(1)} %copy-done.1, bf16[64,4096]{1,0:T(8,128)(2,1)S(1)} %collective-permute-done.refs_2_, bf16[64,4096]{1,0:T(8,128)(2,1)S(1)} %copy-done.10, ...), custom_call_target="tpu_custom_call" | custom-call | flops 1073741824 | bytes 6291456 | tf_op jit(solution)/shard_map/scores/pallas_call | solution.py:119
  88.6 3.7 %scores.7 = (bf16[256,512]{1,0:T(8,128)(2,1)S(1)}, f32[256,1]{1,0:T(8,128)S(1)}) custom-call(s32[1]{0:T(128)} %bitcast.me_ref, bf16[64,4096]{1,0:T(8,128)(2,1)} %collective-permute-done.6.refs_0_.refs_8_, bf16[64,4096]{1,0:T(8,128)(2,1)S(1)} %copy-done.13, bf16[64,4096]{1,0:T(8,128)(2,1)S(1)} %collective-permute-done.8.refs_2_.refs_10_, ...), custom_call_target="tpu_custom_call" | custom-call | flops 1073741824 | bytes 6291456 | tf_op jit(solution)/shard_map/scores/pallas_call | solution.py:119
  92.3 2.8 %scores.9 = (bf16[128,512]{1,0:T(8,128)(2,1)S(1)}, f32[128,1]{1,0:T(8,128)S(1)}) custom-call(s32[1]{0:T(128)} %bitcast.me_ref, bf16[64,4096]{1,0:T(8,128)(2,1)} %collective-permute-done.12.refs_0_.refs_14_, bf16[64,4096]{1,0:T(8,128)(2,1)S(1)} %collective-permute-done.13.refs_1_.refs_15_, bf16[1024,512]{1,0:T(8,128)(2,1)S(1)} %bitcast.35, ...), custom_call_target="tpu_custom_call" | custom-call | flops 536870912 | bytes 5242880 | tf_op jit(solution)/shard_map/scores/pallas_call | solution.py:119
  95.7 2.7 %scores.8 = (bf16[128,512]{1,0:T(8,128)(2,1)S(1)}, f32[128,1]{1,0:T(8,128)S(1)}) custom-call(s32[1]{0:T(128)} %bitcast.me_ref, bf16[64,4096]{1,0:T(8,128)(2,1)} %collective-permute-done.10.refs_0_.refs_12_, bf16[64,4096]{1,0:T(8,128)(2,1)S(1)} %collective-permute-done.11.refs_1_.refs_13_, bf16[1024,512]{1,0:T(8,128)(2,1)S(1)} %bitcast.36, ...), custom_call_target="tpu_custom_call" | custom-call | flops 536870912 | bytes 5242880 | tf_op jit(solution)/shard_map/scores/pallas_call | solution.py:119
  98.5 4.7 %grads.7 = (bf16[1024,256]{1,0:T(8,128)(2,1)S(1)}, bf16[1024,256]{1,0:T(8,128)(2,1)}) custom-call(s32[1]{0:T(128)} %bitcast.me_ref, bf16[64,4096]{1,0:T(8,128)(2,1)S(1)} %copy-done.4, bf16[64,4096]{1,0:T(8,128)(2,1)S(1)} %copy-done.1, bf16[64,4096]{1,0:T(8,128)(2,1)S(1)} %collective-permute-done.refs_2_, bf16[64,4096]{1,0:T(8,128)(2,1)S(1)} %copy-done.10, ...), custom_call_target="tpu_custom_call" | custom-call | flops 1073741824 | bytes 4718592 | tf_op jit(solution)/shard_map/grads/pallas_call | solution.py:166
  105.1 1.5 collective-permute-start.18
  107.1 1.0 reduce.1
  108.2 1.0 reduce.2
  109.2 1.0 reduce.3
  110.2 1.5 reduce.5
  112.5 1.5 reduce.4
  114.0 1.3 reshape.95
  115.3 1.3 scatter_custom_fusion
  116.7 4.9 %all-to-all-start.1 = ((f32[8,1,128]{2,1,0:T(1,128)}), f32[8,1,128]{2,1,0:T(1,128)S(1)}, u32[]{:S(2)}, u32[]{:S(2)}) async-start(f32[8,1,128]{2,1,0:T(1,128)} %bitcast.15), calls=%async_computation.1 | async-start | bytes 8192 | tf_op jit(solution)/shard_map/all_to_all | solution.py:271
  121.6 1.0 copy-done.19
  122.7 1.0 copy-done.22
  123.7 1.0 copy-done.25
  124.8 1.0 copy-done.28
  125.8 1.0 copy-done.31
  129.6 4.4 %grads.6 = (f32[1024,256]{1,0:T(8,128)S(1)}, bf16[1024,256]{1,0:T(8,128)(2,1)}) custom-call(s32[1]{0:T(128)} %bitcast.me_ref, bf16[64,4096]{1,0:T(8,128)(2,1)S(1)} %copy-done.5, bf16[64,4096]{1,0:T(8,128)(2,1)S(1)} %copy-done.2, bf16[64,4096]{1,0:T(8,128)(2,1)S(1)} %copy-done.19, bf16[64,4096]{1,0:T(8,128)(2,1)S(1)} %copy-done.11, ...), custom_call_target="tpu_custom_call" | custom-call | flops 1073741824 | bytes 4718592 | tf_op jit(solution)/shard_map/grads/pallas_call | solution.py:166
  134.6 4.4 %grads.5 = (bf16[1024,256]{1,0:T(8,128)(2,1)}, f32[1024,256]{1,0:T(8,128)S(1)}) custom-call(s32[1]{0:T(128)} %bitcast.me_ref, bf16[64,4096]{1,0:T(8,128)(2,1)S(1)} %copy-done.5, bf16[64,4096]{1,0:T(8,128)(2,1)S(1)} %copy-done.2, bf16[64,4096]{1,0:T(8,128)(2,1)S(1)} %copy-done.19, bf16[64,4096]{1,0:T(8,128)(2,1)S(1)} %copy-done.11, ...), custom_call_target="tpu_custom_call" | custom-call | flops 1073741824 | bytes 4718592 | tf_op jit(solution)/shard_map/grads/pallas_call | solution.py:166
  139.5 2.0 %add_convert_fusion.1 = bf16[1024,256]{1,0:T(8,128)(2,1)} fusion(f32[1024,256]{1,0:T(8,128)S(1)} %get-tuple-element.31, bf16[1024,256]{1,0:T(8,128)(2,1)} %collective-permute-done.21), kind=kLoop, calls=%fused_computation.4 | loop fusion | flops 786432 | bytes 2097152 | tf_op jit(solution)/shard_map/convert_element_type | solution.py:260
  141.5 1.5 collective-permute-start.22
  143.1 2.1 %add_convert_fusion.3 = bf16[1024,256]{1,0:T(8,128)(2,1)} fusion(f32[1024,256]{1,0:T(8,128)S(1)} %get-tuple-element.27, bf16[1024,256]{1,0:T(8,128)(2,1)} %collective-permute-done.18), kind=kLoop, calls=%fused_computation.6 | loop fusion | flops 786432 | bytes 2097152 | tf_op jit(solution)/shard_map/convert_element_type | solution.py:259
  145.2 1.5 collective-permute-start.19
  146.7 3.9 %grads.4 = (f32[1024,256]{1,0:T(8,128)S(1)}, f32[1024,256]{1,0:T(8,128)S(1)}) custom-call(s32[1]{0:T(128)} %bitcast.me_ref, bf16[64,4096]{1,0:T(8,128)(2,1)S(1)} %copy-done.5, bf16[64,4096]{1,0:T(8,128)(2,1)S(1)} %copy-done.2, bf16[64,4096]{1,0:T(8,128)(2,1)S(1)} %copy-done.20, bf16[64,4096]{1,0:T(8,128)(2,1)S(1)} %copy-done.11, ...), custom_call_target="tpu_custom_call" | custom-call | flops 1073741824 | bytes 4718592 | tf_op jit(solution)/shard_map/grads/pallas_call | solution.py:166
  150.7 1.0 copy-done.40
  153.2 11.4 %collective-permute-done.22 = bf16[1024,256]{1,0:T(8,128)(2,1)} collective-permute-done((bf16[1024,256]{1,0:T(8,128)(2,1)}, bf16[1024,256]{1,0:T(8,128)(2,1)}, u32[]{:S(2)}, u32[]{:S(2)}) %collective-permute-start.22) | collective-permute-done | bytes 524320 | tf_op jit(solution)/shard_map/ppermute | solution.py:260
  164.6 1.8 %fusion.1 = bf16[1024,1,256]{2,0,1:T(8,128)(2,1)S(1)} fusion(bf16[1024,256]{1,0:T(8,128)(2,1)} %collective-permute-done.22, f32[1024,256]{1,0:T(8,128)} %copy-done.42, bf16[1024,256]{1,0:T(8,128)(2,1)} %collective-permute-done.20), kind=kLoop, calls=%fused_computation.8 | loop fusion | flops 1310720 | bytes 2621440 | tf_op jit(solution)/shard_map/stack | solution.py:276
  166.5 1.4 fusion
  167.9 2.0 %copy.21 = bf16[1024,2,256]{2,1,0:T(2,128)(2,1)} copy(bf16[1024,2,256]{2,0,1:T(8,128)(2,1)S(1)} %pad_maximum_fusion) | data formatting | bytes 2097152
  (147 shorter events, 18.3 us)
Async XLA Ops:
  0.6 19.4 %copy-start.49 = (bf16[1024,2,256]{2,1,0:T(2,128)(2,1)S(1)}, bf16[1024,2,256]{2,1,0:T(2,128)(2,1)}, u32[]{:S(2)}) copy-start(bf16[1024,2,256]{2,1,0:T(2,128)(2,1)} %param.6) | copy-start | bytes 3145732
  2.0 18.3 %copy-start = (bf16[64,4096]{1,0:T(8,128)(2,1)}, bf16[64,4096]{1,0:T(8,128)(2,1)S(1)}, u32[]{:S(2)}) copy-start(bf16[64,4096]{1,0:T(8,128)(2,1)S(1)} %get-tuple-element.46.refs_1_) | copy-start | bytes 1572868
  2.0 18.3 %copy-start.3 = (bf16[64,4096]{1,0:T(8,128)(2,1)}, bf16[64,4096]{1,0:T(8,128)(2,1)S(1)}, u32[]{:S(2)}) copy-start(bf16[64,4096]{1,0:T(8,128)(2,1)S(1)} %get-tuple-element.47.refs_0_) | copy-start | bytes 1572868
  2.0 16.8 %collective-permute-start.3 = (bf16[64,4096]{1,0:T(8,128)(2,1)S(1)}, bf16[64,4096]{1,0:T(8,128)(2,1)S(1)}, u32[]{:S(2)}, u32[]{:S(2)}) collective-permute-start(bf16[64,4096]{1,0:T(8,128)(2,1)S(1)} %get-tuple-element.46.refs_1_), channel_id=1, source_target_pairs={{0,2},{1,3},{2,6},{3,7},{4,0},{5,1},{6,4},{7,5},{8,10},{9,11},{10,... | collective-permute-start | bytes 1572872 | tf_op jit(solution)/shard_map/ppermute | solution.py:211
  5.1 17.7 %collective-permute-start.1 = (bf16[64,4096]{1,0:T(8,128)(2,1)S(1)}, bf16[64,4096]{1,0:T(8,128)(2,1)S(1)}, u32[]{:S(2)}, u32[]{:S(2)}) collective-permute-start(bf16[64,4096]{1,0:T(8,128)(2,1)S(1)} %get-tuple-element.46.refs_1_), channel_id=1, source_target_pairs={{0,1},{1,0},{2,3},{3,2},{4,5},{5,4},{6,7},{7,6},{8,9},{9,8},{10,11... | collective-permute-start | bytes 1572872 | tf_op jit(solution)/shard_map/ppermute | solution.py:212
  5.1 25.1 %collective-permute-start.2 = (bf16[64,4096]{1,0:T(8,128)(2,1)S(1)}, bf16[64,4096]{1,0:T(8,128)(2,1)}, u32[]{:S(2)}, u32[]{:S(2)}) collective-permute-start(bf16[64,4096]{1,0:T(8,128)(2,1)S(1)} %get-tuple-element.47.refs_0_), channel_id=1, source_target_pairs={{0,2},{1,3},{2,6},{3,7},{4,0},{5,1},{6,4},{7,5},{8,10},{9,11},{10,... | collective-permute-start | bytes 1572872 | tf_op jit(solution)/shard_map/ppermute | solution.py:211
  18.9 21.6 %collective-permute-start.7 = (bf16[64,4096]{1,0:T(8,128)(2,1)S(1)}, bf16[64,4096]{1,0:T(8,128)(2,1)S(1)}, u32[]{:S(2)}, u32[]{:S(2)}) collective-permute-start(bf16[64,4096]{1,0:T(8,128)(2,1)S(1)} %collective-permute-done.3.refs_1_.refs_5_), channel_id=1, source_target_pairs={{0,2},{1,3},{2,6},{3,7},{4,0},{5,1},{6,4},{7,5},{8,10},{9,11},{10,... | collective-permute-start | bytes 1572872 | tf_op jit(solution)/shard_map/ppermute | solution.py:211
  20.0 21.3 %collective-permute-start.5 = (bf16[64,4096]{1,0:T(8,128)(2,1)S(1)}, bf16[64,4096]{1,0:T(8,128)(2,1)S(1)}, u32[]{:S(2)}, u32[]{:S(2)}) collective-permute-start(bf16[64,4096]{1,0:T(8,128)(2,1)S(1)} %collective-permute-done.3.refs_1_.refs_5_), channel_id=1, source_target_pairs={{0,1},{1,0},{2,3},{3,2},{4,5},{5,4},{6,7},{7,6},{8,9},{9,8},{10,11... | collective-permute-start | bytes 1572872 | tf_op jit(solution)/shard_map/ppermute | solution.py:212
  20.0 22.2 %copy-start.50 = (s32[128,8]{0,1:T(8,128)S(1)}, s32[128,8]{0,1:T(8,128)}, u32[]{:S(2)}) copy-start(s32[128,8]{0,1:T(8,128)} %param.8) | copy-start | bytes 12292
  20.3 21.9 %copy-start.51 = (s32[128,8]{0,1:T(8,128)S(1)}, s32[128,8]{0,1:T(8,128)}, u32[]{:S(2)}) copy-start(s32[128,8]{0,1:T(8,128)} %param.7) | copy-start | bytes 12292
  20.3 40.4 %collective-permute-start.16 = (bf16[1024,512]{1,0:T(8,128)(2,1)S(1)}, bf16[1024,512]{1,0:T(8,128)(2,1)S(1)}, u32[]{:S(2)}, u32[]{:S(2)}) collective-permute-start(bf16[1024,512]{1,0:T(8,128)(2,1)S(1)} %bitcast.29), channel_id=1, source_target_pairs={{0,24},{8,16},{16,8},{24,0},{1,25},{9,17},{17,9},{25,1},{2,26},{10... | collective-permute-start | bytes 3145736 | tf_op jit(solution)/shard_map/ppermute | solution.py:219
  23.6 45.7 %collective-permute-start.15 = (bf16[1024,512]{1,0:T(8,128)(2,1)S(1)}, bf16[1024,512]{1,0:T(8,128)(2,1)S(1)}, u32[]{:S(2)}, u32[]{:S(2)}) collective-permute-start(bf16[1024,512]{1,0:T(8,128)(2,1)S(1)} %bitcast.30), channel_id=1, source_target_pairs={{0,16},{8,24},{16,0},{24,8},{1,17},{9,25},{17,1},{25,9},{2,18},{10... | collective-permute-start | bytes 3145736 | tf_op jit(solution)/shard_map/ppermute | solution.py:218
  30.2 39.3 %collective-permute-start.14 = (bf16[1024,512]{1,0:T(8,128)(2,1)S(1)}, bf16[1024,512]{1,0:T(8,128)(2,1)}, u32[]{:S(2)}, u32[]{:S(2)}) collective-permute-start(bf16[1024,512]{1,0:T(8,128)(2,1)S(1)} %bitcast.31), channel_id=1, source_target_pairs={{0,8},{8,0},{16,24},{24,16},{1,9},{9,1},{17,25},{25,17},{2,10},{10... | collective-permute-start | bytes 3145736 | tf_op jit(solution)/shard_map/ppermute | solution.py:217
  40.5 14.4 %collective-permute-start.6 = (bf16[64,4096]{1,0:T(8,128)(2,1)}, bf16[64,4096]{1,0:T(8,128)(2,1)}, u32[]{:S(2)}, u32[]{:S(2)}) collective-permute-start(bf16[64,4096]{1,0:T(8,128)(2,1)} %collective-permute-done.2.refs_0_.refs_4_), channel_id=1, source_target_pairs={{0,2},{1,3},{2,6},{3,7},{4,0},{5,1},{6,4},{7,5},{8,10},{9,11},{10,... | collective-permute-start | bytes 1572872 | tf_op jit(solution)/shard_map/ppermute | solution.py:211
  42.2 13.3 %collective-permute-start.4 = (bf16[64,4096]{1,0:T(8,128)(2,1)}, bf16[64,4096]{1,0:T(8,128)(2,1)}, u32[]{:S(2)}, u32[]{:S(2)}) collective-permute-start(bf16[64,4096]{1,0:T(8,128)(2,1)} %collective-permute-done.2.refs_0_.refs_4_), channel_id=1, source_target_pairs={{0,1},{1,0},{2,3},{3,2},{4,5},{5,4},{6,7},{7,6},{8,9},{9,8},{10,11... | collective-permute-start | bytes 1572872 | tf_op jit(solution)/shard_map/ppermute | solution.py:212
  42.8 16.2 %all-to-all-start = ((s32[8,2,128]{2,1,0:T(2,128)}), s32[8,2,128]{2,1,0:T(2,128)S(1)}, u32[]{:S(2)}, u32[]{:S(2)}) async-start(s32[8,2,128]{2,1,0:T(2,128)} %bitcast.3), calls=%async_computation | async-start | bytes 16384 | tf_op jit(solution)/shard_map/all_to_all | solution.py:226
  54.9 16.1 %collective-permute-start.12 = (bf16[64,4096]{1,0:T(8,128)(2,1)}, bf16[64,4096]{1,0:T(8,128)(2,1)}, u32[]{:S(2)}, u32[]{:S(2)}) collective-permute-start(bf16[64,4096]{1,0:T(8,128)(2,1)} %copy-done.12), channel_id=1, source_target_pairs={{0,2},{1,3},{2,6},{3,7},{4,0},{5,1},{6,4},{7,5},{8,10},{9,11},{10,... | collective-permute-start | bytes 1572872 | tf_op jit(solution)/shard_map/ppermute | solution.py:211
  55.5 24.0 %collective-permute-start.10 = (bf16[64,4096]{1,0:T(8,128)(2,1)}, bf16[64,4096]{1,0:T(8,128)(2,1)}, u32[]{:S(2)}, u32[]{:S(2)}) collective-permute-start(bf16[64,4096]{1,0:T(8,128)(2,1)} %collective-permute-done.6.refs_0_.refs_8_), channel_id=1, source_target_pairs={{0,2},{1,3},{2,6},{3,7},{4,0},{5,1},{6,4},{7,5},{8,10},{9,11},{10,... | collective-permute-start | bytes 1572872 | tf_op jit(solution)/shard_map/ppermute | solution.py:211
  60.7 23.9 %collective-permute-start = (bf16[64,4096]{1,0:T(8,128)(2,1)}, bf16[64,4096]{1,0:T(8,128)(2,1)S(1)}, u32[]{:S(2)}, u32[]{:S(2)}) collective-permute-start(bf16[64,4096]{1,0:T(8,128)(2,1)} %copy-done.3), channel_id=1, source_target_pairs={{0,1},{1,0},{2,3},{3,2},{4,5},{5,4},{6,7},{7,6},{8,9},{9,8},{10,11... | collective-permute-start | bytes 1572872 | tf_op jit(solution)/shard_map/ppermute | solution.py:212
  69.3 19.3 %collective-permute-start.9 = (bf16[64,4096]{1,0:T(8,128)(2,1)}, bf16[64,4096]{1,0:T(8,128)(2,1)S(1)}, u32[]{:S(2)}, u32[]{:S(2)}) collective-permute-start(bf16[64,4096]{1,0:T(8,128)(2,1)} %copy-done.12), channel_id=1, source_target_pairs={{0,1},{1,0},{2,3},{3,2},{4,5},{5,4},{6,7},{7,6},{8,9},{9,8},{10,11... | collective-permute-start | bytes 1572872 | tf_op jit(solution)/shard_map/ppermute | solution.py:212
  69.5 19.1 %collective-permute-start.8 = (bf16[64,4096]{1,0:T(8,128)(2,1)}, bf16[64,4096]{1,0:T(8,128)(2,1)S(1)}, u32[]{:S(2)}, u32[]{:S(2)}) collective-permute-start(bf16[64,4096]{1,0:T(8,128)(2,1)} %collective-permute-done.6.refs_0_.refs_8_), channel_id=1, source_target_pairs={{0,1},{1,0},{2,3},{3,2},{4,5},{5,4},{6,7},{7,6},{8,9},{9,8},{10,11... | collective-permute-start | bytes 1572872 | tf_op jit(solution)/shard_map/ppermute | solution.py:212
  69.8 10.5 %copy-start.7 = (bf16[64,4096]{1,0:T(8,128)(2,1)S(1)}, bf16[64,4096]{1,0:T(8,128)(2,1)}, u32[]{:S(2)}) copy-start(bf16[64,4096]{1,0:T(8,128)(2,1)} %copy-done.6) | copy-start | bytes 1572868
  69.8 10.5 %copy-start.16 = (bf16[64,4096]{1,0:T(8,128)(2,1)S(1)}, bf16[64,4096]{1,0:T(8,128)(2,1)}, u32[]{:S(2)}) copy-start(bf16[64,4096]{1,0:T(8,128)(2,1)} %copy-done.15) | copy-start | bytes 1572868
  71.0 21.3 %collective-permute-start.13 = (bf16[64,4096]{1,0:T(8,128)(2,1)}, bf16[64,4096]{1,0:T(8,128)(2,1)S(1)}, u32[]{:S(2)}, u32[]{:S(2)}) collective-permute-start(bf16[64,4096]{1,0:T(8,128)(2,1)} %collective-permute-done.12.refs_0_.refs_14_), channel_id=1, source_target_pairs={{0,1},{1,0},{2,3},{3,2},{4,5},{5,4},{6,7},{7,6},{8,9},{9,8},{10,11... | collective-permute-start | bytes 1572872 | tf_op jit(solution)/shard_map/ppermute | solution.py:212
  79.5 16.3 %collective-permute-start.11 = (bf16[64,4096]{1,0:T(8,128)(2,1)}, bf16[64,4096]{1,0:T(8,128)(2,1)S(1)}, u32[]{:S(2)}, u32[]{:S(2)}) collective-permute-start(bf16[64,4096]{1,0:T(8,128)(2,1)} %collective-permute-done.10.refs_0_.refs_12_), channel_id=1, source_target_pairs={{0,1},{1,0},{2,3},{3,2},{4,5},{5,4},{6,7},{7,6},{8,9},{9,8},{10,11... | collective-permute-start | bytes 1572872 | tf_op jit(solution)/shard_map/ppermute | solution.py:212
  84.6 13.8 %copy-start.18 = (bf16[64,4096]{1,0:T(8,128)(2,1)}, bf16[64,4096]{1,0:T(8,128)(2,1)S(1)}, u32[]{:S(2)}) copy-start(bf16[64,4096]{1,0:T(8,128)(2,1)S(1)} %collective-permute-done.refs_2_) | copy-start | bytes 1572868
  88.6 9.9 %copy-start.32 = (bf16[256,512]{1,0:T(8,128)(2,1)}, bf16[256,512]{1,0:T(8,128)(2,1)S(1)}, u32[]{:S(2)}) copy-start(bf16[256,512]{1,0:T(8,128)(2,1)S(1)} %get-tuple-element.20.refs_16_) | copy-start | bytes 786436
  88.6 9.9 %copy-start.21 = (bf16[64,4096]{1,0:T(8,128)(2,1)}, bf16[64,4096]{1,0:T(8,128)(2,1)S(1)}, u32[]{:S(2)}) copy-start(bf16[64,4096]{1,0:T(8,128)(2,1)S(1)} %collective-permute-done.9.refs_3_.refs_11_) | copy-start | bytes 1572868
  88.6 9.9 %copy-start.24 = (bf16[64,4096]{1,0:T(8,128)(2,1)}, bf16[64,4096]{1,0:T(8,128)(2,1)S(1)}, u32[]{:S(2)}) copy-start(bf16[64,4096]{1,0:T(8,128)(2,1)S(1)} %collective-permute-done.8.refs_2_.refs_10_) | copy-start | bytes 1572868
  92.3 6.2 %copy-start.35 = (bf16[256,512]{1,0:T(8,128)(2,1)}, bf16[256,512]{1,0:T(8,128)(2,1)S(1)}, u32[]{:S(2)}) copy-start(bf16[256,512]{1,0:T(8,128)(2,1)S(1)} %get-tuple-element.22.refs_18_) | copy-start | bytes 786436
  92.3 6.2 %copy-start.27 = (bf16[64,4096]{1,0:T(8,128)(2,1)}, bf16[64,4096]{1,0:T(8,128)(2,1)S(1)}, u32[]{:S(2)}) copy-start(bf16[64,4096]{1,0:T(8,128)(2,1)S(1)} %collective-permute-done.13.refs_1_.refs_15_) | copy-start | bytes 1572868
  98.4 4.8 %copy-start.38 = (bf16[128,512]{1,0:T(8,128)(2,1)}, bf16[128,512]{1,0:T(8,128)(2,1)S(1)}, u32[]{:S(2)}) copy-start(bf16[128,512]{1,0:T(8,128)(2,1)S(1)} %get-tuple-element.23.refs_19_) | copy-start | bytes 393220
  98.4 4.8 %copy-start.47 = (f32[128,1]{1,0:T(8,128)}, f32[128,1]{1,0:T(8,128)S(1)}, u32[]{:S(2)}) copy-start(f32[128,1]{1,0:T(8,128)S(1)} %get-tuple-element.36) | copy-start | bytes 1540
  98.5 23.1 %copy-start.5 = (bf16[64,4096]{1,0:T(8,128)(2,1)S(1)}, bf16[64,4096]{1,0:T(8,128)(2,1)}, u32[]{:S(2)}) copy-start(bf16[64,4096]{1,0:T(8,128)(2,1)} %copy-done.3) | copy-start | bytes 1572868
  98.5 23.1 %copy-start.8 = (bf16[64,4096]{1,0:T(8,128)(2,1)S(1)}, bf16[64,4096]{1,0:T(8,128)(2,1)}, u32[]{:S(2)}) copy-start(bf16[64,4096]{1,0:T(8,128)(2,1)} %copy-done.6) | copy-start | bytes 1572868
  98.5 23.1 %copy-start.11 = (bf16[64,4096]{1,0:T(8,128)(2,1)S(1)}, bf16[64,4096]{1,0:T(8,128)(2,1)}, u32[]{:S(2)}) copy-start(bf16[64,4096]{1,0:T(8,128)(2,1)} %copy-done.9) | copy-start | bytes 1572868
  98.5 23.1 %copy-start.14 = (bf16[64,4096]{1,0:T(8,128)(2,1)S(1)}, bf16[64,4096]{1,0:T(8,128)(2,1)}, u32[]{:S(2)}) copy-start(bf16[64,4096]{1,0:T(8,128)(2,1)} %copy-done.12) | copy-start | bytes 1572868
  98.5 23.1 %copy-start.17 = (bf16[64,4096]{1,0:T(8,128)(2,1)S(1)}, bf16[64,4096]{1,0:T(8,128)(2,1)}, u32[]{:S(2)}) copy-start(bf16[64,4096]{1,0:T(8,128)(2,1)} %copy-done.15) | copy-start | bytes 1572868
  104.1 17.6 %copy-start.2 = (bf16[64,4096]{1,0:T(8,128)(2,1)S(1)}, bf16[64,4096]{1,0:T(8,128)(2,1)}, u32[]{:S(2)}) copy-start(bf16[64,4096]{1,0:T(8,128)(2,1)} %copy-done) | copy-start | bytes 1572868
  104.1 35.5 %collective-permute-start.21 = (bf16[1024,256]{1,0:T(8,128)(2,1)}, bf16[1024,256]{1,0:T(8,128)(2,1)}, u32[]{:S(2)}, u32[]{:S(2)}) collective-permute-start(bf16[1024,256]{1,0:T(8,128)(2,1)} %get-tuple-element.32), channel_id=1, source_target_pairs={{0,16},{8,24},{16,0},{24,8},{1,17},{9,25},{17,1},{25,9},{2,18},{10... | collective-permute-start | bytes 1572872 | tf_op jit(solution)/shard_map/ppermute | solution.py:253
  105.1 38.0 %collective-permute-start.18 = (bf16[1024,256]{1,0:T(8,128)(2,1)}, bf16[1024,256]{1,0:T(8,128)(2,1)}, u32[]{:S(2)}, u32[]{:S(2)}) collective-permute-start(bf16[1024,256]{1,0:T(8,128)(2,1)} %copy-done.48), channel_id=1, source_target_pairs={{0,8},{8,0},{16,24},{24,16},{1,9},{9,1},{17,25},{25,17},{2,10},{10... | collective-permute-start | bytes 1572872 | tf_op jit(solution)/shard_map/ppermute | solution.py:252
  116.7 36.0 %all-to-all-start.1 = ((f32[8,1,128]{2,1,0:T(1,128)}), f32[8,1,128]{2,1,0:T(1,128)S(1)}, u32[]{:S(2)}, u32[]{:S(2)}) async-start(f32[8,1,128]{2,1,0:T(1,128)} %bitcast.15), calls=%async_computation.1 | async-start | bytes 8192 | tf_op jit(solution)/shard_map/all_to_all | solution.py:271
  134.1 19.1 %collective-permute-start.20 = (bf16[1024,256]{1,0:T(8,128)(2,1)}, bf16[1024,256]{1,0:T(8,128)(2,1)}, u32[]{:S(2)}, u32[]{:S(2)}) collective-permute-start(bf16[1024,256]{1,0:T(8,128)(2,1)} %get-tuple-element.30), channel_id=1, source_target_pairs={{0,16},{8,24},{16,0},{24,8},{1,17},{9,25},{17,1},{25,9},{2,18},{10... | collective-permute-start | bytes 1572872 | tf_op jit(solution)/shard_map/ppermute | solution.py:257
  139.0 27.4 %collective-permute-start.17 = (bf16[1024,256]{1,0:T(8,128)(2,1)}, bf16[1024,256]{1,0:T(8,128)(2,1)}, u32[]{:S(2)}, u32[]{:S(2)}) collective-permute-start(bf16[1024,256]{1,0:T(8,128)(2,1)} %get-tuple-element.26), channel_id=1, source_target_pairs={{0,8},{8,0},{16,24},{24,16},{1,9},{9,1},{17,25},{25,17},{2,10},{10... | collective-permute-start | bytes 1572872 | tf_op jit(solution)/shard_map/ppermute | solution.py:255
  139.5 7.1 %copy-start.34 = (bf16[256,512]{1,0:T(8,128)(2,1)S(1)}, bf16[256,512]{1,0:T(8,128)(2,1)}, u32[]{:S(2)}) copy-start(bf16[256,512]{1,0:T(8,128)(2,1)} %copy-done.32) | copy-start | bytes 786436
  139.5 7.2 %copy-start.37 = (bf16[256,512]{1,0:T(8,128)(2,1)S(1)}, bf16[256,512]{1,0:T(8,128)(2,1)}, u32[]{:S(2)}) copy-start(bf16[256,512]{1,0:T(8,128)(2,1)} %copy-done.35) | copy-start | bytes 786436
  141.5 23.1 %collective-permute-start.22 = (bf16[1024,256]{1,0:T(8,128)(2,1)}, bf16[1024,256]{1,0:T(8,128)(2,1)}, u32[]{:S(2)}, u32[]{:S(2)}) collective-permute-start(bf16[1024,256]{1,0:T(8,128)(2,1)} %add_convert_fusion.1), channel_id=1, source_target_pairs={{0,8},{8,0},{16,24},{24,16},{1,9},{9,1},{17,25},{25,17},{2,10},{10... | collective-permute-start | bytes 1572872 | tf_op jit(solution)/shard_map/ppermute | solution.py:260
  145.2 21.2 %collective-permute-start.19 = (bf16[1024,256]{1,0:T(8,128)(2,1)}, bf16[1024,256]{1,0:T(8,128)(2,1)}, u32[]{:S(2)}, u32[]{:S(2)}) collective-permute-start(bf16[1024,256]{1,0:T(8,128)(2,1)} %add_convert_fusion.3), channel_id=1, source_target_pairs={{0,16},{8,24},{16,0},{24,8},{1,17},{9,25},{17,1},{25,9},{2,18},{10... | collective-permute-start | bytes 1572872 | tf_op jit(solution)/shard_map/ppermute | solution.py:259
  (29 other events, 55.2 us)

commit v2 on v0

--- a/solution.py
+++ b/solution.py
@@ -1,10 +1,19 @@
+import functools
+
 import jax
 import jax.numpy as jnp
 from jax import lax
+from jax.experimental import pallas as pl
+from jax.experimental.pallas import tpu as pltpu
 from jax.sharding import PartitionSpec as P
 
 inv_temp = 2.0
 grad_scale = 0.03125
+
+ring_next = (1, 3, 0, 2)
+ring_prev = (2, 0, 3, 1)
+kernel_vmem = 58 << 20
+lanes = 128
 
 
 def slot_tables(matches, positives, clusters, capacity):
@@ -36,7 +45,7 @@
     return (slot_loss, gradients)
 
 
-def body(samples, weight, matches, positives):
+def slot_body(samples, weight, matches, positives):
     row_count, feat_width = samples.shape
     groups = lax.axis_size("label")
     local_count = weight.shape[1]
@@ -52,17 +61,15 @@
     )
     incoming = incoming.reshape(groups, local_count, capacity, feat_width)
     labels = labels.reshape(groups, local_count, capacity)
-    column_part = incoming
     scores = jnp.einsum(
         "scpd,dcl->scpl",
-        column_part,
+        incoming,
         lax.all_gather(weight, "dp", axis=0, tiled=True),
         preferred_element_type=jnp.float32,
     )
     slot_loss, gradients = slot_terms(scores, labels)
-    column_part = incoming
     weight_grad = lax.psum_scatter(
-        jnp.einsum("scpd,scpl->dcl", column_part, gradients, preferred_element_type=jnp.float32),
+        jnp.einsum("scpd,scpl->dcl", incoming, gradients, preferred_element_type=jnp.float32),
         "dp",
         scatter_dimension=0,
         tiled=True,
@@ -75,6 +82,339 @@
     return (weight_grad, sample_loss)
 
 
+def pack_kernel(parts, samples_ref, matches_ref, positives_ref, next_ref, *outs):
+    next_ref[0] = 0
+    rows, feat_width = samples_ref.shape
+    part = rows // parts
+    cluster = lax.broadcasted_iota(jnp.int32, (lanes, rows), 0)
+    code = jnp.zeros((lanes, rows), jnp.int32)
+    for pick in range(matches_ref.shape[0]):
+        hit = cluster == matches_ref[pick : pick + 1]
+        code = code + jnp.where(hit, positives_ref[pick : pick + 1] + 1, 0)
+    code = code.astype(jnp.float32).T.astype(jnp.bfloat16)
+    for place, out in enumerate(outs):
+        span = slice(place * part, (place + 1) * part)
+        out[:, :feat_width] = samples_ref[span]
+        out[:, feat_width:] = code[span]
+
+
+def pack_call(samples, matches, positives, parts):
+    rows, feat_width = samples.shape
+    whole = pl.BlockSpec(memory_space=pltpu.VMEM)
+    block = jax.ShapeDtypeStruct((rows // parts, feat_width + lanes), jnp.bfloat16)
+    return pl.pallas_call(
+        functools.partial(pack_kernel, parts),
+        out_shape=(jax.ShapeDtypeStruct((1,), jnp.int32),) + (block,) * parts,
+        in_specs=[whole, whole, whole],
+        out_specs=(pl.BlockSpec(memory_space=pltpu.SMEM),) + (whole,) * parts,
+        compiler_params=pltpu.CompilerParams(vmem_limit_bytes=8 << 20),
+        name="pack",
+    )(samples, matches.T, positives.T)
+
+
+def load(sources, targets, sems):
+    copies = [
+        pltpu.make_async_copy(source, target, sems.at[place])
+        for place, (source, target) in enumerate(zip(sources, targets, strict=True))
+    ]
+    for copy in copies:
+        copy.start()
+    return copies
+
+
+def row_scores(me, xs, ws, copies, places, depth):
+    scores = None
+    for w, copy, (offset, first) in zip(ws, copies, places, strict=True):
+        if copy is not None:
+            copy.wait()
+        start = pl.multiple_of((me ^ offset) * depth + first, w.shape[0])
+        rows = jnp.concatenate([x[:, pl.ds(start, w.shape[0])] for x in xs], axis=0)
+        part = jnp.dot(rows, w[...], preferred_element_type=jnp.float32)
+        scores = part if scores is None else scores + part
+    return scores
+
+
+def row_terms(scores, xs, label, local_count, grad_ref, loss_ref, at):
+    feat_width = xs[0].shape[1] - lanes
+    codes = jnp.concatenate([x[:, feat_width:] for x in xs], axis=0).astype(jnp.float32)
+    count = codes.shape[0]
+    lane = lax.broadcasted_iota(jnp.int32, codes.shape, 1)
+    label_count = scores.shape[1] // local_count
+    label_ids = lax.broadcasted_iota(jnp.int32, (count, label_count), 1) + 1
+    label_ids = label_ids.astype(jnp.float32)
+    loss = None
+    for cluster in range(local_count):
+        span = slice(cluster * label_count, (cluster + 1) * label_count)
+        mine = lane == label * local_count + cluster
+        code = jnp.sum(jnp.where(mine, codes, 0.0), axis=1, keepdims=True)
+        logits = scores[:, span] * inv_temp
+        hit = label_ids == code
+        decay = jnp.exp(-jnp.abs(logits))
+        each = jnp.maximum(logits, 0.0) + jnp.log1p(decay) - jnp.where(hit, logits, 0.0)
+        share = jnp.where(logits >= 0.0, 1.0, decay) / (1.0 + decay)
+        valid = code > 0.0
+        grad = (share - jnp.where(hit, 1.0, 0.0)) * (inv_temp * grad_scale)
+        grad_ref[span, at : at + count] = jnp.where(valid, grad, 0.0).T.astype(jnp.bfloat16)
+        sums = jnp.where(valid, jnp.sum(each, axis=1, keepdims=True), 0.0)
+        loss = sums if loss is None else loss + sums
+    loss_ref[:, at : at + count] = jnp.broadcast_to(loss, (count, lanes)).T[0:1]
+
+
+def stage_kernel(groups, places, depth, local_count, offsets, adds, *refs):
+    take = iter(refs)
+
+    def some(count):
+        return [next(take) for _ in range(count)]
+
+    (where_ref,) = some(1)
+    ins = some(sum(groups) + len(places) + adds)
+    next_ref, grad_ref, loss_ref = some(3)
+    outs = some(len(offsets) * (local_count if adds else 1))
+    xs, ws, sums = some(sum(groups)), some(len(places)), some(adds)
+    (sems,), totals = some(1), some(1 - adds)
+    me, label = where_ref[0], where_ref[1]
+    next_ref[0] = me
+    next_ref[1] = label
+    copies = load(ins, xs + ws + sums, sems)
+    weight_copies = copies[len(xs) : len(xs) + len(ws)]
+    first, at = 0, 0
+    for size in groups:
+        for copy in copies[first : first + size]:
+            copy.wait()
+        group = xs[first : first + size]
+        scores = row_scores(me, group, ws, weight_copies, places, depth)
+        weight_copies = [None] * len(ws)
+        row_terms(scores, group, label, local_count, grad_ref, loss_ref, at)
+        first, at = first + size, at + scores.shape[0]
+    for copy in copies[len(xs) + len(ws) :]:
+        copy.wait()
+    grads = grad_ref[...]
+    tile = 256
+    for place, offset in enumerate(offsets):
+        for step in range(depth // tile):
+            start = pl.multiple_of((me ^ offset) * depth + step * tile, tile)
+            span = slice(step * tile, (step + 1) * tile)
+            rows = jnp.concatenate([x[:, pl.ds(start, tile)] for x in xs], axis=0)
+            total = jnp.dot(grads, rows, preferred_element_type=jnp.float32)
+            if not adds:
+                totals[0][place, :, span] = total
+                continue
+            total = total + sums[0][:, span]
+            width = total.shape[0] // local_count
+            for cluster in range(local_count):
+                part = total[cluster * width : (cluster + 1) * width]
+                outs[place * local_count + cluster][:, span] = part.astype(jnp.bfloat16)
+        if not adds:
+            pltpu.make_async_copy(totals[0].at[place], outs[place], sems.at[place]).start()
+    if not adds:
+        for place, out in enumerate(outs):
+            pltpu.make_async_copy(totals[0].at[place], out, sems.at[place]).wait()
+
+
+any_space = pl.BlockSpec(memory_space=pl.ANY)
+whole = pl.BlockSpec(memory_space=pltpu.VMEM)
+scalar = pl.BlockSpec(memory_space=pltpu.SMEM)
+
+
+def stage_call(where, groups, ws, places, local_count, offsets, sums=()):
+    xs = [x for group in groups for x in group]
+    rows = sum(x.shape[0] for x in xs)
+    feat_width = xs[0].shape[1] - lanes
+    depth, columns = ws[0].shape
+    inputs = [*xs, *ws, *sums]
+    scratch = [pltpu.VMEM(array.shape, array.dtype) for array in inputs]
+    scratch.append(pltpu.SemaphoreType.DMA((len(inputs),)))
+    if sums:
+        part = jax.ShapeDtypeStruct((columns // local_count, depth), jnp.bfloat16)
+        outs = [part] * (local_count * len(offsets))
+    else:
+        outs = [jax.ShapeDtypeStruct((columns, depth), jnp.float32)] * len(offsets)
+        scratch.append(pltpu.VMEM((len(offsets), columns, depth), jnp.float32))
+    return pl.pallas_call(
+        functools.partial(
+            stage_kernel,
+            tuple(len(group) for group in groups),
+            places,
+            depth,
+            local_count,
+            offsets,
+            len(sums),
+        ),
+        out_shape=(
+            jax.ShapeDtypeStruct((2,), jnp.int32),
+            jax.ShapeDtypeStruct((columns, rows), jnp.bfloat16),
+            jax.ShapeDtypeStruct((1, rows), jnp.float32),
+            *outs,
+        ),
+        in_specs=[scalar] + [any_space] * len(inputs),
+        out_specs=(scalar, whole, whole) + ((whole,) if sums else (any_space,)) * len(outs),
+        scratch_shapes=scratch,
+        compiler_params=pltpu.CompilerParams(vmem_limit_bytes=kernel_vmem),
+        cost_estimate=pl.CostEstimate(
+            flops=2 * rows * columns * (feat_width + depth * len(offsets)),
+            bytes_accessed=2 * (rows + columns) * feat_width + 4 * columns * depth * len(offsets),
+            transcendentals=2 * rows * columns,
+        ),
+        name="stage",
+    )(where, *inputs)
+
+
+def part_kernel(offset, lows, blocks, parts, gots, *refs):
+    where_ref, refs = refs[0], refs[1:]
+    xs_in, gs_in, refs = refs[:blocks], refs[blocks : blocks + parts], refs[blocks + parts :]
+    sums_in, gots_in, refs = refs[0], refs[1 : 1 + gots], refs[1 + gots :]
+    next_ref, out_ref, held, gs, sums = refs[:5]
+    got, sems = refs[5], refs[-1]
+    next_ref[0] = where_ref[0]
+    next_ref[1] = where_ref[1]
+    width, depth = out_ref.shape
+    begin = pl.multiple_of((where_ref[0] ^ offset) * depth, depth)
+    sources = [x.at[:, pl.ds(begin, depth)] for x in xs_in]
+    targets, at = [], 0
+    for x in xs_in:
+        targets.append(held.at[pl.ds(at, x.shape[0])])
+        at += x.shape[0]
+    at = 0
+    for g in gs_in:
+        sources.append(g.at[pl.ds(lows, width)])
+        targets.append(gs.at[:, pl.ds(at, g.shape[1])])
+        at += g.shape[1]
+    sources.append(sums_in.at[pl.ds(lows, width)])
+    targets.append(sums)
+    if gots_in:
+        sources.append(gots_in[0])
+        targets.append(got)
+    for copy in load(sources, targets, sems):
+        copy.wait()
+    tile = 256
+    for step in range(depth // tile):
+        span = slice(step * tile, (step + 1) * tile)
+        total = jnp.dot(gs[...], held[:, span], preferred_element_type=jnp.float32)
+        total = total + sums[:, span]
+        if gots_in:
+            total = total + got[:, span].astype(jnp.float32)
+        out_ref[:, span] = total.astype(out_ref.dtype)
+
+
+def part_call(where, offset, lows, width, kind, xs, gs, sums, got=()):
+    rows = sum(x.shape[0] for x in xs)
+    depth = sums.shape[1]
+    count = len(xs) + len(gs) + 1 + len(got)
+    return pl.pallas_call(
+        functools.partial(part_kernel, offset, lows, len(xs), len(gs), len(got)),
+        out_shape=(
+            jax.ShapeDtypeStruct((2,), jnp.int32),
+            jax.ShapeDtypeStruct((width, depth), kind),
+        ),
+        in_specs=[scalar] + [any_space] * count,
+        out_specs=(scalar, whole),
+        scratch_shapes=[
+            pltpu.VMEM((rows, depth), jnp.bfloat16),
+            pltpu.VMEM((width, rows), jnp.bfloat16),
+            pltpu.VMEM((width, depth), jnp.float32),
+            *(pltpu.VMEM((width, depth), jnp.bfloat16) for _ in got),
+            pltpu.SemaphoreType.DMA((count,)),
+        ],
+        compiler_params=pltpu.CompilerParams(vmem_limit_bytes=kernel_vmem),
+        cost_estimate=pl.CostEstimate(
+            flops=2 * rows * depth * width,
+            bytes_accessed=2 * rows * depth + 6 * depth * width,
+            transcendentals=0,
+        ),
+        name="part",
+    )(where, *xs, *gs, sums, *got)
+
+
+def after(value, *earlier):
+    return lax.optimization_barrier((value, earlier))[0]
+
+
+def ring_body(samples, weight, matches, positives):
+    row_count, feat_width = samples.shape
+    depth, local_count, label_count = weight.shape
+    groups = lax.axis_size("label")
+    pick_count = matches.shape[1]
+    clusters = groups * local_count
+    dp = lax.axis_index("dp")
+    label = lax.axis_index("label")
+    where = jnp.stack([dp, label]).astype(jnp.int32)
+
+    chips = groups // 2
+    hop = [(z * 2 + c, ring_next[z] * 2 + c) for z in range(chips) for c in range(2)]
+    swap = [(i, i ^ 1) for i in range(groups)]
+    along_x = [(i, i ^ 1) for i in range(4)]
+    along_y = [(i, i ^ 2) for i in range(4)]
+
+    packed, block = pack_call(samples, matches, positives, 1)
+    flat = after(weight.reshape(depth, local_count * label_count), packed)
+    half = depth // 2
+    mine = [block]
+    mine.append(lax.ppermute(block, "label", hop))
+    w_x = lax.ppermute(flat, "dp", along_x)
+    w_y = lax.ppermute(flat, "dp", along_y)
+    mine[1] = after(mine[1], w_x, w_y)
+    mine.append(lax.ppermute(mine[1], "label", hop))
+    far_x = lax.ppermute(w_x[:half], "dp", along_y)
+    far_y = lax.ppermute(w_y[half:], "dp", along_x)
+    mine[2] = after(mine[2], far_x, far_y)
+    ws = [flat, w_x, w_y, far_x, far_y]
+    places = ((0, 0), (1, 0), (2, 0), (3, 0), (3, half))
+    early = [[block, lax.ppermute(block, "label", swap)] for block in mine]
+
+    offsets = (3, 1, 2, 0)
+    last = lax.ppermute(mine[-1], "label", hop)
+    token, _, loss, *sums = stage_call(where, early, ws, places, local_count, offsets)
+    last = after(last, token)
+    losses = [loss]
+    sums = dict(zip(offsets, sums))
+
+    low, full = jnp.bfloat16, jnp.float32
+    xs = [last, lax.ppermute(last, "label", swap)]
+    token, grads, loss, far_0, far_1 = stage_call(
+        token, [xs], ws, places, local_count, (3,), (sums[3],)
+    )
+    losses.append(loss)
+    far_x = lax.ppermute(far_0, "dp", along_x)
+    far_y = lax.ppermute(far_1, "dp", along_y)
+    gs = [grads]
+    order = []
+    for z in range(chips):
+        for c in range(2):
+            at, rows = z, []
+            for _ in range(chips):
+                rows.append([at * 2 + c, at * 2 + 1 - c])
+                at = ring_prev[at]
+            order.append(rows)
+    order = jnp.array(order, jnp.int32)[label]
+
+    width = label_count
+    token, near_x = part_call(token, 1, 0, width, low, xs, gs, sums[1])
+    got_x = lax.ppermute(near_x, "dp", along_x)
+    token, near_y = part_call(token, 2, width, width, low, xs, gs, sums[2])
+    got_y = lax.ppermute(near_y, "dp", along_y)
+    token, own = part_call(token, 0, 0, 2 * width, full, xs, gs, sums[0])
+    token, on_y = part_call(token, 2, 0, width, low, xs, gs, sums[2], (far_x,))
+    pass_y = lax.ppermute(on_y, "dp", along_y)
+    token, on_x = part_call(token, 1, width, width, low, xs, gs, sums[1], (far_y,))
+    pass_x = lax.ppermute(on_x, "dp", along_x)
+    by_step = after(jnp.concatenate(losses, axis=1).reshape(groups, row_count), token)
+    total = jnp.zeros((groups, row_count), jnp.float32)
+    total = total.at[order.reshape(-1)].set(by_step)
+    returned = lax.all_to_all(total, "label", split_axis=0, concat_axis=0, tiled=True)
+    sample_loss = jnp.sum(returned, axis=0) / (pick_count * label_count)
+
+    first = own[:width] + got_x.astype(jnp.float32) + pass_y.astype(jnp.float32)
+    second = own[width:] + got_y.astype(jnp.float32) + pass_x.astype(jnp.float32)
+    weight_grad = jnp.transpose(jnp.stack([first, second]), (2, 0, 1)).astype(jnp.bfloat16)
+    return (weight_grad, sample_loss)
+
+
+def body(samples, weight, matches, positives):
+    if (lax.axis_size("dp"), lax.axis_size("label"), weight.shape[1]) == (4, 8, 2):
+        return ring_body(samples, weight, matches, positives)
+    return slot_body(samples, weight, matches, positives)
+
+
 def solution(mesh):
     placed = (
         P(("dp", "label"), None),

time: 532 us -> 139 us (0.26)
  waiting for transfers between devices: 437 us -> 55.2 us
  Pallas kernels: 0 us -> 40.2 us
  local copies, waits for them, and re-layouts: 35.8 us -> 8.9 us
  matrix products: 21.5 us -> 0 us
  between operations: 14.2 us -> 0.85 us
  blocking collectives: 0 us -> 10.2 us
    all_to_all x3 -> x0, waiting for transfers between devices: 312 us -> none  [the longest x1 306 us: body(): lax.all_to_all(outgoing, 'label', split_axis=0, concat_axis=0, tiled=True)]
    reduce_scatter x1 -> x0, waiting for transfers between devices: 69.1 us -> none  [body(): lax.psum_scatter(jnp.einsum('scpd,scpl->dcl', column_part, gradients, pre...]
    all_gather x1 -> x0, waiting for transfers between devices: 56.1 us -> none  [body(): lax.all_gather(weight, 'dp', axis=0, tiled=True)]
    ppermute x0 -> x17, waiting for transfers between devices: none -> 55.2 us  [the longest x1 21.6 us: ring_body(): w_x = lax.ppermute(flat, 'dp', along_x)]
    pallas_call x0 -> x8, Pallas kernels: none -> 40.2 us  [the longest x2 21.9 us: stage_call(): pl.pallas_call(functools.partial(stage_kernel, tuple((len(group) for grou...]
    dot_general x2 -> x0, matrix products: 21.5 us -> none  [the longest x1 10.8 us: body(): jnp.einsum('scpd,dcl->scpl', column_part, lax.all_gather(weight, 'dp', ax...]
    gather x2 -> x0, local copies, waits for them, and re-layouts: 20.5 us -> none  [the longest x1 14.3 us: body(): outgoing = samples[slot_row].reshape(clusters, capacity, feat_width)]
    ppermute x0 -> x17, starting transfers between devices: none -> 19.7 us  [the longest x1 3.08 us: ring_body(): mine.append(lax.ppermute(block, 'label', hop))]
  transfers between devices with their start and end apart: 5 -> 17, of which waited for: 4 -> 8; matrix products, arithmetic and copies ran while one was open for 5% -> 2% of each run, Pallas kernels for 0% -> 24%
where the time goes in v2:
time: 139 us; the launch traced here: 138 us
  waiting for transfers between devices  55.2 us (40%)
  Pallas kernels  40.2 us (29%)
  starting transfers between devices  19.7 us (14%)
  blocking collectives  10.2 us (7%)
  local copies, waits for them, and re-layouts  8.9 us (6%)
  other arithmetic  3.02 us (2%)
    pallas_call x2, Pallas kernels, stage_call(): pl.pallas_call(functools.partial(stage_kernel, tuple((len(group) for grou...  21.9 us
    ppermute x1, waiting for transfers between devices, ring_body(): w_x = lax.ppermute(flat, 'dp', along_x)  21.6 us
    pallas_call x5, Pallas kernels, part_call(): pl.pallas_call(functools.partial(part_kernel, offset, lows, len(xs), len(...  17.8 us
    all_to_all x1, blocking collectives, ring_body(): lax.all_to_all(total, 'label', split_axis=0, concat_axis=0, tiled=True)  10.2 us
    ppermute x1, waiting for transfers between devices, ring_body(): mine.append(lax.ppermute(mine[1], 'label', hop))  9.5 us
    ppermute x1, waiting for transfers between devices, ring_body(): far_x = lax.ppermute(w_x[:half], 'dp', along_y)  9.23 us
    ppermute x1, waiting for transfers between devices, ring_body(): last = lax.ppermute(mine[-1], 'label', hop)  8.87 us
    unnamed x36, local copies, waits for them, and re-layouts  7.46 us
  transfers between devices with their start and end apart: 17, of which 8 were waited for; matrix products, arithmetic and copies ran while one was open for 2% of the time, Pallas kernels for 24%

profile of v2, /device:TPU:0, one launch (start us, length us, event | category | flops | bytes accessed | tf_op | source)
XLA Modules:
  0.0 138.1 jit_solution(9979645934245558003)
XLA Ops:
  0.6 1.2 copy-done
  1.9 0.7 copy-done.1
  2.5 0.7 copy-done.2
  3.2 0.5 pack.1
  3.8 3.1 %collective-permute-start.1 = (bf16[128,4224]{1,0:T(8,128)(2,1)S(1)}, bf16[128,4224]{1,0:T(8,128)(2,1)}, u32[]{:S(2)}, u32[]{:S(2)}) collective-permute-start(bf16[128,4224]{1,0:T(8,128)(2,1)S(1)} %get-tuple-element.26.refs_1_), channel_id=1, source_target_pairs={{0,2},{1,3},{2,6},{3,7},{4,0},{5,1},{6,4},{7,5},{8,10},{9,11},{10,... | collective-permute-start | bytes 3244040 | tf_op jit(solution)/shard_map/ppermute | solution.py:352
  6.9 0.2 copy.10
  7.1 0.0 copy-start.6
  7.1 1.6 %collective-permute-start.2 = (bf16[1024,512]{1,0:T(8,128)(2,1)S(1)}, bf16[1024,512]{1,0:T(8,128)(2,1)S(1)}, u32[]{:S(2)}, u32[]{:S(2)}) collective-permute-start(bf16[1024,512]{1,0:T(8,128)(2,1)S(1)} %bitcast.18), channel_id=1, source_target_pairs={{0,8},{8,0},{16,24},{24,16},{1,9},{9,1},{17,25},{25,17},{2,10},{10... | collective-permute-start | bytes 3145736 | tf_op jit(solution)/shard_map/ppermute | solution.py:353
  8.7 1.5 %collective-permute-start.3 = (bf16[1024,512]{1,0:T(8,128)(2,1)S(1)}, bf16[1024,512]{1,0:T(8,128)(2,1)S(1)}, u32[]{:S(2)}, u32[]{:S(2)}) collective-permute-start(bf16[1024,512]{1,0:T(8,128)(2,1)S(1)} %bitcast.19), channel_id=1, source_target_pairs={{0,16},{8,24},{16,0},{24,8},{1,17},{9,25},{17,1},{25,9},{2,18},{10... | collective-permute-start | bytes 3145736 | tf_op jit(solution)/shard_map/ppermute | solution.py:354
  10.2 21.6 %collective-permute-done.2.refs_8_.refs_4_ = bf16[1024,512]{1,0:T(8,128)(2,1)S(1)} collective-permute-done((bf16[1024,512]{1,0:T(8,128)(2,1)S(1)}, bf16[1024,512]{1,0:T(8,128)(2,1)S(1)}, u32[]{:S(2)}, u32[]{:S(2)}) %collective-permute-start.2) | collective-permute-done | bytes 1048608 | tf_op jit(solution)/shard_map/ppermute | solution.py:353
  31.8 1.2 collective-permute-done.3.refs_9_.refs_5_
  33.0 2.6 %collective-permute-start.5 = (bf16[128,4224]{1,0:T(8,128)(2,1)}, bf16[128,4224]{1,0:T(8,128)(2,1)}, u32[]{:S(2)}, u32[]{:S(2)}) collective-permute-start(bf16[128,4224]{1,0:T(8,128)(2,1)} %collective-permute-done.1.refs_3_), channel_id=1, source_target_pairs={{0,2},{1,3},{2,6},{3,7},{4,0},{5,1},{6,4},{7,5},{8,10},{9,11},{10,... | collective-permute-start | bytes 3244040 | tf_op jit(solution)/shard_map/ppermute | solution.py:356
  35.6 1.6 %collective-permute-start.6 = (bf16[512,512]{1,0:T(8,128)(2,1)S(1)}, bf16[512,512]{1,0:T(8,128)(2,1)S(1)}, u32[]{:S(2)}, u32[]{:S(2)}) collective-permute-start(bf16[512,512]{1,0:T(8,128)(2,1)S(1)} %slice.16), channel_id=1, source_target_pairs={{0,16},{8,24},{16,0},{24,8},{1,17},{9,25},{17,1},{25,9},{2,18},{10... | collective-permute-start | bytes 1572872 | tf_op jit(solution)/shard_map/ppermute | solution.py:357
  37.3 0.6 collective-permute-start.7
  37.9 0.5 collective-permute-start.4
  38.4 9.2 %collective-permute-done.6.refs_10_.refs_6_ = bf16[512,512]{1,0:T(8,128)(2,1)S(1)} collective-permute-done((bf16[512,512]{1,0:T(8,128)(2,1)S(1)}, bf16[512,512]{1,0:T(8,128)(2,1)S(1)}, u32[]{:S(2)}, u32[]{:S(2)}) %collective-permute-start.6) | collective-permute-done | bytes 524320 | tf_op jit(solution)/shard_map/ppermute | solution.py:357
  47.6 1.3 collective-permute-done.7.refs_11_.refs_7_
  48.9 9.5 %collective-permute-done.5.refs_5_ = bf16[128,4224]{1,0:T(8,128)(2,1)} collective-permute-done((bf16[128,4224]{1,0:T(8,128)(2,1)}, bf16[128,4224]{1,0:T(8,128)(2,1)}, u32[]{:S(2)}, u32[]{:S(2)}) %collective-permute-start.5) | collective-permute-done | bytes 1081376 | tf_op jit(solution)/shard_map/ppermute | solution.py:356
  58.4 0.0 collective-permute-start.8
  58.4 1.6 %collective-permute-start.9 = (bf16[128,4224]{1,0:T(8,128)(2,1)}, bf16[128,4224]{1,0:T(8,128)(2,1)S(1)}, u32[]{:S(2)}, u32[]{:S(2)}) collective-permute-start(bf16[128,4224]{1,0:T(8,128)(2,1)} %collective-permute-done.5.refs_5_), channel_id=1, source_target_pairs={{0,2},{1,3},{2,6},{3,7},{4,0},{5,1},{6,4},{7,5},{8,10},{9,11},{10,... | collective-permute-start | bytes 3244040 | tf_op jit(solution)/shard_map/ppermute | solution.py:365
  60.1 0.7 pad_add_fusion.refs_0_
  60.8 0.7 collective-permute-done.8.refs_6_
  61.5 15.5 %stage.2 = (s32[2]{0:T(128)}, bf16[512,768]{1,0:T(8,128)(2,1)}, f32[1,768]{1,0:T(1,128)}, f32[512,1024]{1,0:T(8,128)}, f32[512,1024]{1,0:T(8,128)}, /*index=5*/f32[512,1024]{1,0:T(8,128)}, f32[512,1024]{1,0:T(8,128)}) custom-call(s32[2]{0:T(128)} %pad_add_fusion.refs_0_, bf16[128,4224]{1,0:T(8,128)(2,1)} %copy-done.3, ...), custom_call_target="tpu_custom_call" | custom-call | flops 6442450944 | bytes 18874368 | tf_op jit(solution)/shard_map/stage/pallas_call | solution.py:233
  77.0 8.9 %collective-permute-done.9.refs_1_ = bf16[128,4224]{1,0:T(8,128)(2,1)S(1)} collective-permute-done((bf16[128,4224]{1,0:T(8,128)(2,1)}, bf16[128,4224]{1,0:T(8,128)(2,1)S(1)}, u32[]{:S(2)}, u32[]{:S(2)}) %collective-permute-start.9) | collective-permute-done | bytes 1081376 | tf_op jit(solution)/shard_map/ppermute | solution.py:365
  85.8 2.7 %collective-permute-done.10.refs_2_ = bf16[128,4224]{1,0:T(8,128)(2,1)S(1)} collective-permute-done((bf16[128,4224]{1,0:T(8,128)(2,1)S(1)}, bf16[128,4224]{1,0:T(8,128)(2,1)S(1)}, u32[]{:S(2)}, u32[]{:S(2)}) %collective-permute-start.10) | collective-permute-done | bytes 1081376 | tf_op jit(solution)/shard_map/ppermute | solution.py:372
  88.5 1.0 copy-done.5
  89.5 6.4 %stage.3 = (s32[2]{0:T(128)}, bf16[512,256]{1,0:T(8,128)(2,1)}, f32[1,256]{1,0:T(1,128)}, bf16[256,1024]{1,0:T(8,128)(2,1)}, bf16[256,1024]{1,0:T(8,128)(2,1)}) custom-call(s32[2]{0:T(128)} %get-tuple-element.29.refs_0_, bf16[128,4224]{1,0:T(8,128)(2,1)} %copy-done.4, bf16[128,4224]{1,0:T(8,128)(2,1)} %copy-done.5, bf16[1024,512]{1,0:T(8,128)(2,1)} %bitcast.21, ...), custom_call_target="tpu_custom_call" | custom-call | flops 1342177280 | bytes 8388608 | tf_op jit(solution)/shard_map/stage/pallas_call | solution.py:233
  96.0 0.9 collective-permute-start.12
  96.9 1.5 %collective-permute-start.15 = (bf16[256,1024]{1,0:T(8,128)(2,1)}, bf16[256,1024]{1,0:T(8,128)(2,1)S(1)}, u32[]{:S(2)}, u32[]{:S(2)}) collective-permute-start(bf16[256,1024]{1,0:T(8,128)(2,1)} %get-tuple-element.46), channel_id=1, source_target_pairs={{0,16},{8,24},{16,0},{24,8},{1,17},{9,25},{17,1},{25,9},{2,18},{10... | collective-permute-start | bytes 1572872 | tf_op jit(solution)/shard_map/ppermute | solution.py:378
  98.4 0.7 constant_dynamic-slice_fusion
  99.1 0.1 reshape_squeeze.3
  99.2 3.2 %part.5 = (s32[2]{0:T(128)}, bf16[256,1024]{1,0:T(8,128)(2,1)}) custom-call(s32[2]{0:T(128)} %get-tuple-element.32.refs_0_, bf16[128,4224]{1,0:T(8,128)(2,1)} %copy-done.4, bf16[128,4224]{1,0:T(8,128)(2,1)} %copy-done.5, bf16[512,256]{1,0:T(8,128)(2,1)} %get-tuple-element.33.refs_3_, f32[512,1024]{1,0:T(8,128)} %get-tuple-element.34.refs_4_), custom_call_target="tpu_custom_call" | custom-call | flops 134217728 | bytes 2097152 | tf_op jit(solution)/shard_map/part/pallas_call | solution.py:303
  102.5 3.2 %part.6 = (s32[2]{0:T(128)}, bf16[256,1024]{1,0:T(8,128)(2,1)}) custom-call(s32[2]{0:T(128)} %get-tuple-element.35.refs_0_, bf16[128,4224]{1,0:T(8,128)(2,1)} %copy-done.4, bf16[128,4224]{1,0:T(8,128)(2,1)} %copy-done.5, bf16[512,256]{1,0:T(8,128)(2,1)} %get-tuple-element.33.refs_3_, f32[512,1024]{1,0:T(8,128)} %get-tuple-element.36.refs_4_), custom_call_target="tpu_custom_call" | custom-call | flops 134217728 | bytes 2097152 | tf_op jit(solution)/shard_map/part/pallas_call | solution.py:303
  105.7 0.6 collective-permute-start.14
  106.3 1.1 collective-permute-start.11
  107.4 4.4 %part.7 = (s32[2]{0:T(128)}, f32[512,1024]{1,0:T(8,128)}) custom-call(s32[2]{0:T(128)} %get-tuple-element.37.refs_0_, bf16[128,4224]{1,0:T(8,128)(2,1)} %copy-done.4, bf16[128,4224]{1,0:T(8,128)(2,1)} %copy-done.5, bf16[512,256]{1,0:T(8,128)(2,1)} %get-tuple-element.33.refs_3_, f32[512,1024]{1,0:T(8,128)} %get-tuple-element.38.refs_4_), custom_call_target="tpu_custom_call" | custom-call | flops 268435456 | bytes 3670016 | tf_op jit(solution)/shard_map/part/pallas_call | solution.py:303
  111.8 0.8 copy-done.14
  112.6 3.4 %part.8 = (s32[2]{0:T(128)}, bf16[256,1024]{1,0:T(8,128)(2,1)}) custom-call(s32[2]{0:T(128)} %get-tuple-element.41.refs_0_, bf16[128,4224]{1,0:T(8,128)(2,1)} %copy-done.4, bf16[128,4224]{1,0:T(8,128)(2,1)} %copy-done.5, bf16[512,256]{1,0:T(8,128)(2,1)} %get-tuple-element.33.refs_3_, f32[512,1024]{1,0:T(8,128)} %get-tuple-element.36.refs_4_, ...), custom_call_target="tpu_custom_call" | custom-call | flops 134217728 | bytes 2097152 | tf_op jit(solution)/shard_map/part/pallas_call | solution.py:303
  116.0 0.8 copy-done.13
  116.8 3.5 %part.9 = (s32[2]{0:T(128)}, bf16[256,1024]{1,0:T(8,128)(2,1)}) custom-call(s32[2]{0:T(128)} %get-tuple-element.45.refs_0_, bf16[128,4224]{1,0:T(8,128)(2,1)} %copy-done.4, bf16[128,4224]{1,0:T(8,128)(2,1)} %copy-done.5, bf16[512,256]{1,0:T(8,128)(2,1)} %get-tuple-element.33.refs_3_, f32[512,1024]{1,0:T(8,128)} %get-tuple-element.34.refs_4_, ...), custom_call_target="tpu_custom_call" | custom-call | flops 134217728 | bytes 2097152 | tf_op jit(solution)/shard_map/part/pallas_call | solution.py:303
  120.4 0.9 collective-permute-start.16
  121.3 1.5 %collective-permute-start.13 = (bf16[256,1024]{1,0:T(8,128)(2,1)}, bf16[256,1024]{1,0:T(8,128)(2,1)}, u32[]{:S(2)}, u32[]{:S(2)}) collective-permute-start(bf16[256,1024]{1,0:T(8,128)(2,1)} %get-tuple-element.43), channel_id=1, source_target_pairs={{0,16},{8,24},{16,0},{24,8},{1,17},{9,25},{17,1},{25,9},{2,18},{10... | collective-permute-start | bytes 1572872 | tf_op jit(solution)/shard_map/ppermute | solution.py:397
  122.9 0.6 scatter_custom_fusion
  123.5 10.2 %all_to_all.9 = f32[8,1,128]{2,1,0:T(1,128)S(1)} all-to-all(f32[8,1,128]{2,1,0:T(1,128)S(1)} %bitcast.23), channel_id=1, replica_groups=mesh['dp'=4,'label'=8] {'label'}, dimensions={0} | all-to-all | bytes 8192 | tf_op jit(solution)/shard_map/all_to_all | solution.py:403
  133.7 0.5 broadcast_multiply_fusion
  134.3 1.7 %fusion = (bf16[1,256,1024]{2,1,0:T(8,128)(2,1)S(1)}, bf16[1,256,1024]{2,1,0:T(8,128)(2,1)S(1)}) fusion(bf16[256,1024]{1,0:T(8,128)(2,1)} %collective-permute-done.13, bf16[256,1024]{1,0:T(8,128)(2,1)S(1)} %collective-permute-done.11, f32[512,1024]{1,0:T(8,128)S(1)} %copy-done.9, bf16[256,1024]{1,0:T(8,128)(2,1)} %collective-permute-done.16, ...), kind=kLoop, calls=%fused_computation.4 | loop fusion | flops 2621440 | bytes 5242880 | tf_op jit(solution)/shard_map/stack | solution.py:408
  136.0 0.1 maximum_bitcast_fusion
  136.1 2.0 %copy.9 = bf16[1024,2,256]{2,1,0:T(2,128)(2,1)} copy(bf16[1024,2,256]{0,2,1:T(8,128)(2,1)S(1)} %maximum_bitcast_fusion) | data formatting | bytes 2097152
  (43 shorter events, 0.2 us)
Async XLA Ops:
  0.6 1.2 copy-start
  1.9 0.7 copy-start.1
  2.5 0.7 copy-start.2
  3.2 3.6 %copy-start.10 = (bf16[1024,2,256]{2,1,0:T(2,128)(2,1)S(1)}, bf16[1024,2,256]{2,1,0:T(2,128)(2,1)}, u32[]{:S(2)}) copy-start(bf16[1024,2,256]{2,1,0:T(2,128)(2,1)} %param.6) | copy-start | bytes 3145732
  3.8 34.1 %copy-start.3 = (bf16[128,4224]{1,0:T(8,128)(2,1)}, bf16[128,4224]{1,0:T(8,128)(2,1)S(1)}, u32[]{:S(2)}) copy-start(bf16[128,4224]{1,0:T(8,128)(2,1)S(1)} %get-tuple-element.26.refs_1_) | copy-start | bytes 3244036
  3.8 29.2 %collective-permute-start.1 = (bf16[128,4224]{1,0:T(8,128)(2,1)S(1)}, bf16[128,4224]{1,0:T(8,128)(2,1)}, u32[]{:S(2)}, u32[]{:S(2)}) collective-permute-start(bf16[128,4224]{1,0:T(8,128)(2,1)S(1)} %get-tuple-element.26.refs_1_), channel_id=1, source_target_pairs={{0,2},{1,3},{2,6},{3,7},{4,0},{5,1},{6,4},{7,5},{8,10},{9,11},{10,... | collective-permute-start | bytes 3244040 | tf_op jit(solution)/shard_map/ppermute | solution.py:352
  7.1 54.4 %copy-start.6 = (bf16[128,8,2,256]{3,1,2,0:T(8,128)(2,1)}, bf16[128,8,2,256]{3,1,2,0:T(8,128)(2,1)S(1)}, u32[]{:S(2)}) copy-start(bf16[128,8,2,256]{3,1,2,0:T(8,128)(2,1)S(1)} %copy.10) | copy-start | bytes 3145732
  7.1 24.7 %collective-permute-start.2 = (bf16[1024,512]{1,0:T(8,128)(2,1)S(1)}, bf16[1024,512]{1,0:T(8,128)(2,1)S(1)}, u32[]{:S(2)}, u32[]{:S(2)}) collective-permute-start(bf16[1024,512]{1,0:T(8,128)(2,1)S(1)} %bitcast.18), channel_id=1, source_target_pairs={{0,8},{8,0},{16,24},{24,16},{1,9},{9,1},{17,25},{25,17},{2,10},{10... | collective-permute-start | bytes 3145736 | tf_op jit(solution)/shard_map/ppermute | solution.py:353
  8.7 24.3 %collective-permute-start.3 = (bf16[1024,512]{1,0:T(8,128)(2,1)S(1)}, bf16[1024,512]{1,0:T(8,128)(2,1)S(1)}, u32[]{:S(2)}, u32[]{:S(2)}) collective-permute-start(bf16[1024,512]{1,0:T(8,128)(2,1)S(1)} %bitcast.19), channel_id=1, source_target_pairs={{0,16},{8,24},{16,0},{24,8},{1,17},{9,25},{17,1},{25,9},{2,18},{10... | collective-permute-start | bytes 3145736 | tf_op jit(solution)/shard_map/ppermute | solution.py:354
  31.8 26.7 %copy-start.7 = (bf16[1024,512]{1,0:T(8,128)(2,1)}, bf16[1024,512]{1,0:T(8,128)(2,1)S(1)}, u32[]{:S(2)}) copy-start(bf16[1024,512]{1,0:T(8,128)(2,1)S(1)} %collective-permute-done.2.refs_8_.refs_4_) | copy-start | bytes 3145732
  33.0 25.4 %copy-start.8 = (bf16[1024,512]{1,0:T(8,128)(2,1)}, bf16[1024,512]{1,0:T(8,128)(2,1)S(1)}, u32[]{:S(2)}) copy-start(bf16[1024,512]{1,0:T(8,128)(2,1)S(1)} %collective-permute-done.3.refs_9_.refs_5_) | copy-start | bytes 3145732
  33.0 25.4 %collective-permute-start.5 = (bf16[128,4224]{1,0:T(8,128)(2,1)}, bf16[128,4224]{1,0:T(8,128)(2,1)}, u32[]{:S(2)}, u32[]{:S(2)}) collective-permute-start(bf16[128,4224]{1,0:T(8,128)(2,1)} %collective-permute-done.1.refs_3_), channel_id=1, source_target_pairs={{0,2},{1,3},{2,6},{3,7},{4,0},{5,1},{6,4},{7,5},{8,10},{9,11},{10,... | collective-permute-start | bytes 3244040 | tf_op jit(solution)/shard_map/ppermute | solution.py:356
  35.6 12.0 %collective-permute-start.6 = (bf16[512,512]{1,0:T(8,128)(2,1)S(1)}, bf16[512,512]{1,0:T(8,128)(2,1)S(1)}, u32[]{:S(2)}, u32[]{:S(2)}) collective-permute-start(bf16[512,512]{1,0:T(8,128)(2,1)S(1)} %slice.16), channel_id=1, source_target_pairs={{0,16},{8,24},{16,0},{24,8},{1,17},{9,25},{17,1},{25,9},{2,18},{10... | collective-permute-start | bytes 1572872 | tf_op jit(solution)/shard_map/ppermute | solution.py:357
  37.3 11.7 %collective-permute-start.7 = (bf16[512,512]{1,0:T(8,128)(2,1)S(1)}, bf16[512,512]{1,0:T(8,128)(2,1)S(1)}, u32[]{:S(2)}, u32[]{:S(2)}) collective-permute-start(bf16[512,512]{1,0:T(8,128)(2,1)S(1)} %slice.17), channel_id=1, source_target_pairs={{0,8},{8,0},{16,24},{24,16},{1,9},{9,1},{17,25},{25,17},{2,10},{10... | collective-permute-start | bytes 1572872 | tf_op jit(solution)/shard_map/ppermute | solution.py:358
  37.9 22.9 %collective-permute-start = (bf16[128,4224]{1,0:T(8,128)(2,1)S(1)}, bf16[128,4224]{1,0:T(8,128)(2,1)}, u32[]{:S(2)}, u32[]{:S(2)}) collective-permute-start(bf16[128,4224]{1,0:T(8,128)(2,1)S(1)} %get-tuple-element.26.refs_1_), channel_id=1, source_target_pairs={{0,1},{1,0},{2,3},{3,2},{4,5},{5,4},{6,7},{7,6},{8,9},{9,8},{10,11... | collective-permute-start | bytes 3244040 | tf_op jit(solution)/shard_map/ppermute | solution.py:362
  37.9 22.9 %collective-permute-start.4 = (bf16[128,4224]{1,0:T(8,128)(2,1)}, bf16[128,4224]{1,0:T(8,128)(2,1)}, u32[]{:S(2)}, u32[]{:S(2)}) collective-permute-start(bf16[128,4224]{1,0:T(8,128)(2,1)} %collective-permute-done.1.refs_3_), channel_id=1, source_target_pairs={{0,1},{1,0},{2,3},{3,2},{4,5},{5,4},{6,7},{7,6},{8,9},{9,8},{10,11... | collective-permute-start | bytes 3244040 | tf_op jit(solution)/shard_map/ppermute | solution.py:362
  47.6 12.5 %copy-start.11 = (bf16[512,512]{1,0:T(8,128)(2,1)}, bf16[512,512]{1,0:T(8,128)(2,1)S(1)}, u32[]{:S(2)}) copy-start(bf16[512,512]{1,0:T(8,128)(2,1)S(1)} %collective-permute-done.6.refs_10_.refs_6_) | copy-start | bytes 1572868
  48.9 11.2 %copy-start.12 = (bf16[512,512]{1,0:T(8,128)(2,1)}, bf16[512,512]{1,0:T(8,128)(2,1)S(1)}, u32[]{:S(2)}) copy-start(bf16[512,512]{1,0:T(8,128)(2,1)S(1)} %collective-permute-done.7.refs_11_.refs_7_) | copy-start | bytes 1572868
  58.4 3.0 %collective-permute-start.8 = (bf16[128,4224]{1,0:T(8,128)(2,1)}, bf16[128,4224]{1,0:T(8,128)(2,1)}, u32[]{:S(2)}, u32[]{:S(2)}) collective-permute-start(bf16[128,4224]{1,0:T(8,128)(2,1)} %collective-permute-done.5.refs_5_), channel_id=1, source_target_pairs={{0,1},{1,0},{2,3},{3,2},{4,5},{5,4},{6,7},{7,6},{8,9},{9,8},{10,11... | collective-permute-start | bytes 3244040 | tf_op jit(solution)/shard_map/ppermute | solution.py:362
  58.4 27.4 %collective-permute-start.9 = (bf16[128,4224]{1,0:T(8,128)(2,1)}, bf16[128,4224]{1,0:T(8,128)(2,1)S(1)}, u32[]{:S(2)}, u32[]{:S(2)}) collective-permute-start(bf16[128,4224]{1,0:T(8,128)(2,1)} %collective-permute-done.5.refs_5_), channel_id=1, source_target_pairs={{0,2},{1,3},{2,6},{3,7},{4,0},{5,1},{6,4},{7,5},{8,10},{9,11},{10,... | collective-permute-start | bytes 3244040 | tf_op jit(solution)/shard_map/ppermute | solution.py:365
  85.8 2.7 %copy-start.4 = (bf16[128,4224]{1,0:T(8,128)(2,1)}, bf16[128,4224]{1,0:T(8,128)(2,1)S(1)}, u32[]{:S(2)}) copy-start(bf16[128,4224]{1,0:T(8,128)(2,1)S(1)} %collective-permute-done.9.refs_1_) | copy-start | bytes 3244036
  85.8 2.7 %collective-permute-start.10 = (bf16[128,4224]{1,0:T(8,128)(2,1)S(1)}, bf16[128,4224]{1,0:T(8,128)(2,1)S(1)}, u32[]{:S(2)}, u32[]{:S(2)}) collective-permute-start(bf16[128,4224]{1,0:T(8,128)(2,1)S(1)} %collective-permute-done.9.refs_1_), channel_id=1, source_target_pairs={{0,1},{1,0},{2,3},{3,2},{4,5},{5,4},{6,7},{7,6},{8,9},{9,8},{10,11... | collective-permute-start | bytes 3244040 | tf_op jit(solution)/shard_map/ppermute | solution.py:372
  88.5 1.0 copy-start.5
  96.0 15.9 %collective-permute-start.12 = (bf16[256,1024]{1,0:T(8,128)(2,1)}, bf16[256,1024]{1,0:T(8,128)(2,1)S(1)}, u32[]{:S(2)}, u32[]{:S(2)}) collective-permute-start(bf16[256,1024]{1,0:T(8,128)(2,1)} %get-tuple-element.42), channel_id=1, source_target_pairs={{0,8},{8,0},{16,24},{24,16},{1,9},{9,1},{17,25},{25,17},{2,10},{10... | collective-permute-start | bytes 1572872 | tf_op jit(solution)/shard_map/ppermute | solution.py:377
  96.9 19.1 %collective-permute-start.15 = (bf16[256,1024]{1,0:T(8,128)(2,1)}, bf16[256,1024]{1,0:T(8,128)(2,1)S(1)}, u32[]{:S(2)}, u32[]{:S(2)}) collective-permute-start(bf16[256,1024]{1,0:T(8,128)(2,1)} %get-tuple-element.46), channel_id=1, source_target_pairs={{0,16},{8,24},{16,0},{24,8},{1,17},{9,25},{17,1},{25,9},{2,18},{10... | collective-permute-start | bytes 1572872 | tf_op jit(solution)/shard_map/ppermute | solution.py:378
  105.7 28.5 %collective-permute-start.14 = (bf16[256,1024]{1,0:T(8,128)(2,1)}, bf16[256,1024]{1,0:T(8,128)(2,1)S(1)}, u32[]{:S(2)}, u32[]{:S(2)}) collective-permute-start(bf16[256,1024]{1,0:T(8,128)(2,1)} %get-tuple-element.44), channel_id=1, source_target_pairs={{0,16},{8,24},{16,0},{24,8},{1,17},{9,25},{17,1},{25,9},{2,18},{10... | collective-permute-start | bytes 1572872 | tf_op jit(solution)/shard_map/ppermute | solution.py:394
  106.3 28.0 %collective-permute-start.11 = (bf16[256,1024]{1,0:T(8,128)(2,1)}, bf16[256,1024]{1,0:T(8,128)(2,1)S(1)}, u32[]{:S(2)}, u32[]{:S(2)}) collective-permute-start(bf16[256,1024]{1,0:T(8,128)(2,1)} %get-tuple-element.40), channel_id=1, source_target_pairs={{0,8},{8,0},{16,24},{24,16},{1,9},{9,1},{17,25},{25,17},{2,10},{10... | collective-permute-start | bytes 1572872 | tf_op jit(solution)/shard_map/ppermute | solution.py:392
  111.8 0.8 copy-start.14
  116.0 0.8 copy-start.13
  116.8 6.0 %copy-start.15 = (f32[1,768]{1,0:T(1,128)S(1)}, f32[1,768]{1,0:T(1,128)}, u32[]{:S(2)}) copy-start(f32[1,768]{1,0:T(1,128)} %get-tuple-element.48) | copy-start | bytes 9220
  116.8 6.0 %copy-start.16 = (f32[1,256]{1,0:T(1,128)S(1)}, f32[1,256]{1,0:T(1,128)}, u32[]{:S(2)}) copy-start(f32[1,256]{1,0:T(1,128)} %get-tuple-element.49) | copy-start | bytes 3076
  116.8 17.4 %copy-start.9 = (f32[512,1024]{1,0:T(8,128)S(1)}, f32[512,1024]{1,0:T(8,128)}, u32[]{:S(2)}) copy-start(f32[512,1024]{1,0:T(8,128)} %get-tuple-element.39) | copy-start | bytes 6291460
  120.4 13.9 %collective-permute-start.16 = (bf16[256,1024]{1,0:T(8,128)(2,1)}, bf16[256,1024]{1,0:T(8,128)(2,1)}, u32[]{:S(2)}, u32[]{:S(2)}) collective-permute-start(bf16[256,1024]{1,0:T(8,128)(2,1)} %get-tuple-element.47), channel_id=1, source_target_pairs={{0,8},{8,0},{16,24},{24,16},{1,9},{9,1},{17,25},{25,17},{2,10},{10... | collective-permute-start | bytes 1572872 | tf_op jit(solution)/shard_map/ppermute | solution.py:399
  121.3 12.9 %collective-permute-start.13 = (bf16[256,1024]{1,0:T(8,128)(2,1)}, bf16[256,1024]{1,0:T(8,128)(2,1)}, u32[]{:S(2)}, u32[]{:S(2)}) collective-permute-start(bf16[256,1024]{1,0:T(8,128)(2,1)} %get-tuple-element.43), channel_id=1, source_target_pairs={{0,16},{8,24},{16,0},{24,8},{1,17},{9,25},{17,1},{25,9},{2,18},{10... | collective-permute-start | bytes 1572872 | tf_op jit(solution)/shard_map/ppermute | solution.py:397

commit v3 on v2

--- a/solution.py
+++ b/solution.py
@@ -12,7 +12,8 @@
 
 ring_next = (1, 3, 0, 2)
 ring_prev = (2, 0, 3, 1)
-kernel_vmem = 58 << 20
+halves = 2
+kernel_vmem = 32 << 20
 lanes = 128
 
 
@@ -82,8 +83,9 @@
     return (weight_grad, sample_loss)
 
 
-def pack_kernel(parts, samples_ref, matches_ref, positives_ref, next_ref, *outs):
-    next_ref[0] = 0
+def pack_kernel(parts, where_ref, samples_ref, matches_ref, positives_ref, next_ref, *outs):
+    next_ref[0] = where_ref[0]
+    next_ref[1] = where_ref[1]
     rows, feat_width = samples_ref.shape
     part = rows // parts
     cluster = lax.broadcasted_iota(jnp.int32, (lanes, rows), 0)
@@ -98,18 +100,17 @@
         out[:, feat_width:] = code[span]
 
 
-def pack_call(samples, matches, positives, parts):
+def pack_call(where, samples, matches, positives, parts):
     rows, feat_width = samples.shape
-    whole = pl.BlockSpec(memory_space=pltpu.VMEM)
     block = jax.ShapeDtypeStruct((rows // parts, feat_width + lanes), jnp.bfloat16)
     return pl.pallas_call(
         functools.partial(pack_kernel, parts),
-        out_shape=(jax.ShapeDtypeStruct((1,), jnp.int32),) + (block,) * parts,
-        in_specs=[whole, whole, whole],
-        out_specs=(pl.BlockSpec(memory_space=pltpu.SMEM),) + (whole,) * parts,
+        out_shape=(jax.ShapeDtypeStruct((2,), jnp.int32),) + (block,) * parts,
+        in_specs=[scalar, whole, whole, whole],
+        out_specs=(scalar,) + (whole,) * parts,
         compiler_params=pltpu.CompilerParams(vmem_limit_bytes=8 << 20),
         name="pack",
-    )(samples, matches.T, positives.T)
+    )(where, samples, matches.T, positives.T)
 
 
 def load(sources, targets, sems):
@@ -216,11 +217,12 @@
 scalar = pl.BlockSpec(memory_space=pltpu.SMEM)
 
 
-def stage_call(where, groups, ws, places, local_count, offsets, sums=()):
+def stage_call(where, groups, ws, places, local_count, offsets):
     xs = [x for group in groups for x in group]
     rows = sum(x.shape[0] for x in xs)
     feat_width = xs[0].shape[1] - lanes
     depth, columns = ws[0].shape
+    sums = ()
     inputs = [*xs, *ws, *sums]
     scratch = [pltpu.VMEM(array.shape, array.dtype) for array in inputs]
     scratch.append(pltpu.SemaphoreType.DMA((len(inputs),)))
@@ -259,74 +261,130 @@
     )(where, *inputs)
 
 
-def part_kernel(offset, lows, blocks, parts, gots, *refs):
-    where_ref, refs = refs[0], refs[1:]
-    xs_in, gs_in, refs = refs[:blocks], refs[blocks : blocks + parts], refs[blocks + parts :]
-    sums_in, gots_in, refs = refs[0], refs[1 : 1 + gots], refs[1 + gots :]
-    next_ref, out_ref, held, gs, sums = refs[:5]
-    got, sems = refs[5], refs[-1]
-    next_ref[0] = where_ref[0]
-    next_ref[1] = where_ref[1]
-    width, depth = out_ref.shape
-    begin = pl.multiple_of((where_ref[0] ^ offset) * depth, depth)
-    sources = [x.at[:, pl.ds(begin, depth)] for x in xs_in]
-    targets, at = [], 0
-    for x in xs_in:
-        targets.append(held.at[pl.ds(at, x.shape[0])])
-        at += x.shape[0]
-    at = 0
-    for g in gs_in:
-        sources.append(g.at[pl.ds(lows, width)])
-        targets.append(gs.at[:, pl.ds(at, g.shape[1])])
-        at += g.shape[1]
-    sources.append(sums_in.at[pl.ds(lows, width)])
-    targets.append(sums)
-    if gots_in:
-        sources.append(gots_in[0])
-        targets.append(got)
-    for copy in load(sources, targets, sems):
-        copy.wait()
+def grad_tiles(me, offset, xs, grads, sums, depth):
     tile = 256
     for step in range(depth // tile):
+        start = pl.multiple_of((me ^ offset) * depth + step * tile, tile)
         span = slice(step * tile, (step + 1) * tile)
-        total = jnp.dot(gs[...], held[:, span], preferred_element_type=jnp.float32)
-        total = total + sums[:, span]
-        if gots_in:
-            total = total + got[:, span].astype(jnp.float32)
-        out_ref[:, span] = total.astype(out_ref.dtype)
-
-
-def part_call(where, offset, lows, width, kind, xs, gs, sums, got=()):
+        rows = jnp.concatenate([x[:, pl.ds(start, tile)] for x in xs], axis=0)
+        total = jnp.dot(grads, rows, preferred_element_type=jnp.float32)
+        yield span, total + sums[:, span]
+
+
+def last_kernel(blocks, places, depth, local_count, offset, where_ref, *refs):
+    xs, ws, refs = refs[:blocks], refs[blocks : blocks + len(places)], refs[blocks + len(places) :]
+    sums, next_ref, grad_ref, loss_ref, *outs = refs
+    me, label = where_ref[0], where_ref[1]
+    next_ref[0] = me
+    next_ref[1] = label
+    scores = row_scores(me, xs, ws, [None] * len(ws), places, depth)
+    row_terms(scores, xs, label, local_count, grad_ref, loss_ref, 0)
+    for span, total in grad_tiles(me, offset, xs, grad_ref[...], sums, depth):
+        width = total.shape[0] // local_count
+        for cluster, out in enumerate(outs):
+            out[:, span] = total[cluster * width : (cluster + 1) * width].astype(out.dtype)
+
+
+def last_call(where, xs, ws, places, local_count, offset, sums):
     rows = sum(x.shape[0] for x in xs)
-    depth = sums.shape[1]
-    count = len(xs) + len(gs) + 1 + len(got)
+    feat_width = xs[0].shape[1] - lanes
+    depth, columns = ws[0].shape
     return pl.pallas_call(
-        functools.partial(part_kernel, offset, lows, len(xs), len(gs), len(got)),
+        functools.partial(last_kernel, len(xs), places, depth, local_count, offset),
         out_shape=(
             jax.ShapeDtypeStruct((2,), jnp.int32),
-            jax.ShapeDtypeStruct((width, depth), kind),
-        ),
-        in_specs=[scalar] + [any_space] * count,
-        out_specs=(scalar, whole),
+            jax.ShapeDtypeStruct((columns, rows), jnp.bfloat16),
+            jax.ShapeDtypeStruct((1, rows), jnp.float32),
+        )
+        + (jax.ShapeDtypeStruct((columns // local_count, depth), jnp.bfloat16),) * local_count,
+        in_specs=[scalar] + [whole] * (len(xs) + len(ws) + 1),
+        out_specs=(scalar,) + (whole,) * (2 + local_count),
+        compiler_params=pltpu.CompilerParams(vmem_limit_bytes=16 << 20),
+        cost_estimate=pl.CostEstimate(
+            flops=2 * rows * columns * (feat_width + depth),
+            bytes_accessed=2 * (rows + columns) * feat_width + 6 * columns * depth,
+            transcendentals=2 * rows * columns,
+        ),
+        name="last",
+    )(where, *xs, *ws, sums)
+
+
+def near_kernel(blocks, where_ref, *refs):
+    ins, (grads, next_ref, near_x, near_y, on_x, on_y, own) = refs[: blocks + 3], refs[
+        blocks + 3 : blocks + 10
+    ]
+    held, sems = refs[blocks + 10 : -1], refs[-1]
+    me = where_ref[0]
+    next_ref[0] = me
+    next_ref[1] = where_ref[1]
+    copies = load(ins, held, sems)
+    xs, sums = held[:blocks], held[blocks:]
+    for copy in copies[: blocks + 1]:
+        copy.wait()
+    grads = grads[...]
+    width, depth = near_x.shape
+    for span, total in grad_tiles(me, 1, xs, grads, sums[0], depth):
+        near_x[:, span] = total[:width].astype(near_x.dtype)
+        on_x[:, span] = total[width:]
+    copies[blocks + 1].wait()
+    for span, total in grad_tiles(me, 2, xs, grads, sums[1], depth):
+        on_y[:, span] = total[:width]
+        near_y[:, span] = total[width:].astype(near_y.dtype)
+    copies[blocks + 2].wait()
+    for span, total in grad_tiles(me, 0, xs, grads, sums[2], depth):
+        own[:, span] = total
+
+
+def near_call(where, xs, grads, sums):
+    columns, depth = sums[0].shape
+    rows = grads.shape[1]
+    half = (columns // 2, depth)
+    inputs = (*xs, sums[1], sums[2], sums[0])
+    return pl.pallas_call(
+        functools.partial(near_kernel, len(xs)),
+        out_shape=(
+            jax.ShapeDtypeStruct((2,), jnp.int32),
+            jax.ShapeDtypeStruct(half, jnp.bfloat16),
+            jax.ShapeDtypeStruct(half, jnp.bfloat16),
+            jax.ShapeDtypeStruct(half, jnp.float32),
+            jax.ShapeDtypeStruct(half, jnp.float32),
+            jax.ShapeDtypeStruct((columns, depth), jnp.float32),
+        ),
+        in_specs=[scalar] + [any_space] * len(inputs) + [whole],
+        out_specs=(scalar,) + (whole,) * 5,
         scratch_shapes=[
-            pltpu.VMEM((rows, depth), jnp.bfloat16),
-            pltpu.VMEM((width, rows), jnp.bfloat16),
-            pltpu.VMEM((width, depth), jnp.float32),
-            *(pltpu.VMEM((width, depth), jnp.bfloat16) for _ in got),
-            pltpu.SemaphoreType.DMA((count,)),
+            *(pltpu.VMEM(array.shape, array.dtype) for array in inputs),
+            pltpu.SemaphoreType.DMA((len(inputs),)),
         ],
-        compiler_params=pltpu.CompilerParams(vmem_limit_bytes=kernel_vmem),
+        compiler_params=pltpu.CompilerParams(vmem_limit_bytes=58 << 20),
         cost_estimate=pl.CostEstimate(
-            flops=2 * rows * depth * width,
-            bytes_accessed=2 * rows * depth + 6 * depth * width,
+            flops=6 * rows * columns * depth,
+            bytes_accessed=22 * columns * depth,
             transcendentals=0,
         ),
-        name="part",
-    )(where, *xs, *gs, sums, *got)
-
-
-def after(value, *earlier):
-    return lax.optimization_barrier((value, earlier))[0]
+        name="near",
+    )(where, *inputs, grads)
+
+
+def join_kernel(on_x, far_y, on_y, far_x, out_x, out_y):
+    out_x[...] = (on_x[...] + far_y[...].astype(jnp.float32)).astype(out_x.dtype)
+    out_y[...] = (on_y[...] + far_x[...].astype(jnp.float32)).astype(out_y.dtype)
+
+
+def join_call(on_x, far_y, on_y, far_x):
+    part = jax.ShapeDtypeStruct(far_x.shape, far_x.dtype)
+    return pl.pallas_call(
+        join_kernel,
+        out_shape=(part, part),
+        in_specs=[whole] * 4,
+        out_specs=(whole, whole),
+        compiler_params=pltpu.CompilerParams(vmem_limit_bytes=16 << 20),
+        name="join",
+    )(on_x, far_y, on_y, far_x)
+
+
+def tie(*values):
+    return lax.optimization_barrier(values)
 
 
 def ring_body(samples, weight, matches, positives):
@@ -345,59 +403,61 @@
     along_x = [(i, i ^ 1) for i in range(4)]
     along_y = [(i, i ^ 2) for i in range(4)]
 
-    packed, block = pack_call(samples, matches, positives, 1)
-    flat = after(weight.reshape(depth, local_count * label_count), packed)
+    where, *blocks = pack_call(where, samples, matches, positives, halves)
+    flat, where = tie(weight.reshape(depth, local_count * label_count), where)
     half = depth // 2
-    mine = [block]
-    mine.append(lax.ppermute(block, "label", hop))
+
+    def hops(blocks):
+        return [lax.ppermute(block, "label", hop) for block in blocks]
+
+    mine = [blocks, hops(blocks)]
     w_x = lax.ppermute(flat, "dp", along_x)
     w_y = lax.ppermute(flat, "dp", along_y)
-    mine[1] = after(mine[1], w_x, w_y)
-    mine.append(lax.ppermute(mine[1], "label", hop))
+    mine[1][-1], w_x, w_y = tie(mine[1][-1], w_x, w_y)
+    mine.append(hops(mine[1]))
     far_x = lax.ppermute(w_x[:half], "dp", along_y)
     far_y = lax.ppermute(w_y[half:], "dp", along_x)
-    mine[2] = after(mine[2], far_x, far_y)
+    mine[2][-1], far_x, far_y = tie(mine[2][-1], far_x, far_y)
+    last = hops(mine[2])
     ws = [flat, w_x, w_y, far_x, far_y]
     places = ((0, 0), (1, 0), (2, 0), (3, 0), (3, half))
-    early = [[block, lax.ppermute(block, "label", swap)] for block in mine]
+
+    def with_mates(blocks):
+        return blocks + [lax.ppermute(block, "label", swap) for block in blocks]
+
+    early = [with_mates(blocks) for blocks in mine]
 
     offsets = (3, 1, 2, 0)
-    last = lax.ppermute(mine[-1], "label", hop)
     token, _, loss, *sums = stage_call(where, early, ws, places, local_count, offsets)
-    last = after(last, token)
+    token, *last = tie(token, *last)
     losses = [loss]
     sums = dict(zip(offsets, sums))
 
-    low, full = jnp.bfloat16, jnp.float32
-    xs = [last, lax.ppermute(last, "label", swap)]
-    token, grads, loss, far_0, far_1 = stage_call(
-        token, [xs], ws, places, local_count, (3,), (sums[3],)
-    )
+    xs = with_mates(last)
+    token, grads, loss, far_0, far_1 = last_call(token, xs, ws, places, local_count, 3, sums[3])
     losses.append(loss)
     far_x = lax.ppermute(far_0, "dp", along_x)
     far_y = lax.ppermute(far_1, "dp", along_y)
-    gs = [grads]
+    token, near_x, near_y, on_x, on_y, own = near_call(token, xs, grads, sums)
+    got_x = lax.ppermute(near_x, "dp", along_x)
+    got_y = lax.ppermute(near_y, "dp", along_y)
+    on_x, on_y = join_call(on_x, far_y, on_y, far_x)
+    width = label_count
+
     order = []
     for z in range(chips):
         for c in range(2):
-            at, rows = z, []
+            at, steps = z, []
             for _ in range(chips):
-                rows.append([at * 2 + c, at * 2 + 1 - c])
+                steps.append([at * 2 + c, at * 2 + 1 - c])
                 at = ring_prev[at]
-            order.append(rows)
+            order.append(steps)
     order = jnp.array(order, jnp.int32)[label]
-
-    width = label_count
-    token, near_x = part_call(token, 1, 0, width, low, xs, gs, sums[1])
-    got_x = lax.ppermute(near_x, "dp", along_x)
-    token, near_y = part_call(token, 2, width, width, low, xs, gs, sums[2])
-    got_y = lax.ppermute(near_y, "dp", along_y)
-    token, own = part_call(token, 0, 0, 2 * width, full, xs, gs, sums[0])
-    token, on_y = part_call(token, 2, 0, width, low, xs, gs, sums[2], (far_x,))
+    by_step, on_x, on_y = tie(
+        jnp.concatenate(losses, axis=1).reshape(groups, row_count), on_x, on_y
+    )
+    pass_x = lax.ppermute(on_x, "dp", along_x)
     pass_y = lax.ppermute(on_y, "dp", along_y)
-    token, on_x = part_call(token, 1, width, width, low, xs, gs, sums[1], (far_y,))
-    pass_x = lax.ppermute(on_x, "dp", along_x)
-    by_step = after(jnp.concatenate(losses, axis=1).reshape(groups, row_count), token)
     total = jnp.zeros((groups, row_count), jnp.float32)
     total = total.at[order.reshape(-1)].set(by_step)
     returned = lax.all_to_all(total, "label", split_axis=0, concat_axis=0, tiled=True)

time: 139 us -> 132 us (0.950)
  Pallas kernels: 40.2 us -> 24 us
  waiting for transfers between devices: 55.2 us -> 62.5 us
  starting transfers between devices: 19.7 us -> 23.1 us
    ppermute x7 -> x14, waiting for transfers between devices: 21.8 us -> 49.8 us  [the longest x6 47.6 us: hops(): return [lax.ppermute(block, 'label', hop) for block in blocks]]
    ppermute x1, waiting for transfers between devices: 21.6 us -> 0.01 us  [ring_body(): w_x = lax.ppermute(flat, 'dp', along_x)]
    pallas_call x2 -> x1, Pallas kernels: 21.9 us -> 12.9 us  [stage_call(): pl.pallas_call(functools.partial(stage_kernel, tuple((len(group) for grou...]
    pallas_call x5 -> x3, Pallas kernels: 17.8 us -> 10 us  [the longest x1 6.99 us: near_call(): pl.pallas_call(functools.partial(near_kernel, len(xs)), out_shape=(jax.Sh...]
    ppermute x1, waiting for transfers between devices: 9.23 us -> 3.65 us  [ring_body(): far_x = lax.ppermute(w_x[:half], 'dp', along_y)]
    ppermute x1, waiting for transfers between devices: 0.01 us -> 4.08 us  [ring_body(): pass_y = lax.ppermute(on_y, 'dp', along_y)]
    ppermute x1, waiting for transfers between devices: 0.01 us -> 3.64 us  [ring_body(): far_y = lax.ppermute(far_1, 'dp', along_y)]
    ppermute x7 -> x14, starting transfers between devices: 7.82 us -> 11.1 us  [the longest x6 9.9 us: hops(): return [lax.ppermute(block, 'label', hop) for block in blocks]]
  transfers between devices with their start and end apart: 17 -> 24, of which waited for: 8 -> 13; matrix products, arithmetic and copies ran while one was open for 2% -> 2% of each run, Pallas kernels for 24% -> 15%
where the time goes in v3:
time: 132 us
  waiting for transfers between devices  62.5 us (47%)
  Pallas kernels  24 us (18%)
  starting transfers between devices  23.1 us (18%)
  blocking collectives  10.2 us (8%)
  local copies, waits for them, and re-layouts  8.2 us (6%)
  other arithmetic  2.83 us (2%)
    ppermute x6, waiting for transfers between devices, hops(): return [lax.ppermute(block, 'label', hop) for block in blocks]  47.6 us
    pallas_call x1, Pallas kernels, stage_call(): pl.pallas_call(functools.partial(stage_kernel, tuple((len(group) for grou...  12.9 us
    all_to_all x1, blocking collectives, ring_body(): lax.all_to_all(total, 'label', split_axis=0, concat_axis=0, tiled=True)  10.2 us
    ppermute x6, starting transfers between devices, hops(): return [lax.ppermute(block, 'label', hop) for block in blocks]  9.9 us
    pallas_call x1, Pallas kernels, near_call(): pl.pallas_call(functools.partial(near_kernel, len(xs)), out_shape=(jax.Sh...  6.99 us
    unnamed x30, local copies, waits for them, and re-layouts  6.76 us
    ppermute x1, waiting for transfers between devices, ring_body(): pass_y = lax.ppermute(on_y, 'dp', along_y)  4.08 us
    ppermute x1, waiting for transfers between devices, ring_body(): far_x = lax.ppermute(w_x[:half], 'dp', along_y)  3.65 us
  transfers between devices with their start and end apart: 24, of which 13 were waited for; matrix products, arithmetic and copies ran while one was open for 2% of the time, Pallas kernels for 15%

profile of v3, /device:TPU:0, one launch (start us, length us, event | category | flops | bytes accessed | tf_op | source)
XLA Modules:
  0.0 131.7 jit_solution(5875399915731829031)
XLA Ops:
  0.7 1.5 %copy.10 = bf16[128,8,2,256]{3,1,2,0:T(8,128)(2,1)S(1)} copy(bf16[128,8,2,256]{3,2,1,0:T(2,128)(2,1)} %bitcast.22) | data formatting | bytes 2097152
  2.3 1.1 pack.1
  3.4 3.0 %collective-permute-start.4 = (bf16[1024,512]{1,0:T(8,128)(2,1)S(1)}, bf16[1024,512]{1,0:T(8,128)(2,1)S(1)}, u32[]{:S(2)}, u32[]{:S(2)}) collective-permute-start(bf16[1024,512]{1,0:T(8,128)(2,1)S(1)} %bitcast.16), channel_id=1, source_target_pairs={{0,8},{8,0},{16,24},{24,16},{1,9},{9,1},{17,25},{25,17},{2,10},{10... | collective-permute-start | bytes 3145736 | tf_op jit(solution)/shard_map/ppermute | solution.py:414
  6.4 1.5 %collective-permute-start.5 = (bf16[1024,512]{1,0:T(8,128)(2,1)S(1)}, bf16[1024,512]{1,0:T(8,128)(2,1)S(1)}, u32[]{:S(2)}, u32[]{:S(2)}) collective-permute-start(bf16[1024,512]{1,0:T(8,128)(2,1)S(1)} %bitcast.17), channel_id=1, source_target_pairs={{0,16},{8,24},{16,0},{24,8},{1,17},{9,25},{17,1},{25,9},{2,18},{10... | collective-permute-start | bytes 3145736 | tf_op jit(solution)/shard_map/ppermute | solution.py:415
  8.0 1.6 %collective-permute-start.2 = (bf16[64,4224]{1,0:T(8,128)(2,1)S(1)}, bf16[64,4224]{1,0:T(8,128)(2,1)S(1)}, u32[]{:S(2)}, u32[]{:S(2)}) collective-permute-start(bf16[64,4224]{1,0:T(8,128)(2,1)S(1)} %get-tuple-element.39.refs_1_), channel_id=1, source_target_pairs={{0,2},{1,3},{2,6},{3,7},{4,0},{5,1},{6,4},{7,5},{8,10},{9,11},{10,... | collective-permute-start | bytes 1622024 | tf_op jit(solution)/shard_map/ppermute | solution.py:411
  9.5 2.6 %collective-permute-start.3 = (bf16[64,4224]{1,0:T(8,128)(2,1)S(1)}, bf16[64,4224]{1,0:T(8,128)(2,1)S(1)}, u32[]{:S(2)}, u32[]{:S(2)}) collective-permute-start(bf16[64,4224]{1,0:T(8,128)(2,1)S(1)} %get-tuple-element.40.refs_2_), channel_id=1, source_target_pairs={{0,2},{1,3},{2,6},{3,7},{4,0},{5,1},{6,4},{7,5},{8,10},{9,11},{10,... | collective-permute-start | bytes 1622024 | tf_op jit(solution)/shard_map/ppermute | solution.py:411
  12.1 11.9 %collective-permute-done.2.refs_5_ = bf16[64,4224]{1,0:T(8,128)(2,1)S(1)} collective-permute-done((bf16[64,4224]{1,0:T(8,128)(2,1)S(1)}, bf16[64,4224]{1,0:T(8,128)(2,1)S(1)}, u32[]{:S(2)}, u32[]{:S(2)}) %collective-permute-start.2) | collective-permute-done | bytes 540704 | tf_op jit(solution)/shard_map/ppermute | solution.py:411
  24.1 0.8 collective-permute-start.8
  24.9 10.8 %collective-permute-done.3.refs_6_ = bf16[64,4224]{1,0:T(8,128)(2,1)S(1)} collective-permute-done((bf16[64,4224]{1,0:T(8,128)(2,1)S(1)}, bf16[64,4224]{1,0:T(8,128)(2,1)S(1)}, u32[]{:S(2)}, u32[]{:S(2)}) %collective-permute-start.3) | collective-permute-done | bytes 540704 | tf_op jit(solution)/shard_map/ppermute | solution.py:411
  35.7 0.8 collective-permute-start.9
  36.5 0.6 collective-permute-start.10
  37.1 0.6 collective-permute-start.11
  37.7 9.5 %collective-permute-done.8.refs_9_ = bf16[64,4224]{1,0:T(8,128)(2,1)S(1)} collective-permute-done((bf16[64,4224]{1,0:T(8,128)(2,1)S(1)}, bf16[64,4224]{1,0:T(8,128)(2,1)S(1)}, u32[]{:S(2)}, u32[]{:S(2)}) %collective-permute-start.8) | collective-permute-done | bytes 540704 | tf_op jit(solution)/shard_map/ppermute | solution.py:411
  47.3 3.6 %collective-permute-done.10.refs_16_.refs_7_ = bf16[512,512]{1,0:T(8,128)(2,1)S(1)} collective-permute-done((bf16[512,512]{1,0:T(8,128)(2,1)S(1)}, bf16[512,512]{1,0:T(8,128)(2,1)S(1)}, u32[]{:S(2)}, u32[]{:S(2)}) %collective-permute-start.10) | collective-permute-done | bytes 524320 | tf_op jit(solution)/shard_map/ppermute | solution.py:418
  50.9 0.3 collective-permute-done.11.refs_17_.refs_8_
  51.2 0.2 collective-permute-start.7
  51.4 5.7 %collective-permute-done.9.refs_10_ = bf16[64,4224]{1,0:T(8,128)(2,1)S(1)} collective-permute-done((bf16[64,4224]{1,0:T(8,128)(2,1)S(1)}, bf16[64,4224]{1,0:T(8,128)(2,1)S(1)}, u32[]{:S(2)}, u32[]{:S(2)}) %collective-permute-start.9) | collective-permute-done | bytes 540704 | tf_op jit(solution)/shard_map/ppermute | solution.py:411
  57.1 0.5 collective-permute-start.13
  57.6 0.8 collective-permute-start.14
  58.4 3.4 %collective-permute-start.15 = (bf16[64,4224]{1,0:T(8,128)(2,1)S(1)}, bf16[64,4224]{1,0:T(8,128)(2,1)S(1)}, u32[]{:S(2)}, u32[]{:S(2)}) collective-permute-start(bf16[64,4224]{1,0:T(8,128)(2,1)S(1)} %collective-permute-done.9.refs_10_), channel_id=1, source_target_pairs={{0,2},{1,3},{2,6},{3,7},{4,0},{5,1},{6,4},{7,5},{8,10},{9,11},{10,... | collective-permute-start | bytes 1622024 | tf_op jit(solution)/shard_map/ppermute | solution.py:411
  61.8 12.9 %stage.1 = (s32[2]{0:T(128)S(1)}, bf16[512,768]{1,0:T(8,128)(2,1)}, f32[1,768]{1,0:T(1,128)S(1)}, f32[512,1024]{1,0:T(8,128)S(1)}, f32[512,1024]{1,0:T(8,128)S(1...) custom-call(s32[2]{0:T(128)S(1)} %get-tuple-element.38.refs_0_, bf16[64,4224]{1,0:T(8,128)(2,1)S(1)} %get-tuple-element.39.refs_1_, ...), custom_call_target="tpu_custom_call" | custom-call | flops 6442450944 | bytes 18874368 | tf_op jit(solution)/shard_map/stage/pallas_call | solution.py:235
  74.7 9.6 %collective-permute-done.15.refs_1_ = bf16[64,4224]{1,0:T(8,128)(2,1)S(1)} collective-permute-done((bf16[64,4224]{1,0:T(8,128)(2,1)S(1)}, bf16[64,4224]{1,0:T(8,128)(2,1)S(1)}, u32[]{:S(2)}, u32[]{:S(2)}) %collective-permute-start.15) | collective-permute-done | bytes 540704 | tf_op jit(solution)/shard_map/ppermute | solution.py:411
  84.3 0.5 collective-permute-start.17
  84.8 1.4 %collective-permute-done.16.refs_2_ = bf16[64,4224]{1,0:T(8,128)(2,1)S(1)} collective-permute-done((bf16[64,4224]{1,0:T(8,128)(2,1)S(1)}, bf16[64,4224]{1,0:T(8,128)(2,1)S(1)}, u32[]{:S(2)}, u32[]{:S(2)}) %collective-permute-start.16) | collective-permute-done | bytes 540704 | tf_op jit(solution)/shard_map/ppermute | solution.py:426
  86.3 0.8 collective-permute-done.17.refs_3_
  87.0 2.7 %last.1 = (s32[2]{0:T(128)S(1)}, bf16[512,256]{1,0:T(8,128)(2,1)S(1)}, f32[1,256]{1,0:T(1,128)S(1)}, bf16[256,1024]{1,0:T(8,128)(2,1)S(1)}, bf16[256,1024]{1,0:T(8,128)(2,1)S(1)}) custom-call(s32[2]{0:T(128)S(1)} %get-tuple-element.49.where_ref, bf16[64,4224]{1,0:T(8,128)(2,1)S(1)} %collective-permute-done.14.refs_0_, ...), custom_call_target="tpu_custom_call" | custom-call | flops 1342177280 | bytes 9437184 | tf_op jit(solution)/shard_map/last/pallas_call | solution.py:292
  89.8 0.7 copy-done.10
  90.5 0.5 collective-permute-start.19
  91.0 0.5 collective-permute-start.20
  91.6 7.0 %near.1 = (s32[2]{0:T(128)}, bf16[256,1024]{1,0:T(8,128)(2,1)}, bf16[256,1024]{1,0:T(8,128)(2,1)}, f32[256,1024]{1,0:T(8,128)}, f32[256,1024]{1,0:T(8,128)}, /*index=5*/f32[512,1024]{1,0:T(8,128)}) custom-call(s32[2]{0:T(128)} %copy-done.13, bf16[64,4224]{1,0:T(8,128)(2,1)} %copy-done, bf16[64,4224]{1,0:T(8,128)(2,1)} %copy-done.1, ...), custom_call_target="tpu_custom_call" | custom-call | flops 805306368 | bytes 11534336 | tf_op jit(solution)/shard_map/near/pallas_call | solution.py:343
  98.6 1.6 %collective-permute-start.18 = (bf16[256,1024]{1,0:T(8,128)(2,1)}, bf16[256,1024]{1,0:T(8,128)(2,1)S(1)}, u32[]{:S(2)}, u32[]{:S(2)}) collective-permute-start(bf16[256,1024]{1,0:T(8,128)(2,1)} %get-tuple-element.59), channel_id=1, source_target_pairs={{0,8},{8,0},{16,24},{24,16},{1,9},{9,1},{17,25},{25,17},{2,10},{10... | collective-permute-start | bytes 1572872 | tf_op jit(solution)/shard_map/ppermute | solution.py:442
  100.1 1.5 %collective-permute-start.22 = (bf16[256,1024]{1,0:T(8,128)(2,1)}, bf16[256,1024]{1,0:T(8,128)(2,1)S(1)}, u32[]{:S(2)}, u32[]{:S(2)}) collective-permute-start(bf16[256,1024]{1,0:T(8,128)(2,1)} %get-tuple-element.69), channel_id=1, source_target_pairs={{0,16},{8,24},{16,0},{24,8},{1,17},{9,25},{17,1},{25,9},{2,18},{10... | collective-permute-start | bytes 1572872 | tf_op jit(solution)/shard_map/ppermute | solution.py:443
  101.7 3.6 %collective-permute-done.19.far_y = bf16[256,1024]{1,0:T(8,128)(2,1)S(1)} collective-permute-done((bf16[256,1024]{1,0:T(8,128)(2,1)S(1)}, bf16[256,1024]{1,0:T(8,128)(2,1)S(1)}, u32[]{:S(2)}, u32[]{:S(2)}) %collective-permute-start.19) | collective-permute-done | bytes 524320 | tf_op jit(solution)/shard_map/ppermute | solution.py:440
  105.3 0.5 collective-permute-done.20.far_x
  105.8 1.2 copy-done.7
  107.0 1.2 copy-done.8
  108.3 0.3 join.1
  108.6 1.6 %collective-permute-start.21 = (bf16[256,1024]{1,0:T(8,128)(2,1)S(1)}, bf16[256,1024]{1,0:T(8,128)(2,1)S(1)}, u32[]{:S(2)}, u32[]{:S(2)}) collective-permute-start(bf16[256,1024]{1,0:T(8,128)(2,1)S(1)} %get-tuple-element.68), channel_id=1, source_target_pairs={{0,16},{8,24},{16,0},{24,8},{1,17},{9,25},{17,1},{25,9},{2,18},{10... | collective-permute-start | bytes 1572872 | tf_op jit(solution)/shard_map/ppermute | solution.py:460
  110.2 0.5 collective-permute-start.23
  110.7 0.7 constant_dynamic-slice_fusion
  111.5 0.6 scatter_custom_fusion
  112.1 10.2 %all_to_all.9 = f32[8,1,128]{2,1,0:T(1,128)S(1)} all-to-all(f32[8,1,128]{2,1,0:T(1,128)S(1)} %bitcast.23), channel_id=1, replica_groups=mesh['dp'=4,'label'=8] {'label'}, dimensions={0} | all-to-all | bytes 8192 | tf_op jit(solution)/shard_map/all_to_all | solution.py:463
  122.4 0.5 broadcast_multiply_fusion
  122.9 4.1 %collective-permute-done.21 = bf16[256,1024]{1,0:T(8,128)(2,1)S(1)} collective-permute-done((bf16[256,1024]{1,0:T(8,128)(2,1)S(1)}, bf16[256,1024]{1,0:T(8,128)(2,1)S(1)}, u32[]{:S(2)}, u32[]{:S(2)}) %collective-permute-start.21) | collective-permute-done | bytes 524320 | tf_op jit(solution)/shard_map/ppermute | solution.py:460
  127.0 0.5 collective-permute-done.23
  127.5 2.1 %fusion = (bf16[1,256,1024]{2,1,0:T(8,128)(2,1)S(1)}, bf16[1,256,1024]{2,1,0:T(8,128)(2,1)S(1)}) fusion(bf16[256,1024]{1,0:T(8,128)(2,1)S(1)} %collective-permute-done.21, bf16[256,1024]{1,0:T(8,128)(2,1)S(1)} %collective-permute-done.18, f32[512,1024]{1,0:T(8,128)} %get-tuple-element.58, bf16[256,1024]{1,0:T(8,128)(2,1)S(1)} %collective-permute-done.23, ...), kind=kLoop, calls=%fused_computation.4 | loop fusion | flops 2621440 | bytes 5242880 | tf_op jit(solution)/shard_map/stack | solution.py:468
  129.6 0.1 maximum_bitcast_fusion
  129.7 2.0 %copy.9 = bf16[1024,2,256]{2,1,0:T(2,128)(2,1)} copy(bf16[1024,2,256]{0,2,1:T(8,128)(2,1)S(1)} %maximum_bitcast_fusion) | data formatting | bytes 2097152
  (48 shorter events, 0.4 us)
Async XLA Ops:
  0.6 1.7 %copy-start.11 = (s32[128,8]{0,1:T(8,128)S(1)}, s32[128,8]{0,1:T(8,128)}, u32[]{:S(2)}) copy-start(s32[128,8]{0,1:T(8,128)} %param.7) | copy-start | bytes 12292
  0.6 1.7 %copy-start.12 = (s32[128,8]{0,1:T(8,128)S(1)}, s32[128,8]{0,1:T(8,128)}, u32[]{:S(2)}) copy-start(s32[128,8]{0,1:T(8,128)} %param.8) | copy-start | bytes 12292
  0.7 1.6 %copy-start.9 = (bf16[128,4096]{1,0:T(8,128)(2,1)S(1)}, bf16[128,4096]{1,0:T(8,128)(2,1)}, u32[]{:S(2)}) copy-start(bf16[128,4096]{1,0:T(8,128)(2,1)} %samples_ref.1) | copy-start | bytes 3145732
  3.4 32.2 %collective-permute-start.4 = (bf16[1024,512]{1,0:T(8,128)(2,1)S(1)}, bf16[1024,512]{1,0:T(8,128)(2,1)S(1)}, u32[]{:S(2)}, u32[]{:S(2)}) collective-permute-start(bf16[1024,512]{1,0:T(8,128)(2,1)S(1)} %bitcast.16), channel_id=1, source_target_pairs={{0,8},{8,0},{16,24},{24,16},{1,9},{9,1},{17,25},{25,17},{2,10},{10... | collective-permute-start | bytes 3145736 | tf_op jit(solution)/shard_map/ppermute | solution.py:414
  6.4 29.2 %collective-permute-start.5 = (bf16[1024,512]{1,0:T(8,128)(2,1)S(1)}, bf16[1024,512]{1,0:T(8,128)(2,1)S(1)}, u32[]{:S(2)}, u32[]{:S(2)}) collective-permute-start(bf16[1024,512]{1,0:T(8,128)(2,1)S(1)} %bitcast.17), channel_id=1, source_target_pairs={{0,16},{8,24},{16,0},{24,8},{1,17},{9,25},{17,1},{25,9},{2,18},{10... | collective-permute-start | bytes 3145736 | tf_op jit(solution)/shard_map/ppermute | solution.py:415
  8.0 16.1 %collective-permute-start.2 = (bf16[64,4224]{1,0:T(8,128)(2,1)S(1)}, bf16[64,4224]{1,0:T(8,128)(2,1)S(1)}, u32[]{:S(2)}, u32[]{:S(2)}) collective-permute-start(bf16[64,4224]{1,0:T(8,128)(2,1)S(1)} %get-tuple-element.39.refs_1_), channel_id=1, source_target_pairs={{0,2},{1,3},{2,6},{3,7},{4,0},{5,1},{6,4},{7,5},{8,10},{9,11},{10,... | collective-permute-start | bytes 1622024 | tf_op jit(solution)/shard_map/ppermute | solution.py:411
  9.5 26.1 %collective-permute-start.3 = (bf16[64,4224]{1,0:T(8,128)(2,1)S(1)}, bf16[64,4224]{1,0:T(8,128)(2,1)S(1)}, u32[]{:S(2)}, u32[]{:S(2)}) collective-permute-start(bf16[64,4224]{1,0:T(8,128)(2,1)S(1)} %get-tuple-element.40.refs_2_), channel_id=1, source_target_pairs={{0,2},{1,3},{2,6},{3,7},{4,0},{5,1},{6,4},{7,5},{8,10},{9,11},{10,... | collective-permute-start | bytes 1622024 | tf_op jit(solution)/shard_map/ppermute | solution.py:411
  24.1 23.2 %collective-permute-start.8 = (bf16[64,4224]{1,0:T(8,128)(2,1)S(1)}, bf16[64,4224]{1,0:T(8,128)(2,1)S(1)}, u32[]{:S(2)}, u32[]{:S(2)}) collective-permute-start(bf16[64,4224]{1,0:T(8,128)(2,1)S(1)} %collective-permute-done.2.refs_5_), channel_id=1, source_target_pairs={{0,2},{1,3},{2,6},{3,7},{4,0},{5,1},{6,4},{7,5},{8,10},{9,11},{10,... | collective-permute-start | bytes 1622024 | tf_op jit(solution)/shard_map/ppermute | solution.py:411
  35.7 21.4 %collective-permute-start.9 = (bf16[64,4224]{1,0:T(8,128)(2,1)S(1)}, bf16[64,4224]{1,0:T(8,128)(2,1)S(1)}, u32[]{:S(2)}, u32[]{:S(2)}) collective-permute-start(bf16[64,4224]{1,0:T(8,128)(2,1)S(1)} %collective-permute-done.3.refs_6_), channel_id=1, source_target_pairs={{0,2},{1,3},{2,6},{3,7},{4,0},{5,1},{6,4},{7,5},{8,10},{9,11},{10,... | collective-permute-start | bytes 1622024 | tf_op jit(solution)/shard_map/ppermute | solution.py:411
  36.5 20.6 %collective-permute-start = (bf16[64,4224]{1,0:T(8,128)(2,1)S(1)}, bf16[64,4224]{1,0:T(8,128)(2,1)S(1)}, u32[]{:S(2)}, u32[]{:S(2)}) collective-permute-start(bf16[64,4224]{1,0:T(8,128)(2,1)S(1)} %get-tuple-element.39.refs_1_), channel_id=1, source_target_pairs={{0,1},{1,0},{2,3},{3,2},{4,5},{5,4},{6,7},{7,6},{8,9},{9,8},{10,11... | collective-permute-start | bytes 1622024 | tf_op jit(solution)/shard_map/ppermute | solution.py:426
  36.5 14.4 %collective-permute-start.10 = (bf16[512,512]{1,0:T(8,128)(2,1)S(1)}, bf16[512,512]{1,0:T(8,128)(2,1)S(1)}, u32[]{:S(2)}, u32[]{:S(2)}) collective-permute-start(bf16[512,512]{1,0:T(8,128)(2,1)S(1)} %slice.12), channel_id=1, source_target_pairs={{0,16},{8,24},{16,0},{24,8},{1,17},{9,25},{17,1},{25,9},{2,18},{10... | collective-permute-start | bytes 1572872 | tf_op jit(solution)/shard_map/ppermute | solution.py:418
  37.1 14.1 %collective-permute-start.11 = (bf16[512,512]{1,0:T(8,128)(2,1)S(1)}, bf16[512,512]{1,0:T(8,128)(2,1)S(1)}, u32[]{:S(2)}, u32[]{:S(2)}) collective-permute-start(bf16[512,512]{1,0:T(8,128)(2,1)S(1)} %slice.13), channel_id=1, source_target_pairs={{0,8},{8,0},{16,24},{24,16},{1,9},{9,1},{17,25},{25,17},{2,10},{10... | collective-permute-start | bytes 1572872 | tf_op jit(solution)/shard_map/ppermute | solution.py:419
  47.3 10.3 %collective-permute-start.1 = (bf16[64,4224]{1,0:T(8,128)(2,1)S(1)}, bf16[64,4224]{1,0:T(8,128)(2,1)S(1)}, u32[]{:S(2)}, u32[]{:S(2)}) collective-permute-start(bf16[64,4224]{1,0:T(8,128)(2,1)S(1)} %get-tuple-element.40.refs_2_), channel_id=1, source_target_pairs={{0,1},{1,0},{2,3},{3,2},{4,5},{5,4},{6,7},{7,6},{8,9},{9,8},{10,11... | collective-permute-start | bytes 1622024 | tf_op jit(solution)/shard_map/ppermute | solution.py:426
  50.9 7.5 %collective-permute-start.6 = (bf16[64,4224]{1,0:T(8,128)(2,1)S(1)}, bf16[64,4224]{1,0:T(8,128)(2,1)S(1)}, u32[]{:S(2)}, u32[]{:S(2)}) collective-permute-start(bf16[64,4224]{1,0:T(8,128)(2,1)S(1)} %collective-permute-done.2.refs_5_), channel_id=1, source_target_pairs={{0,1},{1,0},{2,3},{3,2},{4,5},{5,4},{6,7},{7,6},{8,9},{9,8},{10,11... | collective-permute-start | bytes 1622024 | tf_op jit(solution)/shard_map/ppermute | solution.py:426
  51.2 10.5 %collective-permute-start.7 = (bf16[64,4224]{1,0:T(8,128)(2,1)S(1)}, bf16[64,4224]{1,0:T(8,128)(2,1)S(1)}, u32[]{:S(2)}, u32[]{:S(2)}) collective-permute-start(bf16[64,4224]{1,0:T(8,128)(2,1)S(1)} %collective-permute-done.3.refs_6_), channel_id=1, source_target_pairs={{0,1},{1,0},{2,3},{3,2},{4,5},{5,4},{6,7},{7,6},{8,9},{9,8},{10,11... | collective-permute-start | bytes 1622024 | tf_op jit(solution)/shard_map/ppermute | solution.py:426
  57.1 4.7 %collective-permute-start.12 = (bf16[64,4224]{1,0:T(8,128)(2,1)S(1)}, bf16[64,4224]{1,0:T(8,128)(2,1)S(1)}, u32[]{:S(2)}, u32[]{:S(2)}) collective-permute-start(bf16[64,4224]{1,0:T(8,128)(2,1)S(1)} %collective-permute-done.8.refs_9_), channel_id=1, source_target_pairs={{0,1},{1,0},{2,3},{3,2},{4,5},{5,4},{6,7},{7,6},{8,9},{9,8},{10,11... | collective-permute-start | bytes 1622024 | tf_op jit(solution)/shard_map/ppermute | solution.py:426
  57.1 4.7 %collective-permute-start.13 = (bf16[64,4224]{1,0:T(8,128)(2,1)S(1)}, bf16[64,4224]{1,0:T(8,128)(2,1)S(1)}, u32[]{:S(2)}, u32[]{:S(2)}) collective-permute-start(bf16[64,4224]{1,0:T(8,128)(2,1)S(1)} %collective-permute-done.9.refs_10_), channel_id=1, source_target_pairs={{0,1},{1,0},{2,3},{3,2},{4,5},{5,4},{6,7},{7,6},{8,9},{9,8},{10,11... | collective-permute-start | bytes 1622024 | tf_op jit(solution)/shard_map/ppermute | solution.py:426
  57.6 17.1 %collective-permute-start.14 = (bf16[64,4224]{1,0:T(8,128)(2,1)S(1)}, bf16[64,4224]{1,0:T(8,128)(2,1)S(1)}, u32[]{:S(2)}, u32[]{:S(2)}) collective-permute-start(bf16[64,4224]{1,0:T(8,128)(2,1)S(1)} %collective-permute-done.8.refs_9_), channel_id=1, source_target_pairs={{0,2},{1,3},{2,6},{3,7},{4,0},{5,1},{6,4},{7,5},{8,10},{9,11},{10,... | collective-permute-start | bytes 1622024 | tf_op jit(solution)/shard_map/ppermute | solution.py:411
  58.4 25.9 %collective-permute-start.15 = (bf16[64,4224]{1,0:T(8,128)(2,1)S(1)}, bf16[64,4224]{1,0:T(8,128)(2,1)S(1)}, u32[]{:S(2)}, u32[]{:S(2)}) collective-permute-start(bf16[64,4224]{1,0:T(8,128)(2,1)S(1)} %collective-permute-done.9.refs_10_), channel_id=1, source_target_pairs={{0,2},{1,3},{2,6},{3,7},{4,0},{5,1},{6,4},{7,5},{8,10},{9,11},{10,... | collective-permute-start | bytes 1622024 | tf_op jit(solution)/shard_map/ppermute | solution.py:411
  74.7 15.1 %copy-start.4 = (f32[512,1024]{1,0:T(8,128)}, f32[512,1024]{1,0:T(8,128)S(1)}, u32[]{:S(2)}) copy-start(f32[512,1024]{1,0:T(8,128)S(1)} %get-tuple-element.54.refs_4_) | copy-start | bytes 6291460
  74.7 15.1 %copy-start.5 = (f32[512,1024]{1,0:T(8,128)}, f32[512,1024]{1,0:T(8,128)S(1)}, u32[]{:S(2)}) copy-start(f32[512,1024]{1,0:T(8,128)S(1)} %get-tuple-element.55.refs_5_) | copy-start | bytes 6291460
  74.7 15.1 %copy-start.6 = (f32[512,1024]{1,0:T(8,128)}, f32[512,1024]{1,0:T(8,128)S(1)}, u32[]{:S(2)}) copy-start(f32[512,1024]{1,0:T(8,128)S(1)} %get-tuple-element.56.refs_6_) | copy-start | bytes 6291460
  74.7 15.1 %copy-start = (bf16[64,4224]{1,0:T(8,128)(2,1)}, bf16[64,4224]{1,0:T(8,128)(2,1)S(1)}, u32[]{:S(2)}) copy-start(bf16[64,4224]{1,0:T(8,128)(2,1)S(1)} %collective-permute-done.14.refs_0_) | copy-start | bytes 1622020
  84.3 5.5 %copy-start.1 = (bf16[64,4224]{1,0:T(8,128)(2,1)}, bf16[64,4224]{1,0:T(8,128)(2,1)S(1)}, u32[]{:S(2)}) copy-start(bf16[64,4224]{1,0:T(8,128)(2,1)S(1)} %collective-permute-done.15.refs_1_) | copy-start | bytes 1622020
  84.3 1.9 %collective-permute-start.16 = (bf16[64,4224]{1,0:T(8,128)(2,1)S(1)}, bf16[64,4224]{1,0:T(8,128)(2,1)S(1)}, u32[]{:S(2)}, u32[]{:S(2)}) collective-permute-start(bf16[64,4224]{1,0:T(8,128)(2,1)S(1)} %collective-permute-done.14.refs_0_), channel_id=1, source_target_pairs={{0,1},{1,0},{2,3},{3,2},{4,5},{5,4},{6,7},{7,6},{8,9},{9,8},{10,11... | collective-permute-start | bytes 1622024 | tf_op jit(solution)/shard_map/ppermute | solution.py:426
  84.3 2.7 %collective-permute-start.17 = (bf16[64,4224]{1,0:T(8,128)(2,1)S(1)}, bf16[64,4224]{1,0:T(8,128)(2,1)S(1)}, u32[]{:S(2)}, u32[]{:S(2)}) collective-permute-start(bf16[64,4224]{1,0:T(8,128)(2,1)S(1)} %collective-permute-done.15.refs_1_), channel_id=1, source_target_pairs={{0,1},{1,0},{2,3},{3,2},{4,5},{5,4},{6,7},{7,6},{8,9},{9,8},{10,11... | collective-permute-start | bytes 1622024 | tf_op jit(solution)/shard_map/ppermute | solution.py:426
  86.3 3.5 %copy-start.2 = (bf16[64,4224]{1,0:T(8,128)(2,1)}, bf16[64,4224]{1,0:T(8,128)(2,1)S(1)}, u32[]{:S(2)}) copy-start(bf16[64,4224]{1,0:T(8,128)(2,1)S(1)} %collective-permute-done.16.refs_2_) | copy-start | bytes 1622020
  87.0 2.8 %copy-start.3 = (bf16[64,4224]{1,0:T(8,128)(2,1)}, bf16[64,4224]{1,0:T(8,128)(2,1)S(1)}, u32[]{:S(2)}) copy-start(bf16[64,4224]{1,0:T(8,128)(2,1)S(1)} %collective-permute-done.17.refs_3_) | copy-start | bytes 1622020
  89.8 0.7 copy-start.10
  90.5 0.5 copy-start.13
  90.5 14.8 %collective-permute-start.19 = (bf16[256,1024]{1,0:T(8,128)(2,1)S(1)}, bf16[256,1024]{1,0:T(8,128)(2,1)S(1)}, u32[]{:S(2)}, u32[]{:S(2)}) collective-permute-start(bf16[256,1024]{1,0:T(8,128)(2,1)S(1)} %get-tuple-element.63), channel_id=1, source_target_pairs={{0,16},{8,24},{16,0},{24,8},{1,17},{9,25},{17,1},{25,9},{2,18},{10... | collective-permute-start | bytes 1572872 | tf_op jit(solution)/shard_map/ppermute | solution.py:440
  91.0 14.8 %collective-permute-start.20 = (bf16[256,1024]{1,0:T(8,128)(2,1)S(1)}, bf16[256,1024]{1,0:T(8,128)(2,1)S(1)}, u32[]{:S(2)}, u32[]{:S(2)}) collective-permute-start(bf16[256,1024]{1,0:T(8,128)(2,1)S(1)} %get-tuple-element.65), channel_id=1, source_target_pairs={{0,8},{8,0},{16,24},{24,16},{1,9},{9,1},{17,25},{25,17},{2,10},{10... | collective-permute-start | bytes 1572872 | tf_op jit(solution)/shard_map/ppermute | solution.py:439
  98.6 24.3 %collective-permute-start.18 = (bf16[256,1024]{1,0:T(8,128)(2,1)}, bf16[256,1024]{1,0:T(8,128)(2,1)S(1)}, u32[]{:S(2)}, u32[]{:S(2)}) collective-permute-start(bf16[256,1024]{1,0:T(8,128)(2,1)} %get-tuple-element.59), channel_id=1, source_target_pairs={{0,8},{8,0},{16,24},{24,16},{1,9},{9,1},{17,25},{25,17},{2,10},{10... | collective-permute-start | bytes 1572872 | tf_op jit(solution)/shard_map/ppermute | solution.py:442
  100.1 22.7 %collective-permute-start.22 = (bf16[256,1024]{1,0:T(8,128)(2,1)}, bf16[256,1024]{1,0:T(8,128)(2,1)S(1)}, u32[]{:S(2)}, u32[]{:S(2)}) collective-permute-start(bf16[256,1024]{1,0:T(8,128)(2,1)} %get-tuple-element.69), channel_id=1, source_target_pairs={{0,16},{8,24},{16,0},{24,8},{1,17},{9,25},{17,1},{25,9},{2,18},{10... | collective-permute-start | bytes 1572872 | tf_op jit(solution)/shard_map/ppermute | solution.py:443
  105.8 1.2 copy-start.7
  107.0 1.2 copy-start.8
  108.6 18.4 %collective-permute-start.21 = (bf16[256,1024]{1,0:T(8,128)(2,1)S(1)}, bf16[256,1024]{1,0:T(8,128)(2,1)S(1)}, u32[]{:S(2)}, u32[]{:S(2)}) collective-permute-start(bf16[256,1024]{1,0:T(8,128)(2,1)S(1)} %get-tuple-element.68), channel_id=1, source_target_pairs={{0,16},{8,24},{16,0},{24,8},{1,17},{9,25},{17,1},{25,9},{2,18},{10... | collective-permute-start | bytes 1572872 | tf_op jit(solution)/shard_map/ppermute | solution.py:460
  110.2 17.3 %collective-permute-start.23 = (bf16[256,1024]{1,0:T(8,128)(2,1)S(1)}, bf16[256,1024]{1,0:T(8,128)(2,1)S(1)}, u32[]{:S(2)}, u32[]{:S(2)}) collective-permute-start(bf16[256,1024]{1,0:T(8,128)(2,1)S(1)} %get-tuple-element.70), channel_id=1, source_target_pairs={{0,8},{8,0},{16,24},{24,16},{1,9},{9,1},{17,25},{25,17},{2,10},{10... | collective-permute-start | bytes 1572872 | tf_op jit(solution)/shard_map/ppermute | solution.py:459

commit v4 on v3

--- a/solution.py
+++ b/solution.py
@@ -356,7 +356,7 @@
             *(pltpu.VMEM(array.shape, array.dtype) for array in inputs),
             pltpu.SemaphoreType.DMA((len(inputs),)),
         ],
-        compiler_params=pltpu.CompilerParams(vmem_limit_bytes=58 << 20),
+        compiler_params=pltpu.CompilerParams(vmem_limit_bytes=24 << 20),
         cost_estimate=pl.CostEstimate(
             flops=6 * rows * columns * depth,
             bytes_accessed=22 * columns * depth,
@@ -378,9 +378,49 @@
         out_shape=(part, part),
         in_specs=[whole] * 4,
         out_specs=(whole, whole),
-        compiler_params=pltpu.CompilerParams(vmem_limit_bytes=16 << 20),
+        compiler_params=pltpu.CompilerParams(vmem_limit_bytes=4 << 20),
         name="join",
     )(on_x, far_y, on_y, far_x)
+
+
+def base_kernel(own, got_x, got_y, out):
+    width = got_x.shape[0]
+    out[:width] = own[:width] + got_x[...].astype(jnp.float32)
+    out[width:] = own[width:] + got_y[...].astype(jnp.float32)
+
+
+def base_call(own, got_x, got_y):
+    return pl.pallas_call(
+        base_kernel,
+        out_shape=jax.ShapeDtypeStruct(own.shape, own.dtype),
+        in_specs=[whole] * 3,
+        out_specs=whole,
+        compiler_params=pltpu.CompilerParams(vmem_limit_bytes=4 << 20),
+        name="base",
+    )(own, got_x, got_y)
+
+
+def final_kernel(base, pass_y, pass_x, out):
+    tile = 256
+    width = pass_y.shape[0]
+    for step in range(out.shape[0] // tile):
+        span = slice(step * tile, (step + 1) * tile)
+        first = base[:width, span] + pass_y[:, span].astype(jnp.float32)
+        second = base[width:, span] + pass_x[:, span].astype(jnp.float32)
+        out[span, :width] = first.T.astype(out.dtype)
+        out[span, width:] = second.T.astype(out.dtype)
+
+
+def final_call(base, pass_y, pass_x):
+    columns, depth = base.shape
+    return pl.pallas_call(
+        final_kernel,
+        out_shape=jax.ShapeDtypeStruct((depth, columns), jnp.bfloat16),
+        in_specs=[whole] * 3,
+        out_specs=whole,
+        compiler_params=pltpu.CompilerParams(vmem_limit_bytes=4 << 20),
+        name="final",
+    )(base, pass_y, pass_x)
 
 
 def tie(*values):
@@ -442,7 +482,6 @@
     got_x = lax.ppermute(near_x, "dp", along_x)
     got_y = lax.ppermute(near_y, "dp", along_y)
     on_x, on_y = join_call(on_x, far_y, on_y, far_x)
-    width = label_count
 
     order = []
     for z in range(chips):
@@ -463,9 +502,8 @@
     returned = lax.all_to_all(total, "label", split_axis=0, concat_axis=0, tiled=True)
     sample_loss = jnp.sum(returned, axis=0) / (pick_count * label_count)
 
-    first = own[:width] + got_x.astype(jnp.float32) + pass_y.astype(jnp.float32)
-    second = own[width:] + got_y.astype(jnp.float32) + pass_x.astype(jnp.float32)
-    weight_grad = jnp.transpose(jnp.stack([first, second]), (2, 0, 1)).astype(jnp.bfloat16)
+    weight_grad = final_call(base_call(own, got_x, got_y), pass_y, pass_x)
+    weight_grad = weight_grad.reshape(depth, local_count, label_count)
     return (weight_grad, sample_loss)
 
 

time: 132 us -> 131 us (level)
  blocking collectives: 10.2 us -> 0 us
  waiting for transfers between devices: 62.5 us -> 68.7 us
  starting transfers between devices: 23.1 us -> 27.8 us
  other arithmetic: 2.83 us -> 0.63 us
    all_to_all x1 -> x0, blocking collectives: 10.2 us -> none  [ring_body(): lax.all_to_all(total, 'label', split_axis=0, concat_axis=0, tiled=True)]
    all_to_all x0 -> x1, starting transfers between devices: none -> 4.86 us  [ring_body(): lax.all_to_all(total, 'label', split_axis=0, concat_axis=0, tiled=True)]
    all_to_all x0 -> x1, waiting for transfers between devices: none -> 3.78 us  [ring_body(): lax.all_to_all(total, 'label', split_axis=0, concat_axis=0, tiled=True)]
    pallas_call x1, Pallas kernels: 6.99 us -> 3.22 us  [near_call(): pl.pallas_call(functools.partial(near_kernel, len(xs)), out_shape=(jax.Sh...]
    ppermute x1, waiting for transfers between devices: 3.64 us -> 6.45 us  [ring_body(): far_y = lax.ppermute(far_1, 'dp', along_y)]
    unnamed x30 -> x11, local copies, waits for them, and re-layouts: 6.76 us -> 4.47 us
    another operation x1 -> x0, other arithmetic: 2.1 us -> none  [ring_body(): jnp.stack([first, second])]
    pallas_call x1, Pallas kernels: 0.29 us -> 2.32 us  [join_call(): pl.pallas_call(join_kernel, out_shape=(part, part), in_specs=[whole] * 4,...]
  transfers between devices with their start and end apart: 24 -> 25, of which waited for: 13 -> 14; matrix products, arithmetic and copies ran while one was open for 2% -> 2% of each run, Pallas kernels for 15% -> 14%
where the time goes in v4:
time: 131 us; the launch traced here: 130 us
  waiting for transfers between devices  68.7 us (52%)
  starting transfers between devices  27.8 us (21%)
  Pallas kernels  24.9 us (19%)
  local copies, waits for them, and re-layouts  7.57 us (6%)
    ppermute x6, waiting for transfers between devices, hops(): return [lax.ppermute(block, 'label', hop) for block in blocks]  47.6 us
    pallas_call x1, Pallas kernels, stage_call(): pl.pallas_call(functools.partial(stage_kernel, tuple((len(group) for grou...  12.9 us
    ppermute x6, starting transfers between devices, hops(): return [lax.ppermute(block, 'label', hop) for block in blocks]  9.9 us
    ppermute x1, waiting for transfers between devices, ring_body(): far_y = lax.ppermute(far_1, 'dp', along_y)  6.45 us
    all_to_all x1, starting transfers between devices, ring_body(): lax.all_to_all(total, 'label', split_axis=0, concat_axis=0, tiled=True)  4.86 us
    unnamed x11, local copies, waits for them, and re-layouts  4.47 us
    ppermute x1, waiting for transfers between devices, ring_body(): pass_y = lax.ppermute(on_y, 'dp', along_y)  3.85 us
    all_to_all x1, waiting for transfers between devices, ring_body(): lax.all_to_all(total, 'label', split_axis=0, concat_axis=0, tiled=True)  3.78 us
  transfers between devices with their start and end apart: 25, of which 14 were waited for; matrix products, arithmetic and copies ran while one was open for 2% of the time, Pallas kernels for 14%

profile of v4, /device:TPU:0, one launch (start us, length us, event | category | flops | bytes accessed | tf_op | source)
XLA Modules:
  0.0 130.4 jit_solution(1808644563515394634)
XLA Ops:
  0.7 1.5 %copy.7 = bf16[128,8,2,256]{3,1,2,0:T(8,128)(2,1)S(1)} copy(bf16[128,8,2,256]{3,2,1,0:T(2,128)(2,1)} %bitcast.16) | data formatting | bytes 2097152
  2.3 1.1 pack.1
  3.4 3.0 %collective-permute-start.4 = (bf16[1024,512]{1,0:T(8,128)(2,1)S(1)}, bf16[1024,512]{1,0:T(8,128)(2,1)S(1)}, u32[]{:S(2)}, u32[]{:S(2)}) collective-permute-start(bf16[1024,512]{1,0:T(8,128)(2,1)S(1)} %bitcast.10), channel_id=1, source_target_pairs={{0,8},{8,0},{16,24},{24,16},{1,9},{9,1},{17,25},{25,17},{2,10},{10... | collective-permute-start | bytes 3145736 | tf_op jit(solution)/shard_map/ppermute | solution.py:454
  6.5 1.5 %collective-permute-start.5 = (bf16[1024,512]{1,0:T(8,128)(2,1)S(1)}, bf16[1024,512]{1,0:T(8,128)(2,1)S(1)}, u32[]{:S(2)}, u32[]{:S(2)}) collective-permute-start(bf16[1024,512]{1,0:T(8,128)(2,1)S(1)} %bitcast.11), channel_id=1, source_target_pairs={{0,16},{8,24},{16,0},{24,8},{1,17},{9,25},{17,1},{25,9},{2,18},{10... | collective-permute-start | bytes 3145736 | tf_op jit(solution)/shard_map/ppermute | solution.py:455
  8.0 1.6 %collective-permute-start.2 = (bf16[64,4224]{1,0:T(8,128)(2,1)S(1)}, bf16[64,4224]{1,0:T(8,128)(2,1)S(1)}, u32[]{:S(2)}, u32[]{:S(2)}) collective-permute-start(bf16[64,4224]{1,0:T(8,128)(2,1)S(1)} %get-tuple-element.39.refs_1_), channel_id=1, source_target_pairs={{0,2},{1,3},{2,6},{3,7},{4,0},{5,1},{6,4},{7,5},{8,10},{9,11},{10,... | collective-permute-start | bytes 1622024 | tf_op jit(solution)/shard_map/ppermute | solution.py:451
  9.5 2.6 %collective-permute-start.3 = (bf16[64,4224]{1,0:T(8,128)(2,1)S(1)}, bf16[64,4224]{1,0:T(8,128)(2,1)S(1)}, u32[]{:S(2)}, u32[]{:S(2)}) collective-permute-start(bf16[64,4224]{1,0:T(8,128)(2,1)S(1)} %get-tuple-element.40.refs_2_), channel_id=1, source_target_pairs={{0,2},{1,3},{2,6},{3,7},{4,0},{5,1},{6,4},{7,5},{8,10},{9,11},{10,... | collective-permute-start | bytes 1622024 | tf_op jit(solution)/shard_map/ppermute | solution.py:451
  12.1 11.9 %collective-permute-done.2.refs_5_ = bf16[64,4224]{1,0:T(8,128)(2,1)S(1)} collective-permute-done((bf16[64,4224]{1,0:T(8,128)(2,1)S(1)}, bf16[64,4224]{1,0:T(8,128)(2,1)S(1)}, u32[]{:S(2)}, u32[]{:S(2)}) %collective-permute-start.2) | collective-permute-done | bytes 540704 | tf_op jit(solution)/shard_map/ppermute | solution.py:451
  24.1 0.8 collective-permute-start.8
  24.9 10.8 %collective-permute-done.3.refs_6_ = bf16[64,4224]{1,0:T(8,128)(2,1)S(1)} collective-permute-done((bf16[64,4224]{1,0:T(8,128)(2,1)S(1)}, bf16[64,4224]{1,0:T(8,128)(2,1)S(1)}, u32[]{:S(2)}, u32[]{:S(2)}) %collective-permute-start.3) | collective-permute-done | bytes 540704 | tf_op jit(solution)/shard_map/ppermute | solution.py:451
  35.7 0.8 collective-permute-start.9
  36.5 0.6 collective-permute-start.10
  37.1 0.6 collective-permute-start.11
  37.7 9.5 %collective-permute-done.8.refs_9_ = bf16[64,4224]{1,0:T(8,128)(2,1)S(1)} collective-permute-done((bf16[64,4224]{1,0:T(8,128)(2,1)S(1)}, bf16[64,4224]{1,0:T(8,128)(2,1)S(1)}, u32[]{:S(2)}, u32[]{:S(2)}) %collective-permute-start.8) | collective-permute-done | bytes 540704 | tf_op jit(solution)/shard_map/ppermute | solution.py:451
  47.3 3.6 %collective-permute-done.10.refs_16_.refs_7_ = bf16[512,512]{1,0:T(8,128)(2,1)S(1)} collective-permute-done((bf16[512,512]{1,0:T(8,128)(2,1)S(1)}, bf16[512,512]{1,0:T(8,128)(2,1)S(1)}, u32[]{:S(2)}, u32[]{:S(2)}) %collective-permute-start.10) | collective-permute-done | bytes 524320 | tf_op jit(solution)/shard_map/ppermute | solution.py:458
  50.9 0.3 collective-permute-done.11.refs_17_.refs_8_
  51.2 0.2 collective-permute-start.7
  51.4 5.7 %collective-permute-done.9.refs_10_ = bf16[64,4224]{1,0:T(8,128)(2,1)S(1)} collective-permute-done((bf16[64,4224]{1,0:T(8,128)(2,1)S(1)}, bf16[64,4224]{1,0:T(8,128)(2,1)S(1)}, u32[]{:S(2)}, u32[]{:S(2)}) %collective-permute-start.9) | collective-permute-done | bytes 540704 | tf_op jit(solution)/shard_map/ppermute | solution.py:451
  57.1 0.5 collective-permute-start.13
  57.6 0.8 collective-permute-start.14
  58.4 3.4 %collective-permute-start.15 = (bf16[64,4224]{1,0:T(8,128)(2,1)S(1)}, bf16[64,4224]{1,0:T(8,128)(2,1)S(1)}, u32[]{:S(2)}, u32[]{:S(2)}) collective-permute-start(bf16[64,4224]{1,0:T(8,128)(2,1)S(1)} %collective-permute-done.9.refs_10_), channel_id=1, source_target_pairs={{0,2},{1,3},{2,6},{3,7},{4,0},{5,1},{6,4},{7,5},{8,10},{9,11},{10,... | collective-permute-start | bytes 1622024 | tf_op jit(solution)/shard_map/ppermute | solution.py:451
  61.8 12.9 %stage.1 = (s32[2]{0:T(128)S(1)}, bf16[512,768]{1,0:T(8,128)(2,1)}, f32[1,768]{1,0:T(1,128)S(1)}, f32[512,1024]{1,0:T(8,128)S(1)}, f32[512,1024]{1,0:T(8,128)S(1...) custom-call(s32[2]{0:T(128)S(1)} %get-tuple-element.38.refs_0_, bf16[64,4224]{1,0:T(8,128)(2,1)S(1)} %get-tuple-element.39.refs_1_, ...), custom_call_target="tpu_custom_call" | custom-call | flops 6442450944 | bytes 18874368 | tf_op jit(solution)/shard_map/stage/pallas_call | solution.py:235
  74.7 9.7 %collective-permute-done.15.refs_1_ = bf16[64,4224]{1,0:T(8,128)(2,1)S(1)} collective-permute-done((bf16[64,4224]{1,0:T(8,128)(2,1)S(1)}, bf16[64,4224]{1,0:T(8,128)(2,1)S(1)}, u32[]{:S(2)}, u32[]{:S(2)}) %collective-permute-start.15) | collective-permute-done | bytes 540704 | tf_op jit(solution)/shard_map/ppermute | solution.py:451
  84.3 0.5 collective-permute-start.17
  84.8 1.4 %collective-permute-done.16.refs_2_ = bf16[64,4224]{1,0:T(8,128)(2,1)S(1)} collective-permute-done((bf16[64,4224]{1,0:T(8,128)(2,1)S(1)}, bf16[64,4224]{1,0:T(8,128)(2,1)S(1)}, u32[]{:S(2)}, u32[]{:S(2)}) %collective-permute-start.16) | collective-permute-done | bytes 540704 | tf_op jit(solution)/shard_map/ppermute | solution.py:466
  86.3 0.8 collective-permute-done.17.refs_3_
  87.0 3.6 %last.1 = (s32[2]{0:T(128)S(1)}, bf16[512,256]{1,0:T(8,128)(2,1)S(1)}, f32[1,256]{1,0:T(1,128)S(1)}, bf16[256,1024]{1,0:T(8,128)(2,1)}, bf16[256,1024]{1,0:T(8,128)(2,1)}) custom-call(s32[2]{0:T(128)S(1)} %get-tuple-element.49.where_ref, bf16[64,4224]{1,0:T(8,128)(2,1)S(1)} %collective-permute-done.14.refs_0_, ...), custom_call_target="tpu_custom_call" | custom-call | flops 1342177280 | bytes 9437184 | tf_op jit(solution)/shard_map/last/pallas_call | solution.py:292
  90.7 0.6 collective-permute-start.20
  91.3 0.5 collective-permute-start.21
  91.7 3.2 %near.1 = (s32[2]{0:T(128)}, bf16[256,1024]{1,0:T(8,128)(2,1)}, bf16[256,1024]{1,0:T(8,128)(2,1)}, f32[256,1024]{1,0:T(8,128)S(1)}, f32[256,1024]{1,0:T(8,128)S(1)}, /*index=5*/f32[512,1024]{1,0:T(8,128)S(1)}) custom-call(s32[2]{0:T(128)S(1)} %get-tuple-element.53.where_ref, bf16[64,4224]{1,0:T(8,128)(2,1)S(1)} %collective-permute-done.14.refs_0_, ...), custom_call_target="tpu_custom_call" | custom-call | flops 805306368 | bytes 11534336 | tf_op jit(solution)/shard_map/near/pallas_call | solution.py:343
  95.0 1.3 %copy-done = f32[512,1024]{1,0:T(8,128)} copy-done((f32[512,1024]{1,0:T(8,128)}, f32[512,1024]{1,0:T(8,128)S(1)}, u32[]{:S(2)}) %copy-start) | copy-done | bytes 2097176
  96.3 1.5 %collective-permute-start.18 = (bf16[256,1024]{1,0:T(8,128)(2,1)}, bf16[256,1024]{1,0:T(8,128)(2,1)S(1)}, u32[]{:S(2)}, u32[]{:S(2)}) collective-permute-start(bf16[256,1024]{1,0:T(8,128)(2,1)} %get-tuple-element.59), channel_id=1, source_target_pairs={{0,8},{8,0},{16,24},{24,16},{1,9},{9,1},{17,25},{25,17},{2,10},{10... | collective-permute-start | bytes 1572872 | tf_op jit(solution)/shard_map/ppermute | solution.py:482
  97.9 1.5 %collective-permute-start.19 = (bf16[256,1024]{1,0:T(8,128)(2,1)}, bf16[256,1024]{1,0:T(8,128)(2,1)S(1)}, u32[]{:S(2)}, u32[]{:S(2)}) collective-permute-start(bf16[256,1024]{1,0:T(8,128)(2,1)} %get-tuple-element.60), channel_id=1, source_target_pairs={{0,16},{8,24},{16,0},{24,8},{1,17},{9,25},{17,1},{25,9},{2,18},{10... | collective-permute-start | bytes 1572872 | tf_op jit(solution)/shard_map/ppermute | solution.py:483
  99.4 6.4 %collective-permute-done.20.far_y = bf16[256,1024]{1,0:T(8,128)(2,1)} collective-permute-done((bf16[256,1024]{1,0:T(8,128)(2,1)}, bf16[256,1024]{1,0:T(8,128)(2,1)}, u32[]{:S(2)}, u32[]{:S(2)}) %collective-permute-start.20) | collective-permute-done | bytes 524320 | tf_op jit(solution)/shard_map/ppermute | solution.py:480
  105.8 0.6 collective-permute-done.21.far_x
  106.4 2.3 %join.1 = (bf16[256,1024]{1,0:T(8,128)(2,1)}, bf16[256,1024]{1,0:T(8,128)(2,1)}) custom-call(f32[256,1024]{1,0:T(8,128)S(1)} %get-tuple-element.63.on_x, bf16[256,1024]{1,0:T(8,128)(2,1)} %collective-permute-done.20.far_y, f32[256,1024]{1,0:T(8,128)S(1)} %get-tuple-element.65.on_y, bf16[256,1024]{1,0:T(8,128)(2,1)} %collective-permute-done.21.far_x), custom_call_target="tpu_custom_call" | custom-call | tf_op jit(solution)/shard_map/join/pallas_call | solution.py:376
  108.7 1.5 %collective-permute-start.22 = (bf16[256,1024]{1,0:T(8,128)(2,1)}, bf16[256,1024]{1,0:T(8,128)(2,1)}, u32[]{:S(2)}, u32[]{:S(2)}) collective-permute-start(bf16[256,1024]{1,0:T(8,128)(2,1)} %get-tuple-element.69), channel_id=1, source_target_pairs={{0,16},{8,24},{16,0},{24,8},{1,17},{9,25},{17,1},{25,9},{2,18},{10... | collective-permute-start | bytes 1572872 | tf_op jit(solution)/shard_map/ppermute | solution.py:499
  110.2 0.5 collective-permute-start.23
  110.8 0.7 constant_dynamic-slice_fusion
  111.5 1.2 scatter_custom_fusion
  112.7 4.9 %all-to-all-start = ((f32[8,1,128]{2,1,0:T(1,128)}), f32[8,1,128]{2,1,0:T(1,128)S(1)}, u32[]{:S(2)}, u32[]{:S(2)}) async-start(f32[8,1,128]{2,1,0:T(1,128)} %bitcast.6), calls=%async_computation | async-start | bytes 8192 | tf_op jit(solution)/shard_map/all_to_all | solution.py:502
  117.6 1.6 %copy-done.1 = f32[512,1024]{1,0:T(8,128)S(1)} copy-done((f32[512,1024]{1,0:T(8,128)S(1)}, f32[512,1024]{1,0:T(8,128)}, u32[]{:S(2)}) %copy-start.1) | copy-done | bytes 2097176
  119.2 0.2 base.1
  119.3 3.8 %all-to-all-done = f32[8,1,128]{2,1,0:T(1,128)S(1)} async-done(((f32[8,1,128]{2,1,0:T(1,128)}), f32[8,1,128]{2,1,0:T(1,128)S(1)}, u32[]{:S(2)}, u32[]{:S(2)}) %all-to-all-start) | async-done | bytes 4128 | tf_op jit(solution)/shard_map/all_to_all | solution.py:502
  123.1 0.5 broadcast_multiply_fusion
  123.6 3.8 %collective-permute-done.22.pass_y = bf16[256,1024]{1,0:T(8,128)(2,1)} collective-permute-done((bf16[256,1024]{1,0:T(8,128)(2,1)}, bf16[256,1024]{1,0:T(8,128)(2,1)}, u32[]{:S(2)}, u32[]{:S(2)}) %collective-permute-start.22) | collective-permute-done | bytes 524320 | tf_op jit(solution)/shard_map/ppermute | solution.py:499
  127.5 0.2 collective-permute-done.23.pass_x
  127.7 1.6 %final.1 = bf16[1024,512]{1,0:T(8,128)(2,1)S(1)} custom-call(f32[512,1024]{1,0:T(8,128)S(1)} %base.1, bf16[256,1024]{1,0:T(8,128)(2,1)} %collective-permute-done.22.pass_y, bf16[256,1024]{1,0:T(8,128)(2,1)} %collective-permute-done.23.pass_x), custom_call_target="tpu_custom_call" | custom-call | tf_op jit(solution)/shard_map/final/pallas_call | solution.py:416
  129.3 1.1 reshape.45
  (31 shorter events, 0.3 us)
Async XLA Ops:
  0.6 1.7 %copy-start.3 = (s32[128,8]{0,1:T(8,128)S(1)}, s32[128,8]{0,1:T(8,128)}, u32[]{:S(2)}) copy-start(s32[128,8]{0,1:T(8,128)} %param.7) | copy-start | bytes 12292
  0.6 1.7 %copy-start.4 = (s32[128,8]{0,1:T(8,128)S(1)}, s32[128,8]{0,1:T(8,128)}, u32[]{:S(2)}) copy-start(s32[128,8]{0,1:T(8,128)} %param.8) | copy-start | bytes 12292
  0.7 1.6 %copy-start.2 = (bf16[128,4096]{1,0:T(8,128)(2,1)S(1)}, bf16[128,4096]{1,0:T(8,128)(2,1)}, u32[]{:S(2)}) copy-start(bf16[128,4096]{1,0:T(8,128)(2,1)} %samples_ref.1) | copy-start | bytes 3145732
  3.4 32.2 %collective-permute-start.4 = (bf16[1024,512]{1,0:T(8,128)(2,1)S(1)}, bf16[1024,512]{1,0:T(8,128)(2,1)S(1)}, u32[]{:S(2)}, u32[]{:S(2)}) collective-permute-start(bf16[1024,512]{1,0:T(8,128)(2,1)S(1)} %bitcast.10), channel_id=1, source_target_pairs={{0,8},{8,0},{16,24},{24,16},{1,9},{9,1},{17,25},{25,17},{2,10},{10... | collective-permute-start | bytes 3145736 | tf_op jit(solution)/shard_map/ppermute | solution.py:454
  6.5 29.2 %collective-permute-start.5 = (bf16[1024,512]{1,0:T(8,128)(2,1)S(1)}, bf16[1024,512]{1,0:T(8,128)(2,1)S(1)}, u32[]{:S(2)}, u32[]{:S(2)}) collective-permute-start(bf16[1024,512]{1,0:T(8,128)(2,1)S(1)} %bitcast.11), channel_id=1, source_target_pairs={{0,16},{8,24},{16,0},{24,8},{1,17},{9,25},{17,1},{25,9},{2,18},{10... | collective-permute-start | bytes 3145736 | tf_op jit(solution)/shard_map/ppermute | solution.py:455
  8.0 16.1 %collective-permute-start.2 = (bf16[64,4224]{1,0:T(8,128)(2,1)S(1)}, bf16[64,4224]{1,0:T(8,128)(2,1)S(1)}, u32[]{:S(2)}, u32[]{:S(2)}) collective-permute-start(bf16[64,4224]{1,0:T(8,128)(2,1)S(1)} %get-tuple-element.39.refs_1_), channel_id=1, source_target_pairs={{0,2},{1,3},{2,6},{3,7},{4,0},{5,1},{6,4},{7,5},{8,10},{9,11},{10,... | collective-permute-start | bytes 1622024 | tf_op jit(solution)/shard_map/ppermute | solution.py:451
  9.5 26.1 %collective-permute-start.3 = (bf16[64,4224]{1,0:T(8,128)(2,1)S(1)}, bf16[64,4224]{1,0:T(8,128)(2,1)S(1)}, u32[]{:S(2)}, u32[]{:S(2)}) collective-permute-start(bf16[64,4224]{1,0:T(8,128)(2,1)S(1)} %get-tuple-element.40.refs_2_), channel_id=1, source_target_pairs={{0,2},{1,3},{2,6},{3,7},{4,0},{5,1},{6,4},{7,5},{8,10},{9,11},{10,... | collective-permute-start | bytes 1622024 | tf_op jit(solution)/shard_map/ppermute | solution.py:451
  24.1 23.2 %collective-permute-start.8 = (bf16[64,4224]{1,0:T(8,128)(2,1)S(1)}, bf16[64,4224]{1,0:T(8,128)(2,1)S(1)}, u32[]{:S(2)}, u32[]{:S(2)}) collective-permute-start(bf16[64,4224]{1,0:T(8,128)(2,1)S(1)} %collective-permute-done.2.refs_5_), channel_id=1, source_target_pairs={{0,2},{1,3},{2,6},{3,7},{4,0},{5,1},{6,4},{7,5},{8,10},{9,11},{10,... | collective-permute-start | bytes 1622024 | tf_op jit(solution)/shard_map/ppermute | solution.py:451
  35.7 21.4 %collective-permute-start.9 = (bf16[64,4224]{1,0:T(8,128)(2,1)S(1)}, bf16[64,4224]{1,0:T(8,128)(2,1)S(1)}, u32[]{:S(2)}, u32[]{:S(2)}) collective-permute-start(bf16[64,4224]{1,0:T(8,128)(2,1)S(1)} %collective-permute-done.3.refs_6_), channel_id=1, source_target_pairs={{0,2},{1,3},{2,6},{3,7},{4,0},{5,1},{6,4},{7,5},{8,10},{9,11},{10,... | collective-permute-start | bytes 1622024 | tf_op jit(solution)/shard_map/ppermute | solution.py:451
  36.5 20.6 %collective-permute-start = (bf16[64,4224]{1,0:T(8,128)(2,1)S(1)}, bf16[64,4224]{1,0:T(8,128)(2,1)S(1)}, u32[]{:S(2)}, u32[]{:S(2)}) collective-permute-start(bf16[64,4224]{1,0:T(8,128)(2,1)S(1)} %get-tuple-element.39.refs_1_), channel_id=1, source_target_pairs={{0,1},{1,0},{2,3},{3,2},{4,5},{5,4},{6,7},{7,6},{8,9},{9,8},{10,11... | collective-permute-start | bytes 1622024 | tf_op jit(solution)/shard_map/ppermute | solution.py:466
  36.5 14.4 %collective-permute-start.10 = (bf16[512,512]{1,0:T(8,128)(2,1)S(1)}, bf16[512,512]{1,0:T(8,128)(2,1)S(1)}, u32[]{:S(2)}, u32[]{:S(2)}) collective-permute-start(bf16[512,512]{1,0:T(8,128)(2,1)S(1)} %slice.6), channel_id=1, source_target_pairs={{0,16},{8,24},{16,0},{24,8},{1,17},{9,25},{17,1},{25,9},{2,18},{10... | collective-permute-start | bytes 1572872 | tf_op jit(solution)/shard_map/ppermute | solution.py:458
  37.1 14.1 %collective-permute-start.11 = (bf16[512,512]{1,0:T(8,128)(2,1)S(1)}, bf16[512,512]{1,0:T(8,128)(2,1)S(1)}, u32[]{:S(2)}, u32[]{:S(2)}) collective-permute-start(bf16[512,512]{1,0:T(8,128)(2,1)S(1)} %slice.7), channel_id=1, source_target_pairs={{0,8},{8,0},{16,24},{24,16},{1,9},{9,1},{17,25},{25,17},{2,10},{10... | collective-permute-start | bytes 1572872 | tf_op jit(solution)/shard_map/ppermute | solution.py:459
  47.3 10.3 %collective-permute-start.1 = (bf16[64,4224]{1,0:T(8,128)(2,1)S(1)}, bf16[64,4224]{1,0:T(8,128)(2,1)S(1)}, u32[]{:S(2)}, u32[]{:S(2)}) collective-permute-start(bf16[64,4224]{1,0:T(8,128)(2,1)S(1)} %get-tuple-element.40.refs_2_), channel_id=1, source_target_pairs={{0,1},{1,0},{2,3},{3,2},{4,5},{5,4},{6,7},{7,6},{8,9},{9,8},{10,11... | collective-permute-start | bytes 1622024 | tf_op jit(solution)/shard_map/ppermute | solution.py:466
  50.9 7.5 %collective-permute-start.6 = (bf16[64,4224]{1,0:T(8,128)(2,1)S(1)}, bf16[64,4224]{1,0:T(8,128)(2,1)S(1)}, u32[]{:S(2)}, u32[]{:S(2)}) collective-permute-start(bf16[64,4224]{1,0:T(8,128)(2,1)S(1)} %collective-permute-done.2.refs_5_), channel_id=1, source_target_pairs={{0,1},{1,0},{2,3},{3,2},{4,5},{5,4},{6,7},{7,6},{8,9},{9,8},{10,11... | collective-permute-start | bytes 1622024 | tf_op jit(solution)/shard_map/ppermute | solution.py:466
  51.2 10.5 %collective-permute-start.7 = (bf16[64,4224]{1,0:T(8,128)(2,1)S(1)}, bf16[64,4224]{1,0:T(8,128)(2,1)S(1)}, u32[]{:S(2)}, u32[]{:S(2)}) collective-permute-start(bf16[64,4224]{1,0:T(8,128)(2,1)S(1)} %collective-permute-done.3.refs_6_), channel_id=1, source_target_pairs={{0,1},{1,0},{2,3},{3,2},{4,5},{5,4},{6,7},{7,6},{8,9},{9,8},{10,11... | collective-permute-start | bytes 1622024 | tf_op jit(solution)/shard_map/ppermute | solution.py:466
  57.1 4.7 %collective-permute-start.12 = (bf16[64,4224]{1,0:T(8,128)(2,1)S(1)}, bf16[64,4224]{1,0:T(8,128)(2,1)S(1)}, u32[]{:S(2)}, u32[]{:S(2)}) collective-permute-start(bf16[64,4224]{1,0:T(8,128)(2,1)S(1)} %collective-permute-done.8.refs_9_), channel_id=1, source_target_pairs={{0,1},{1,0},{2,3},{3,2},{4,5},{5,4},{6,7},{7,6},{8,9},{9,8},{10,11... | collective-permute-start | bytes 1622024 | tf_op jit(solution)/shard_map/ppermute | solution.py:466
  57.1 4.7 %collective-permute-start.13 = (bf16[64,4224]{1,0:T(8,128)(2,1)S(1)}, bf16[64,4224]{1,0:T(8,128)(2,1)S(1)}, u32[]{:S(2)}, u32[]{:S(2)}) collective-permute-start(bf16[64,4224]{1,0:T(8,128)(2,1)S(1)} %collective-permute-done.9.refs_10_), channel_id=1, source_target_pairs={{0,1},{1,0},{2,3},{3,2},{4,5},{5,4},{6,7},{7,6},{8,9},{9,8},{10,11... | collective-permute-start | bytes 1622024 | tf_op jit(solution)/shard_map/ppermute | solution.py:466
  57.6 17.1 %collective-permute-start.14 = (bf16[64,4224]{1,0:T(8,128)(2,1)S(1)}, bf16[64,4224]{1,0:T(8,128)(2,1)S(1)}, u32[]{:S(2)}, u32[]{:S(2)}) collective-permute-start(bf16[64,4224]{1,0:T(8,128)(2,1)S(1)} %collective-permute-done.8.refs_9_), channel_id=1, source_target_pairs={{0,2},{1,3},{2,6},{3,7},{4,0},{5,1},{6,4},{7,5},{8,10},{9,11},{10,... | collective-permute-start | bytes 1622024 | tf_op jit(solution)/shard_map/ppermute | solution.py:451
  58.4 25.9 %collective-permute-start.15 = (bf16[64,4224]{1,0:T(8,128)(2,1)S(1)}, bf16[64,4224]{1,0:T(8,128)(2,1)S(1)}, u32[]{:S(2)}, u32[]{:S(2)}) collective-permute-start(bf16[64,4224]{1,0:T(8,128)(2,1)S(1)} %collective-permute-done.9.refs_10_), channel_id=1, source_target_pairs={{0,2},{1,3},{2,6},{3,7},{4,0},{5,1},{6,4},{7,5},{8,10},{9,11},{10,... | collective-permute-start | bytes 1622024 | tf_op jit(solution)/shard_map/ppermute | solution.py:451
  84.3 1.9 %collective-permute-start.16 = (bf16[64,4224]{1,0:T(8,128)(2,1)S(1)}, bf16[64,4224]{1,0:T(8,128)(2,1)S(1)}, u32[]{:S(2)}, u32[]{:S(2)}) collective-permute-start(bf16[64,4224]{1,0:T(8,128)(2,1)S(1)} %collective-permute-done.14.refs_0_), channel_id=1, source_target_pairs={{0,1},{1,0},{2,3},{3,2},{4,5},{5,4},{6,7},{7,6},{8,9},{9,8},{10,11... | collective-permute-start | bytes 1622024 | tf_op jit(solution)/shard_map/ppermute | solution.py:466
  84.3 2.7 %collective-permute-start.17 = (bf16[64,4224]{1,0:T(8,128)(2,1)S(1)}, bf16[64,4224]{1,0:T(8,128)(2,1)S(1)}, u32[]{:S(2)}, u32[]{:S(2)}) collective-permute-start(bf16[64,4224]{1,0:T(8,128)(2,1)S(1)} %collective-permute-done.15.refs_1_), channel_id=1, source_target_pairs={{0,1},{1,0},{2,3},{3,2},{4,5},{5,4},{6,7},{7,6},{8,9},{9,8},{10,11... | collective-permute-start | bytes 1622024 | tf_op jit(solution)/shard_map/ppermute | solution.py:466
  90.7 15.1 %collective-permute-start.20 = (bf16[256,1024]{1,0:T(8,128)(2,1)}, bf16[256,1024]{1,0:T(8,128)(2,1)}, u32[]{:S(2)}, u32[]{:S(2)}) collective-permute-start(bf16[256,1024]{1,0:T(8,128)(2,1)} %get-tuple-element.64), channel_id=1, source_target_pairs={{0,16},{8,24},{16,0},{24,8},{1,17},{9,25},{17,1},{25,9},{2,18},{10... | collective-permute-start | bytes 1572872 | tf_op jit(solution)/shard_map/ppermute | solution.py:480
  91.3 15.1 %collective-permute-start.21 = (bf16[256,1024]{1,0:T(8,128)(2,1)}, bf16[256,1024]{1,0:T(8,128)(2,1)}, u32[]{:S(2)}, u32[]{:S(2)}) collective-permute-start(bf16[256,1024]{1,0:T(8,128)(2,1)} %get-tuple-element.66), channel_id=1, source_target_pairs={{0,8},{8,0},{16,24},{24,16},{1,9},{9,1},{17,25},{25,17},{2,10},{10... | collective-permute-start | bytes 1572872 | tf_op jit(solution)/shard_map/ppermute | solution.py:479
  95.0 1.3 %copy-start = (f32[512,1024]{1,0:T(8,128)}, f32[512,1024]{1,0:T(8,128)S(1)}, u32[]{:S(2)}) copy-start(f32[512,1024]{1,0:T(8,128)S(1)} %get-tuple-element.58.own) | copy-start | bytes 6291460
  96.3 21.2 %collective-permute-start.18 = (bf16[256,1024]{1,0:T(8,128)(2,1)}, bf16[256,1024]{1,0:T(8,128)(2,1)S(1)}, u32[]{:S(2)}, u32[]{:S(2)}) collective-permute-start(bf16[256,1024]{1,0:T(8,128)(2,1)} %get-tuple-element.59), channel_id=1, source_target_pairs={{0,8},{8,0},{16,24},{24,16},{1,9},{9,1},{17,25},{25,17},{2,10},{10... | collective-permute-start | bytes 1572872 | tf_op jit(solution)/shard_map/ppermute | solution.py:482
  97.9 19.7 %collective-permute-start.19 = (bf16[256,1024]{1,0:T(8,128)(2,1)}, bf16[256,1024]{1,0:T(8,128)(2,1)S(1)}, u32[]{:S(2)}, u32[]{:S(2)}) collective-permute-start(bf16[256,1024]{1,0:T(8,128)(2,1)} %get-tuple-element.60), channel_id=1, source_target_pairs={{0,16},{8,24},{16,0},{24,8},{1,17},{9,25},{17,1},{25,9},{2,18},{10... | collective-permute-start | bytes 1572872 | tf_op jit(solution)/shard_map/ppermute | solution.py:483
  108.7 18.8 %collective-permute-start.22 = (bf16[256,1024]{1,0:T(8,128)(2,1)}, bf16[256,1024]{1,0:T(8,128)(2,1)}, u32[]{:S(2)}, u32[]{:S(2)}) collective-permute-start(bf16[256,1024]{1,0:T(8,128)(2,1)} %get-tuple-element.69), channel_id=1, source_target_pairs={{0,16},{8,24},{16,0},{24,8},{1,17},{9,25},{17,1},{25,9},{2,18},{10... | collective-permute-start | bytes 1572872 | tf_op jit(solution)/shard_map/ppermute | solution.py:499
  110.2 17.5 %collective-permute-start.23 = (bf16[256,1024]{1,0:T(8,128)(2,1)}, bf16[256,1024]{1,0:T(8,128)(2,1)}, u32[]{:S(2)}, u32[]{:S(2)}) collective-permute-start(bf16[256,1024]{1,0:T(8,128)(2,1)} %get-tuple-element.70), channel_id=1, source_target_pairs={{0,8},{8,0},{16,24},{24,16},{1,9},{9,1},{17,25},{25,17},{2,10},{10... | collective-permute-start | bytes 1572872 | tf_op jit(solution)/shard_map/ppermute | solution.py:498
  112.7 10.4 %all-to-all-start = ((f32[8,1,128]{2,1,0:T(1,128)}), f32[8,1,128]{2,1,0:T(1,128)S(1)}, u32[]{:S(2)}, u32[]{:S(2)}) async-start(f32[8,1,128]{2,1,0:T(1,128)} %bitcast.6), calls=%async_computation | async-start | bytes 8192 | tf_op jit(solution)/shard_map/all_to_all | solution.py:502
  117.6 1.6 %copy-start.1 = (f32[512,1024]{1,0:T(8,128)S(1)}, f32[512,1024]{1,0:T(8,128)}, u32[]{:S(2)}) copy-start(f32[512,1024]{1,0:T(8,128)} %copy-done) | copy-start | bytes 6291460

commit v5 on v4

--- a/solution.py
+++ b/solution.py
@@ -83,31 +83,29 @@
     return (weight_grad, sample_loss)
 
 
-def pack_kernel(parts, where_ref, samples_ref, matches_ref, positives_ref, next_ref, *outs):
+def pack_kernel(where_ref, samples_ref, matches_ref, positives_ref, next_ref, out):
     next_ref[0] = where_ref[0]
     next_ref[1] = where_ref[1]
-    rows, feat_width = samples_ref.shape
-    part = rows // parts
-    cluster = lax.broadcasted_iota(jnp.int32, (lanes, rows), 0)
-    code = jnp.zeros((lanes, rows), jnp.int32)
+    count, feat_width = samples_ref.shape
+    half = lanes // 2
+    cluster = lax.broadcasted_iota(jnp.int32, (half, 2 * count), 0)
+    code = jnp.zeros((half, 2 * count), jnp.int32)
     for pick in range(matches_ref.shape[0]):
         hit = cluster == matches_ref[pick : pick + 1]
         code = code + jnp.where(hit, positives_ref[pick : pick + 1] + 1, 0)
-    code = code.astype(jnp.float32).T.astype(jnp.bfloat16)
-    for place, out in enumerate(outs):
-        span = slice(place * part, (place + 1) * part)
-        out[:, :feat_width] = samples_ref[span]
-        out[:, feat_width:] = code[span]
-
-
-def pack_call(where, samples, matches, positives, parts):
+    code = jnp.concatenate([code[:, :count], code[:, count:]], axis=0)
+    out[:, :feat_width] = samples_ref[...]
+    out[:, feat_width:] = code.astype(jnp.float32).T.astype(jnp.bfloat16)
+
+
+def pack_call(where, samples, matches, positives):
     rows, feat_width = samples.shape
-    block = jax.ShapeDtypeStruct((rows // parts, feat_width + lanes), jnp.bfloat16)
-    return pl.pallas_call(
-        functools.partial(pack_kernel, parts),
-        out_shape=(jax.ShapeDtypeStruct((2,), jnp.int32),) + (block,) * parts,
+    block = jax.ShapeDtypeStruct((rows, feat_width + lanes), jnp.bfloat16)
+    return pl.pallas_call(
+        pack_kernel,
+        out_shape=(jax.ShapeDtypeStruct((2,), jnp.int32),) + (block,),
         in_specs=[scalar, whole, whole, whole],
-        out_specs=(scalar,) + (whole,) * parts,
+        out_specs=(scalar, whole),
         compiler_params=pltpu.CompilerParams(vmem_limit_bytes=8 << 20),
         name="pack",
     )(where, samples, matches.T, positives.T)
@@ -136,10 +134,13 @@
 
 
 def row_terms(scores, xs, label, local_count, grad_ref, loss_ref, at):
-    feat_width = xs[0].shape[1] - lanes
-    codes = jnp.concatenate([x[:, feat_width:] for x in xs], axis=0).astype(jnp.float32)
+    feat_width = xs[0].shape[1]
+    codes = [x[:, feat_width:].astype(jnp.float32) for x in xs[1::2] for _ in range(2)]
+    codes = jnp.concatenate(codes, axis=0)
     count = codes.shape[0]
     lane = lax.broadcasted_iota(jnp.int32, codes.shape, 1)
+    row = lax.broadcasted_iota(jnp.int32, codes.shape, 0)
+    lane = lane - jnp.where((row // xs[0].shape[0]) % 2 == 1, lanes // 2, 0)
     label_count = scores.shape[1] // local_count
     label_ids = lax.broadcasted_iota(jnp.int32, (count, label_count), 1) + 1
     label_ids = label_ids.astype(jnp.float32)
@@ -220,7 +221,7 @@
 def stage_call(where, groups, ws, places, local_count, offsets):
     xs = [x for group in groups for x in group]
     rows = sum(x.shape[0] for x in xs)
-    feat_width = xs[0].shape[1] - lanes
+    feat_width = xs[0].shape[1]
     depth, columns = ws[0].shape
     sums = ()
     inputs = [*xs, *ws, *sums]
@@ -287,7 +288,7 @@
 
 def last_call(where, xs, ws, places, local_count, offset, sums):
     rows = sum(x.shape[0] for x in xs)
-    feat_width = xs[0].shape[1] - lanes
+    feat_width = xs[0].shape[1]
     depth, columns = ws[0].shape
     return pl.pallas_call(
         functools.partial(last_kernel, len(xs), places, depth, local_count, offset),
@@ -443,7 +444,9 @@
     along_x = [(i, i ^ 1) for i in range(4)]
     along_y = [(i, i ^ 2) for i in range(4)]
 
-    where, *blocks = pack_call(where, samples, matches, positives, halves)
+    part = row_count // halves
+    where, coded = pack_call(where, samples[part:], matches, positives)
+    blocks = [samples[:part], coded]
     flat, where = tie(weight.reshape(depth, local_count * label_count), where)
     half = depth // 2
 
@@ -453,11 +456,11 @@
     mine = [blocks, hops(blocks)]
     w_x = lax.ppermute(flat, "dp", along_x)
     w_y = lax.ppermute(flat, "dp", along_y)
-    mine[1][-1], w_x, w_y = tie(mine[1][-1], w_x, w_y)
+    mine[1][0], w_x, w_y = tie(mine[1][0], w_x, w_y)
     mine.append(hops(mine[1]))
     far_x = lax.ppermute(w_x[:half], "dp", along_y)
     far_y = lax.ppermute(w_y[half:], "dp", along_x)
-    mine[2][-1], far_x, far_y = tie(mine[2][-1], far_x, far_y)
+    mine[2][0], far_x, far_y = tie(mine[2][0], far_x, far_y)
     last = hops(mine[2])
     ws = [flat, w_x, w_y, far_x, far_y]
     places = ((0, 0), (1, 0), (2, 0), (3, 0), (3, half))

time: 131 us -> 130 us (level)
    ppermute x1, waiting for transfers between devices: 3.65 us -> 0.01 us  [ring_body(): far_x = lax.ppermute(w_x[:half], 'dp', along_y)]
    ppermute x6, waiting for transfers between devices: 47.6 us -> 50.3 us  [hops(): return [lax.ppermute(block, 'label', hop) for block in blocks]]
    slice x0 -> x1, local copies, waits for them, and re-layouts: none -> 1.35 us  [ring_body(): blocks = [samples[:part], coded]]
  transfers between devices with their start and end apart: 25 -> 25, of which waited for: 14 -> 11; matrix products, arithmetic and copies ran while one was open for 2% -> 2% of each run, Pallas kernels for 14% -> 14%
where the time goes in v5:
time: 130 us
  waiting for transfers between devices  67.4 us (52%)
  starting transfers between devices  28.3 us (22%)
  Pallas kernels  24.7 us (19%)
  local copies, waits for them, and re-layouts  7.78 us (6%)
    ppermute x6, waiting for transfers between devices, hops(): return [lax.ppermute(block, 'label', hop) for block in blocks]  50.3 us
    pallas_call x1, Pallas kernels, stage_call(): pl.pallas_call(functools.partial(stage_kernel, tuple((len(group) for grou...  12.7 us
    ppermute x6, starting transfers between devices, hops(): return [lax.ppermute(block, 'label', hop) for block in blocks]  10.3 us
    ppermute x1, waiting for transfers between devices, ring_body(): far_y = lax.ppermute(far_1, 'dp', along_y)  6.48 us
    all_to_all x1, starting transfers between devices, ring_body(): lax.all_to_all(total, 'label', split_axis=0, concat_axis=0, tiled=True)  4.86 us
    ppermute x1, waiting for transfers between devices, ring_body(): pass_y = lax.ppermute(on_y, 'dp', along_y)  3.84 us
    all_to_all x1, waiting for transfers between devices, ring_body(): lax.all_to_all(total, 'label', split_axis=0, concat_axis=0, tiled=True)  3.77 us
    pallas_call x1, Pallas kernels, last_call(): pl.pallas_call(functools.partial(last_kernel, len(xs), places, depth, loc...  3.65 us
  transfers between devices with their start and end apart: 25, of which 11 were waited for; matrix products, arithmetic and copies ran while one was open for 2% of the time, Pallas kernels for 14%

profile of v5, /device:TPU:0, one launch (start us, length us, event | category | flops | bytes accessed | tf_op | source)
XLA Modules:
  0.0 129.5 jit_solution(12914405672732872029)
XLA Ops:
  0.7 1.4 %fusion.3 = (bf16[64,4096]{1,0:T(8,128)(2,1)S(1)}, bf16[64,4096]{1,0:T(8,128)(2,1)S(1)}) fusion(bf16[128,4096]{1,0:T(8,128)(2,1)} %param.5), kind=kLoop, calls=%fused_computation.9 | loop fusion | bytes 2097152 | tf_op jit(solution)/shard_map/slice | solution.py:449
  2.0 0.2 copy-done.4
  2.2 0.2 copy.7
  2.5 1.1 pack.1
  3.6 3.0 %collective-permute-start.3 = (bf16[1024,512]{1,0:T(8,128)(2,1)S(1)}, bf16[1024,512]{1,0:T(8,128)(2,1)S(1)}, u32[]{:S(2)}, u32[]{:S(2)}) collective-permute-start(bf16[1024,512]{1,0:T(8,128)(2,1)S(1)} %bitcast.10), channel_id=1, source_target_pairs={{0,8},{8,0},{16,24},{24,16},{1,9},{9,1},{17,25},{25,17},{2,10},{10... | collective-permute-start | bytes 3145736 | tf_op jit(solution)/shard_map/ppermute | solution.py:457
  6.6 1.5 %collective-permute-start.4 = (bf16[1024,512]{1,0:T(8,128)(2,1)S(1)}, bf16[1024,512]{1,0:T(8,128)(2,1)S(1)}, u32[]{:S(2)}, u32[]{:S(2)}) collective-permute-start(bf16[1024,512]{1,0:T(8,128)(2,1)S(1)} %bitcast.11), channel_id=1, source_target_pairs={{0,16},{8,24},{16,0},{24,8},{1,17},{9,25},{17,1},{25,9},{2,18},{10... | collective-permute-start | bytes 3145736 | tf_op jit(solution)/shard_map/ppermute | solution.py:458
  8.2 1.6 %collective-permute-start.5 = (bf16[64,4224]{1,0:T(8,128)(2,1)S(1)}, bf16[64,4224]{1,0:T(8,128)(2,1)S(1)}, u32[]{:S(2)}, u32[]{:S(2)}) collective-permute-start(bf16[64,4224]{1,0:T(8,128)(2,1)S(1)} %get-tuple-element.38.refs_2_), channel_id=1, source_target_pairs={{0,2},{1,3},{2,6},{3,7},{4,0},{5,1},{6,4},{7,5},{8,10},{9,11},{10,... | collective-permute-start | bytes 1622024 | tf_op jit(solution)/shard_map/ppermute | solution.py:454
  9.7 2.6 %collective-permute-start.2 = (bf16[64,4096]{1,0:T(8,128)(2,1)S(1)}, bf16[64,4096]{1,0:T(8,128)(2,1)S(1)}, u32[]{:S(2)}, u32[]{:S(2)}) collective-permute-start(bf16[64,4096]{1,0:T(8,128)(2,1)S(1)} %get-tuple-element.70.refs_1_), channel_id=1, source_target_pairs={{0,2},{1,3},{2,6},{3,7},{4,0},{5,1},{6,4},{7,5},{8,10},{9,11},{10,... | collective-permute-start | bytes 1572872 | tf_op jit(solution)/shard_map/ppermute | solution.py:454
  12.3 11.9 %collective-permute-done.5.refs_6_ = bf16[64,4224]{1,0:T(8,128)(2,1)S(1)} collective-permute-done((bf16[64,4224]{1,0:T(8,128)(2,1)S(1)}, bf16[64,4224]{1,0:T(8,128)(2,1)S(1)}, u32[]{:S(2)}, u32[]{:S(2)}) %collective-permute-start.5) | collective-permute-done | bytes 540704 | tf_op jit(solution)/shard_map/ppermute | solution.py:454
  24.3 0.8 collective-permute-start.11
  25.1 10.4 %collective-permute-done.2.refs_5_ = bf16[64,4096]{1,0:T(8,128)(2,1)S(1)} collective-permute-done((bf16[64,4096]{1,0:T(8,128)(2,1)S(1)}, bf16[64,4096]{1,0:T(8,128)(2,1)S(1)}, u32[]{:S(2)}, u32[]{:S(2)}) %collective-permute-start.2) | collective-permute-done | bytes 524320 | tf_op jit(solution)/shard_map/ppermute | solution.py:454
  35.6 0.6 collective-permute-start.10
  36.2 0.2 collective-permute-start.9
  36.4 1.1 collective-permute-start.8
  37.6 9.5 %collective-permute-done.11.refs_10_ = bf16[64,4224]{1,0:T(8,128)(2,1)S(1)} collective-permute-done((bf16[64,4224]{1,0:T(8,128)(2,1)S(1)}, bf16[64,4224]{1,0:T(8,128)(2,1)S(1)}, u32[]{:S(2)}, u32[]{:S(2)}) %collective-permute-start.11) | collective-permute-done | bytes 540704 | tf_op jit(solution)/shard_map/ppermute | solution.py:454
  47.1 0.5 collective-permute-start.7
  47.7 8.9 %collective-permute-done.8.refs_9_ = bf16[64,4096]{1,0:T(8,128)(2,1)S(1)} collective-permute-done((bf16[64,4096]{1,0:T(8,128)(2,1)S(1)}, bf16[64,4096]{1,0:T(8,128)(2,1)S(1)}, u32[]{:S(2)}, u32[]{:S(2)}) %collective-permute-start.8) | collective-permute-done | bytes 524320 | tf_op jit(solution)/shard_map/ppermute | solution.py:454
  56.6 0.5 collective-permute-start.12
  57.1 0.8 collective-permute-start.15
  57.9 3.4 %collective-permute-start.14 = (bf16[64,4096]{1,0:T(8,128)(2,1)S(1)}, bf16[64,4096]{1,0:T(8,128)(2,1)S(1)}, u32[]{:S(2)}, u32[]{:S(2)}) collective-permute-start(bf16[64,4096]{1,0:T(8,128)(2,1)S(1)} %collective-permute-done.8.refs_9_), channel_id=1, source_target_pairs={{0,2},{1,3},{2,6},{3,7},{4,0},{5,1},{6,4},{7,5},{8,10},{9,11},{10,... | collective-permute-start | bytes 1572872 | tf_op jit(solution)/shard_map/ppermute | solution.py:454
  61.3 12.7 %stage.1 = (s32[2]{0:T(128)S(1)}, bf16[512,768]{1,0:T(8,128)(2,1)}, f32[1,768]{1,0:T(1,128)S(1)}, f32[512,1024]{1,0:T(8,128)S(1)}, f32[512,1024]{1,0:T(8,128)S(1...) custom-call(s32[2]{0:T(128)S(1)} %get-tuple-element.37.refs_0_, bf16[64,4096]{1,0:T(8,128)(2,1)S(1)} %get-tuple-element.70.refs_1_, ...), custom_call_target="tpu_custom_call" | custom-call | flops 6442450944 | bytes 18874368 | tf_op jit(solution)/shard_map/stage/pallas_call | solution.py:236
  74.0 9.5 %collective-permute-done.14.refs_0_ = bf16[64,4096]{1,0:T(8,128)(2,1)S(1)} collective-permute-done((bf16[64,4096]{1,0:T(8,128)(2,1)S(1)}, bf16[64,4096]{1,0:T(8,128)(2,1)S(1)}, u32[]{:S(2)}, u32[]{:S(2)}) %collective-permute-start.14) | collective-permute-done | bytes 524320 | tf_op jit(solution)/shard_map/ppermute | solution.py:454
  83.5 0.5 collective-permute-start.16
  84.0 2.2 %collective-permute-done.16.refs_2_ = bf16[64,4096]{1,0:T(8,128)(2,1)S(1)} collective-permute-done((bf16[64,4096]{1,0:T(8,128)(2,1)S(1)}, bf16[64,4096]{1,0:T(8,128)(2,1)S(1)}, u32[]{:S(2)}, u32[]{:S(2)}) %collective-permute-start.16) | collective-permute-done | bytes 524320 | tf_op jit(solution)/shard_map/ppermute | solution.py:469
  86.2 3.6 %last.1 = (s32[2]{0:T(128)S(1)}, bf16[512,256]{1,0:T(8,128)(2,1)S(1)}, f32[1,256]{1,0:T(1,128)S(1)}, bf16[256,1024]{1,0:T(8,128)(2,1)}, bf16[256,1024]{1,0:T(8,128)(2,1)}) custom-call(s32[2]{0:T(128)S(1)} %get-tuple-element.47.where_ref, bf16[64,4096]{1,0:T(8,128)(2,1)S(1)} %collective-permute-done.14.refs_0_, ...), custom_call_target="tpu_custom_call" | custom-call | flops 1342177280 | bytes 9437184 | tf_op jit(solution)/shard_map/last/pallas_call | solution.py:293
  89.8 0.6 collective-permute-start.20
  90.4 0.5 collective-permute-start.21
  90.9 3.2 %near.1 = (s32[2]{0:T(128)}, bf16[256,1024]{1,0:T(8,128)(2,1)}, bf16[256,1024]{1,0:T(8,128)(2,1)}, f32[256,1024]{1,0:T(8,128)S(1)}, f32[256,1024]{1,0:T(8,128)S(1)}, /*index=5*/f32[512,1024]{1,0:T(8,128)S(1)}) custom-call(s32[2]{0:T(128)S(1)} %get-tuple-element.51.where_ref, bf16[64,4096]{1,0:T(8,128)(2,1)S(1)} %collective-permute-done.14.refs_0_, ...), custom_call_target="tpu_custom_call" | custom-call | flops 805306368 | bytes 11534336 | tf_op jit(solution)/shard_map/near/pallas_call | solution.py:344
  94.0 1.4 %copy-done = f32[512,1024]{1,0:T(8,128)} copy-done((f32[512,1024]{1,0:T(8,128)}, f32[512,1024]{1,0:T(8,128)S(1)}, u32[]{:S(2)}) %copy-start) | copy-done | bytes 2097176
  95.4 1.5 %collective-permute-start.18 = (bf16[256,1024]{1,0:T(8,128)(2,1)}, bf16[256,1024]{1,0:T(8,128)(2,1)S(1)}, u32[]{:S(2)}, u32[]{:S(2)}) collective-permute-start(bf16[256,1024]{1,0:T(8,128)(2,1)} %get-tuple-element.57), channel_id=1, source_target_pairs={{0,8},{8,0},{16,24},{24,16},{1,9},{9,1},{17,25},{25,17},{2,10},{10... | collective-permute-start | bytes 1572872 | tf_op jit(solution)/shard_map/ppermute | solution.py:485
  96.9 1.5 %collective-permute-start.19 = (bf16[256,1024]{1,0:T(8,128)(2,1)}, bf16[256,1024]{1,0:T(8,128)(2,1)S(1)}, u32[]{:S(2)}, u32[]{:S(2)}) collective-permute-start(bf16[256,1024]{1,0:T(8,128)(2,1)} %get-tuple-element.58), channel_id=1, source_target_pairs={{0,16},{8,24},{16,0},{24,8},{1,17},{9,25},{17,1},{25,9},{2,18},{10... | collective-permute-start | bytes 1572872 | tf_op jit(solution)/shard_map/ppermute | solution.py:486
  98.5 6.5 %collective-permute-done.20.far_y = bf16[256,1024]{1,0:T(8,128)(2,1)} collective-permute-done((bf16[256,1024]{1,0:T(8,128)(2,1)}, bf16[256,1024]{1,0:T(8,128)(2,1)}, u32[]{:S(2)}, u32[]{:S(2)}) %collective-permute-start.20) | collective-permute-done | bytes 524320 | tf_op jit(solution)/shard_map/ppermute | solution.py:483
  105.0 0.5 collective-permute-done.21.far_x
  105.5 2.3 %join.1 = (bf16[256,1024]{1,0:T(8,128)(2,1)}, bf16[256,1024]{1,0:T(8,128)(2,1)}) custom-call(f32[256,1024]{1,0:T(8,128)S(1)} %get-tuple-element.61.on_x, bf16[256,1024]{1,0:T(8,128)(2,1)} %collective-permute-done.20.far_y, f32[256,1024]{1,0:T(8,128)S(1)} %get-tuple-element.63.on_y, bf16[256,1024]{1,0:T(8,128)(2,1)} %collective-permute-done.21.far_x), custom_call_target="tpu_custom_call" | custom-call | tf_op jit(solution)/shard_map/join/pallas_call | solution.py:377
  107.8 1.5 %collective-permute-start.22 = (bf16[256,1024]{1,0:T(8,128)(2,1)}, bf16[256,1024]{1,0:T(8,128)(2,1)}, u32[]{:S(2)}, u32[]{:S(2)}) collective-permute-start(bf16[256,1024]{1,0:T(8,128)(2,1)} %get-tuple-element.67), channel_id=1, source_target_pairs={{0,16},{8,24},{16,0},{24,8},{1,17},{9,25},{17,1},{25,9},{2,18},{10... | collective-permute-start | bytes 1572872 | tf_op jit(solution)/shard_map/ppermute | solution.py:502
  109.3 0.6 collective-permute-start.23
  109.9 0.7 constant_dynamic-slice_fusion
  110.6 0.1 reshape_squeeze.3
  110.7 1.2 scatter_custom_fusion
  111.8 4.9 %all-to-all-start = ((f32[8,1,128]{2,1,0:T(1,128)}), f32[8,1,128]{2,1,0:T(1,128)S(1)}, u32[]{:S(2)}, u32[]{:S(2)}) async-start(f32[8,1,128]{2,1,0:T(1,128)} %bitcast.6), calls=%async_computation | async-start | bytes 8192 | tf_op jit(solution)/shard_map/all_to_all | solution.py:505
  116.7 1.6 %copy-done.1 = f32[512,1024]{1,0:T(8,128)S(1)} copy-done((f32[512,1024]{1,0:T(8,128)S(1)}, f32[512,1024]{1,0:T(8,128)}, u32[]{:S(2)}) %copy-start.1) | copy-done | bytes 2097176
  118.3 0.2 base.1
  118.5 3.8 %all-to-all-done = f32[8,1,128]{2,1,0:T(1,128)S(1)} async-done(((f32[8,1,128]{2,1,0:T(1,128)}), f32[8,1,128]{2,1,0:T(1,128)S(1)}, u32[]{:S(2)}, u32[]{:S(2)}) %all-to-all-start) | async-done | bytes 4128 | tf_op jit(solution)/shard_map/all_to_all | solution.py:505
  122.3 0.5 broadcast_multiply_fusion
  122.8 3.8 %collective-permute-done.22.pass_y = bf16[256,1024]{1,0:T(8,128)(2,1)} collective-permute-done((bf16[256,1024]{1,0:T(8,128)(2,1)}, bf16[256,1024]{1,0:T(8,128)(2,1)}, u32[]{:S(2)}, u32[]{:S(2)}) %collective-permute-start.22) | collective-permute-done | bytes 524320 | tf_op jit(solution)/shard_map/ppermute | solution.py:502
  126.6 0.2 collective-permute-done.23.pass_x
  126.9 1.6 %final.1 = bf16[1024,512]{1,0:T(8,128)(2,1)S(1)} custom-call(f32[512,1024]{1,0:T(8,128)S(1)} %base.1, bf16[256,1024]{1,0:T(8,128)(2,1)} %collective-permute-done.22.pass_y, bf16[256,1024]{1,0:T(8,128)(2,1)} %collective-permute-done.23.pass_x), custom_call_target="tpu_custom_call" | custom-call | tf_op jit(solution)/shard_map/final/pallas_call | solution.py:417
  128.4 1.1 reshape.45
  (32 shorter events, 0.3 us)
Async XLA Ops:
  0.6 1.5 %copy-start.4 = (bf16[1024,2,256]{2,1,0:T(2,128)(2,1)S(1)}, bf16[1024,2,256]{2,1,0:T(2,128)(2,1)}, u32[]{:S(2)}) copy-start(bf16[1024,2,256]{2,1,0:T(2,128)(2,1)} %param.6) | copy-start | bytes 3145732
  0.6 1.8 %copy-start.2 = (s32[128,8]{0,1:T(8,128)S(1)}, s32[128,8]{0,1:T(8,128)}, u32[]{:S(2)}) copy-start(s32[128,8]{0,1:T(8,128)} %param.7) | copy-start | bytes 12292
  0.7 1.8 %copy-start.3 = (s32[128,8]{0,1:T(8,128)S(1)}, s32[128,8]{0,1:T(8,128)}, u32[]{:S(2)}) copy-start(s32[128,8]{0,1:T(8,128)} %param.8) | copy-start | bytes 12292
  3.6 31.9 %collective-permute-start.3 = (bf16[1024,512]{1,0:T(8,128)(2,1)S(1)}, bf16[1024,512]{1,0:T(8,128)(2,1)S(1)}, u32[]{:S(2)}, u32[]{:S(2)}) collective-permute-start(bf16[1024,512]{1,0:T(8,128)(2,1)S(1)} %bitcast.10), channel_id=1, source_target_pairs={{0,8},{8,0},{16,24},{24,16},{1,9},{9,1},{17,25},{25,17},{2,10},{10... | collective-permute-start | bytes 3145736 | tf_op jit(solution)/shard_map/ppermute | solution.py:457
  6.6 28.9 %collective-permute-start.4 = (bf16[1024,512]{1,0:T(8,128)(2,1)S(1)}, bf16[1024,512]{1,0:T(8,128)(2,1)S(1)}, u32[]{:S(2)}, u32[]{:S(2)}) collective-permute-start(bf16[1024,512]{1,0:T(8,128)(2,1)S(1)} %bitcast.11), channel_id=1, source_target_pairs={{0,16},{8,24},{16,0},{24,8},{1,17},{9,25},{17,1},{25,9},{2,18},{10... | collective-permute-start | bytes 3145736 | tf_op jit(solution)/shard_map/ppermute | solution.py:458
  8.2 16.1 %collective-permute-start.5 = (bf16[64,4224]{1,0:T(8,128)(2,1)S(1)}, bf16[64,4224]{1,0:T(8,128)(2,1)S(1)}, u32[]{:S(2)}, u32[]{:S(2)}) collective-permute-start(bf16[64,4224]{1,0:T(8,128)(2,1)S(1)} %get-tuple-element.38.refs_2_), channel_id=1, source_target_pairs={{0,2},{1,3},{2,6},{3,7},{4,0},{5,1},{6,4},{7,5},{8,10},{9,11},{10,... | collective-permute-start | bytes 1622024 | tf_op jit(solution)/shard_map/ppermute | solution.py:454
  9.7 25.8 %collective-permute-start.2 = (bf16[64,4096]{1,0:T(8,128)(2,1)S(1)}, bf16[64,4096]{1,0:T(8,128)(2,1)S(1)}, u32[]{:S(2)}, u32[]{:S(2)}) collective-permute-start(bf16[64,4096]{1,0:T(8,128)(2,1)S(1)} %get-tuple-element.70.refs_1_), channel_id=1, source_target_pairs={{0,2},{1,3},{2,6},{3,7},{4,0},{5,1},{6,4},{7,5},{8,10},{9,11},{10,... | collective-permute-start | bytes 1572872 | tf_op jit(solution)/shard_map/ppermute | solution.py:454
  24.3 22.8 %collective-permute-start.11 = (bf16[64,4224]{1,0:T(8,128)(2,1)S(1)}, bf16[64,4224]{1,0:T(8,128)(2,1)S(1)}, u32[]{:S(2)}, u32[]{:S(2)}) collective-permute-start(bf16[64,4224]{1,0:T(8,128)(2,1)S(1)} %collective-permute-done.5.refs_6_), channel_id=1, source_target_pairs={{0,2},{1,3},{2,6},{3,7},{4,0},{5,1},{6,4},{7,5},{8,10},{9,11},{10,... | collective-permute-start | bytes 1622024 | tf_op jit(solution)/shard_map/ppermute | solution.py:454
  35.6 11.5 %collective-permute-start.10 = (bf16[512,512]{1,0:T(8,128)(2,1)S(1)}, bf16[512,512]{1,0:T(8,128)(2,1)S(1)}, u32[]{:S(2)}, u32[]{:S(2)}) collective-permute-start(bf16[512,512]{1,0:T(8,128)(2,1)S(1)} %slice.15), channel_id=1, source_target_pairs={{0,8},{8,0},{16,24},{24,16},{1,9},{9,1},{17,25},{25,17},{2,10},{10... | collective-permute-start | bytes 1572872 | tf_op jit(solution)/shard_map/ppermute | solution.py:462
  36.2 11.4 %collective-permute-start.9 = (bf16[512,512]{1,0:T(8,128)(2,1)S(1)}, bf16[512,512]{1,0:T(8,128)(2,1)S(1)}, u32[]{:S(2)}, u32[]{:S(2)}) collective-permute-start(bf16[512,512]{1,0:T(8,128)(2,1)S(1)} %slice.14), channel_id=1, source_target_pairs={{0,16},{8,24},{16,0},{24,8},{1,17},{9,25},{17,1},{25,9},{2,18},{10... | collective-permute-start | bytes 1572872 | tf_op jit(solution)/shard_map/ppermute | solution.py:461
  36.4 20.2 %collective-permute-start.8 = (bf16[64,4096]{1,0:T(8,128)(2,1)S(1)}, bf16[64,4096]{1,0:T(8,128)(2,1)S(1)}, u32[]{:S(2)}, u32[]{:S(2)}) collective-permute-start(bf16[64,4096]{1,0:T(8,128)(2,1)S(1)} %collective-permute-done.2.refs_5_), channel_id=1, source_target_pairs={{0,2},{1,3},{2,6},{3,7},{4,0},{5,1},{6,4},{7,5},{8,10},{9,11},{10,... | collective-permute-start | bytes 1572872 | tf_op jit(solution)/shard_map/ppermute | solution.py:454
  37.6 19.0 %collective-permute-start = (bf16[64,4096]{1,0:T(8,128)(2,1)S(1)}, bf16[64,4096]{1,0:T(8,128)(2,1)S(1)}, u32[]{:S(2)}, u32[]{:S(2)}) collective-permute-start(bf16[64,4096]{1,0:T(8,128)(2,1)S(1)} %get-tuple-element.70.refs_1_), channel_id=1, source_target_pairs={{0,1},{1,0},{2,3},{3,2},{4,5},{5,4},{6,7},{7,6},{8,9},{9,8},{10,11... | collective-permute-start | bytes 1572872 | tf_op jit(solution)/shard_map/ppermute | solution.py:469
  47.1 10.0 %collective-permute-start.1 = (bf16[64,4224]{1,0:T(8,128)(2,1)S(1)}, bf16[64,4224]{1,0:T(8,128)(2,1)S(1)}, u32[]{:S(2)}, u32[]{:S(2)}) collective-permute-start(bf16[64,4224]{1,0:T(8,128)(2,1)S(1)} %get-tuple-element.38.refs_2_), channel_id=1, source_target_pairs={{0,1},{1,0},{2,3},{3,2},{4,5},{5,4},{6,7},{7,6},{8,9},{9,8},{10,11... | collective-permute-start | bytes 1622024 | tf_op jit(solution)/shard_map/ppermute | solution.py:469
  47.1 10.8 %collective-permute-start.7 = (bf16[64,4224]{1,0:T(8,128)(2,1)S(1)}, bf16[64,4224]{1,0:T(8,128)(2,1)S(1)}, u32[]{:S(2)}, u32[]{:S(2)}) collective-permute-start(bf16[64,4224]{1,0:T(8,128)(2,1)S(1)} %collective-permute-done.5.refs_6_), channel_id=1, source_target_pairs={{0,1},{1,0},{2,3},{3,2},{4,5},{5,4},{6,7},{7,6},{8,9},{9,8},{10,11... | collective-permute-start | bytes 1622024 | tf_op jit(solution)/shard_map/ppermute | solution.py:469
  47.6 13.7 %collective-permute-start.13 = (bf16[64,4224]{1,0:T(8,128)(2,1)S(1)}, bf16[64,4224]{1,0:T(8,128)(2,1)S(1)}, u32[]{:S(2)}, u32[]{:S(2)}) collective-permute-start(bf16[64,4224]{1,0:T(8,128)(2,1)S(1)} %collective-permute-done.11.refs_10_), channel_id=1, source_target_pairs={{0,1},{1,0},{2,3},{3,2},{4,5},{5,4},{6,7},{7,6},{8,9},{9,8},{10,11... | collective-permute-start | bytes 1622024 | tf_op jit(solution)/shard_map/ppermute | solution.py:469
  56.6 4.7 %collective-permute-start.6 = (bf16[64,4096]{1,0:T(8,128)(2,1)S(1)}, bf16[64,4096]{1,0:T(8,128)(2,1)S(1)}, u32[]{:S(2)}, u32[]{:S(2)}) collective-permute-start(bf16[64,4096]{1,0:T(8,128)(2,1)S(1)} %collective-permute-done.2.refs_5_), channel_id=1, source_target_pairs={{0,1},{1,0},{2,3},{3,2},{4,5},{5,4},{6,7},{7,6},{8,9},{9,8},{10,11... | collective-permute-start | bytes 1572872 | tf_op jit(solution)/shard_map/ppermute | solution.py:469
  56.6 4.7 %collective-permute-start.12 = (bf16[64,4096]{1,0:T(8,128)(2,1)S(1)}, bf16[64,4096]{1,0:T(8,128)(2,1)S(1)}, u32[]{:S(2)}, u32[]{:S(2)}) collective-permute-start(bf16[64,4096]{1,0:T(8,128)(2,1)S(1)} %collective-permute-done.8.refs_9_), channel_id=1, source_target_pairs={{0,1},{1,0},{2,3},{3,2},{4,5},{5,4},{6,7},{7,6},{8,9},{9,8},{10,11... | collective-permute-start | bytes 1572872 | tf_op jit(solution)/shard_map/ppermute | solution.py:469
  57.1 16.9 %collective-permute-start.15 = (bf16[64,4224]{1,0:T(8,128)(2,1)S(1)}, bf16[64,4224]{1,0:T(8,128)(2,1)S(1)}, u32[]{:S(2)}, u32[]{:S(2)}) collective-permute-start(bf16[64,4224]{1,0:T(8,128)(2,1)S(1)} %collective-permute-done.11.refs_10_), channel_id=1, source_target_pairs={{0,2},{1,3},{2,6},{3,7},{4,0},{5,1},{6,4},{7,5},{8,10},{9,11},{10,... | collective-permute-start | bytes 1622024 | tf_op jit(solution)/shard_map/ppermute | solution.py:454
  57.9 25.6 %collective-permute-start.14 = (bf16[64,4096]{1,0:T(8,128)(2,1)S(1)}, bf16[64,4096]{1,0:T(8,128)(2,1)S(1)}, u32[]{:S(2)}, u32[]{:S(2)}) collective-permute-start(bf16[64,4096]{1,0:T(8,128)(2,1)S(1)} %collective-permute-done.8.refs_9_), channel_id=1, source_target_pairs={{0,2},{1,3},{2,6},{3,7},{4,0},{5,1},{6,4},{7,5},{8,10},{9,11},{10,... | collective-permute-start | bytes 1572872 | tf_op jit(solution)/shard_map/ppermute | solution.py:454
  83.5 2.7 %collective-permute-start.17 = (bf16[64,4224]{1,0:T(8,128)(2,1)S(1)}, bf16[64,4224]{1,0:T(8,128)(2,1)S(1)}, u32[]{:S(2)}, u32[]{:S(2)}) collective-permute-start(bf16[64,4224]{1,0:T(8,128)(2,1)S(1)} %collective-permute-done.15.refs_1_), channel_id=1, source_target_pairs={{0,1},{1,0},{2,3},{3,2},{4,5},{5,4},{6,7},{7,6},{8,9},{9,8},{10,11... | collective-permute-start | bytes 1622024 | tf_op jit(solution)/shard_map/ppermute | solution.py:469
  83.5 2.7 %collective-permute-start.16 = (bf16[64,4096]{1,0:T(8,128)(2,1)S(1)}, bf16[64,4096]{1,0:T(8,128)(2,1)S(1)}, u32[]{:S(2)}, u32[]{:S(2)}) collective-permute-start(bf16[64,4096]{1,0:T(8,128)(2,1)S(1)} %collective-permute-done.14.refs_0_), channel_id=1, source_target_pairs={{0,1},{1,0},{2,3},{3,2},{4,5},{5,4},{6,7},{7,6},{8,9},{9,8},{10,11... | collective-permute-start | bytes 1572872 | tf_op jit(solution)/shard_map/ppermute | solution.py:469
  89.8 15.1 %collective-permute-start.20 = (bf16[256,1024]{1,0:T(8,128)(2,1)}, bf16[256,1024]{1,0:T(8,128)(2,1)}, u32[]{:S(2)}, u32[]{:S(2)}) collective-permute-start(bf16[256,1024]{1,0:T(8,128)(2,1)} %get-tuple-element.62), channel_id=1, source_target_pairs={{0,16},{8,24},{16,0},{24,8},{1,17},{9,25},{17,1},{25,9},{2,18},{10... | collective-permute-start | bytes 1572872 | tf_op jit(solution)/shard_map/ppermute | solution.py:483
  90.4 15.1 %collective-permute-start.21 = (bf16[256,1024]{1,0:T(8,128)(2,1)}, bf16[256,1024]{1,0:T(8,128)(2,1)}, u32[]{:S(2)}, u32[]{:S(2)}) collective-permute-start(bf16[256,1024]{1,0:T(8,128)(2,1)} %get-tuple-element.64), channel_id=1, source_target_pairs={{0,8},{8,0},{16,24},{24,16},{1,9},{9,1},{17,25},{25,17},{2,10},{10... | collective-permute-start | bytes 1572872 | tf_op jit(solution)/shard_map/ppermute | solution.py:482
  94.0 1.4 %copy-start = (f32[512,1024]{1,0:T(8,128)}, f32[512,1024]{1,0:T(8,128)S(1)}, u32[]{:S(2)}) copy-start(f32[512,1024]{1,0:T(8,128)S(1)} %get-tuple-element.56.own) | copy-start | bytes 6291460
  95.4 21.3 %collective-permute-start.18 = (bf16[256,1024]{1,0:T(8,128)(2,1)}, bf16[256,1024]{1,0:T(8,128)(2,1)S(1)}, u32[]{:S(2)}, u32[]{:S(2)}) collective-permute-start(bf16[256,1024]{1,0:T(8,128)(2,1)} %get-tuple-element.57), channel_id=1, source_target_pairs={{0,8},{8,0},{16,24},{24,16},{1,9},{9,1},{17,25},{25,17},{2,10},{10... | collective-permute-start | bytes 1572872 | tf_op jit(solution)/shard_map/ppermute | solution.py:485
  96.9 19.8 %collective-permute-start.19 = (bf16[256,1024]{1,0:T(8,128)(2,1)}, bf16[256,1024]{1,0:T(8,128)(2,1)S(1)}, u32[]{:S(2)}, u32[]{:S(2)}) collective-permute-start(bf16[256,1024]{1,0:T(8,128)(2,1)} %get-tuple-element.58), channel_id=1, source_target_pairs={{0,16},{8,24},{16,0},{24,8},{1,17},{9,25},{17,1},{25,9},{2,18},{10... | collective-permute-start | bytes 1572872 | tf_op jit(solution)/shard_map/ppermute | solution.py:486
  107.8 18.8 %collective-permute-start.22 = (bf16[256,1024]{1,0:T(8,128)(2,1)}, bf16[256,1024]{1,0:T(8,128)(2,1)}, u32[]{:S(2)}, u32[]{:S(2)}) collective-permute-start(bf16[256,1024]{1,0:T(8,128)(2,1)} %get-tuple-element.67), channel_id=1, source_target_pairs={{0,16},{8,24},{16,0},{24,8},{1,17},{9,25},{17,1},{25,9},{2,18},{10... | collective-permute-start | bytes 1572872 | tf_op jit(solution)/shard_map/ppermute | solution.py:502
  109.3 17.5 %collective-permute-start.23 = (bf16[256,1024]{1,0:T(8,128)(2,1)}, bf16[256,1024]{1,0:T(8,128)(2,1)}, u32[]{:S(2)}, u32[]{:S(2)}) collective-permute-start(bf16[256,1024]{1,0:T(8,128)(2,1)} %get-tuple-element.68), channel_id=1, source_target_pairs={{0,8},{8,0},{16,24},{24,16},{1,9},{9,1},{17,25},{25,17},{2,10},{10... | collective-permute-start | bytes 1572872 | tf_op jit(solution)/shard_map/ppermute | solution.py:501
  111.8 10.4 %all-to-all-start = ((f32[8,1,128]{2,1,0:T(1,128)}), f32[8,1,128]{2,1,0:T(1,128)S(1)}, u32[]{:S(2)}, u32[]{:S(2)}) async-start(f32[8,1,128]{2,1,0:T(1,128)} %bitcast.6), calls=%async_computation | async-start | bytes 8192 | tf_op jit(solution)/shard_map/all_to_all | solution.py:505
  116.7 1.6 %copy-start.1 = (f32[512,1024]{1,0:T(8,128)S(1)}, f32[512,1024]{1,0:T(8,128)}, u32[]{:S(2)}) copy-start(f32[512,1024]{1,0:T(8,128)} %copy-done) | copy-start | bytes 6291460
